TPU v7x, 512 devices: a whole 4x8x8 slice. The times are simulated.
512 devices in a mesh: patch: 32 (over x, z), lag: 16 (over y, core).
Axes of the slice: x: 4, y: 8, z: 8, core: 2. Of those that a mesh axis runs over, the one named last changes fastest.
Arguments:
- history: bfloat16 [16, 128, 32768], P('lag', None, 'patch'), may hold values from -6 to 6
- coupling: bfloat16 [16, 32768, 1024], P('lag', 'patch'), may hold values from -0.046875 to 0.046875
- inverse: bfloat16 [32768, 1024], P('patch'), may hold values from -0.1875 to 0.1875
- cotangent: bfloat16 [6, 128, 32768], P(None, 'lag', 'patch'), may hold values from -6 to 6
- targets: int32 [16, 32], P('lag'), may hold values from 0 to 31
Outputs:
- adjoint: bfloat16 [6, 128, 32768], P(None, 'lag', 'patch')
Inputs may be any that keep to these rules, and one draw needn't show every extreme that they name: `targets`: each lag and source patch lists exactly one target patch; several sources may list the same target.
All inputs are finite; a program needn't handle non-finite values.
Results may differ from a plain program's by a relative error of at most 0.0085.
Values may be sent and summed in bfloat16 or wider, within the bound.
No kernel may reach another device: no remote copies, remote signals or barrier semaphores. Data moves between devices by JAX's collectives and lax.ppermute only.
A program may use at most 64 MiB of HBM per device.

v0:
```python
import jax
import jax.numpy as jnp
from jax import lax
from jax.sharding import PartitionSpec as P

STEPS = 6


def passed_along(value, axis, by):
    size = lax.axis_size(axis)
    pairs = [(i, i + by) for i in range(size) if 0 <= i + by < size]
    return lax.ppermute(value, axis, pairs)


def on_device(history, coupling, inverse, cotangent, targets):
    history_now = history[0]
    coupling_tile = coupling[0]
    target_row = targets[0]
    patch_count = lax.axis_size("patch")
    rows_total = history_now.shape[0]
    unknowns = history_now.shape[1]
    block_rows = rows_total // patch_count
    lag_index = lax.axis_index("lag")
    results = []
    for turn_index in range(STEPS):
        pieces = lax.all_to_all(
            history_now.reshape(patch_count, block_rows, unknowns),
            "patch",
            split_axis=0,
            concat_axis=0,
            tiled=True,
        )
        chosen = jnp.take(pieces, target_row, axis=0)
        partial_value = jnp.einsum(
            "prj,jk->prk",
            lax.all_to_all(chosen, "patch", split_axis=0, concat_axis=0, tiled=True),
            coupling_tile,
            preferred_element_type=jnp.float32,
        )
        partial_value = partial_value.reshape(rows_total, unknowns)
        summed = lax.psum_scatter(partial_value, "lag", scatter_dimension=0, tiled=True)
        residual = (cotangent[turn_index].astype(jnp.float32) - summed).astype(jnp.bfloat16)
        own_rows = jnp.dot(residual, inverse, preferred_element_type=jnp.float32).astype(
            jnp.bfloat16
        )
        if turn_index + 1 < STEPS:
            latest = lax.all_gather(own_rows, "lag", axis=0, tiled=True)
        results.append(own_rows)
        if turn_index + 1 < STEPS:
            shifted = passed_along(history_now, "lag", 1)
            history_now = jnp.where(lag_index == 0, latest, shifted)
    return jnp.stack(results)


def solution(mesh):
    placed = (
        P("lag", None, "patch"),
        P("lag", "patch", None),
        P("patch", None),
        P(None, "lag", "patch"),
        P("lag", None),
    )
    return jax.shard_map(
        on_device, mesh=mesh, in_specs=placed, out_specs=P(None, "lag", "patch"), check_vma=False
    )
```

profile of v0, /device:TPU:25, one launch (start us, length us, event | category | flops | bytes accessed | tf_op | source)
XLA Modules:
  0.0 679.0 jit_solution(8315219850976885158)
XLA Ops:
  6.5 1.9 reshape_squeeze.3
  8.4 12.9 %all-to-all-start = ((bf16[32,4,1024]{2,1,0:T(4,128)(2,1)}), bf16[32,4,1024]{2,1,0:T(4,128)(2,1)S(1)}, u32[]{:S(2)}, u32[]{:S(2)}) async-start(bf16[32,4,1024]{2,1,0:T(4,128)(2,1)} %reshape_squeeze.3), calls=%async_computation | async-start | bytes 524288 | tf_op jit(solution)/shard_map/all_to_all | solution.py:26
  21.4 0.7 compare_select_fusion
  22.0 0.7 compare_and_fusion
  22.7 8.3 %all-to-all-done = bf16[32,4,1024]{2,1,0:T(4,128)(2,1)S(1)} async-done(((bf16[32,4,1024]{2,1,0:T(4,128)(2,1)}), bf16[32,4,1024]{2,1,0:T(4,128)(2,1)S(1)}, u32[]{:S(2)}, u32[]{:S(2)}) %all-to-all-start) | async-done | bytes 262176 | tf_op jit(solution)/shard_map/all_to_all | solution.py:26
  31.0 0.8 gather_fusion
  31.8 0.2 broadcast_select_fusion.5
  32.0 15.8 %all_to_all.60 = bf16[32,4,1024]{2,1,0:T(4,128)(2,1)S(1)} all-to-all(bf16[32,4,1024]{2,1,0:T(4,128)(2,1)S(1)} %broadcast_select_fusion.5), channel_id=1, replica_groups=mesh['patch'=32,'lag'=16] {'patch'}, dimensions={0} | all-to-all | bytes 524288 | tf_op jit(solution)/shard_map/all_to_all | solution.py:36
  47.8 0.1 dot_general.48
  47.9 1.2 fusion.10
  49.2 8.0 %collective-permute-start = (bf16[128,1024]{1,0:T(8,128)(2,1)S(1)}, bf16[128,1024]{1,0:T(8,128)(2,1)S(1)}, u32[]{:S(2)}, u32[]{:S(2)}) collective-permute-start(bf16[128,1024]{1,0:T(8,128)(2,1)S(1)} %bitcast.90), channel_id=1, source_target_pairs={{0,1},{1,2},{2,3},{3,4},{4,5},{5,6},{6,7},{7,8},{8,9},{9,10},{10,1... | collective-permute-start | bytes 786440 | tf_op jit(solution)/shard_map/ppermute | solution.py:12
  57.2 50.9 %reduce-scatter.7.cloned.1.call-done = f32[8,1024]{1,0:T(8,128)} async-done(((f32[128,1024]{1,0:T(8,128)}), f32[8,1024]{1,0:T(8,128)}) %reduce-scatter.7.cloned.1.call-update) | async-done | bytes 32784 | tf_op jit(solution)/shard_map/reduce_scatter | solution.py:41
  108.1 2.0 bitcast_dynamic-update-slice_fusion.4
  110.1 14.1 %all_gather.15 = bf16[128,1024]{1,0:T(8,128)(2,1)S(1)} all-gather(bf16[8,1024]{1,0:T(8,128)(2,1)S(1)} %get-tuple-element.7), channel_id=1, replica_groups=mesh['patch'=32,'lag'=16] {'lag'}, dimensions={0}, use_global_device_ids=true | all-gather | bytes 278528 | tf_op jit(solution)/shard_map/all_gather | solution.py:47
  124.3 0.1 reshape.44
  124.4 19.6 %all_to_all.61 = bf16[32,4,1024]{2,1,0:T(4,128)(2,1)S(1)} all-to-all(bf16[32,4,1024]{2,1,0:T(4,128)(2,1)S(1)} %reshape.44), channel_id=1, replica_groups=mesh['patch'=32,'lag'=16] {'patch'}, dimensions={0} | all-to-all | bytes 524288 | tf_op jit(solution)/shard_map/all_to_all | solution.py:26
  144.0 0.8 gather_fusion.1
  144.8 0.2 broadcast_select_fusion.4
  145.0 16.0 %all_to_all.62 = bf16[32,4,1024]{2,1,0:T(4,128)(2,1)S(1)} all-to-all(bf16[32,4,1024]{2,1,0:T(4,128)(2,1)S(1)} %broadcast_select_fusion.4), channel_id=1, replica_groups=mesh['patch'=32,'lag'=16] {'patch'}, dimensions={0} | all-to-all | bytes 524288 | tf_op jit(solution)/shard_map/all_to_all | solution.py:36
  161.0 0.1 dot_general.51
  161.1 1.2 fusion.8
  162.4 6.4 collective-permute-start.1
  168.8 51.4 %reduce-scatter.9.cloned.1.call-done = f32[8,1024]{1,0:T(8,128)} async-done(((f32[128,1024]{1,0:T(8,128)}), f32[8,1024]{1,0:T(8,128)}) %reduce-scatter.9.cloned.1.call-update) | async-done | bytes 32784 | tf_op jit(solution)/shard_map/reduce_scatter | solution.py:41
  220.2 2.0 bitcast_dynamic-update-slice_fusion.3
  222.2 14.1 %all_gather.16 = bf16[128,1024]{1,0:T(8,128)(2,1)S(1)} all-gather(bf16[8,1024]{1,0:T(8,128)(2,1)S(1)} %get-tuple-element.9), channel_id=1, replica_groups=mesh['patch'=32,'lag'=16] {'lag'}, dimensions={0}, use_global_device_ids=true | all-gather | bytes 278528 | tf_op jit(solution)/shard_map/all_gather | solution.py:47
  236.4 0.1 reshape.45
  236.5 19.8 %all_to_all.63 = bf16[32,4,1024]{2,1,0:T(4,128)(2,1)S(1)} all-to-all(bf16[32,4,1024]{2,1,0:T(4,128)(2,1)S(1)} %reshape.45), channel_id=1, replica_groups=mesh['patch'=32,'lag'=16] {'patch'}, dimensions={0} | all-to-all | bytes 524288 | tf_op jit(solution)/shard_map/all_to_all | solution.py:26
  256.3 0.8 gather_fusion.2
  257.1 0.2 broadcast_select_fusion.3
  257.3 16.0 %all_to_all.64 = bf16[32,4,1024]{2,1,0:T(4,128)(2,1)S(1)} all-to-all(bf16[32,4,1024]{2,1,0:T(4,128)(2,1)S(1)} %broadcast_select_fusion.3), channel_id=1, replica_groups=mesh['patch'=32,'lag'=16] {'patch'}, dimensions={0} | all-to-all | bytes 524288 | tf_op jit(solution)/shard_map/all_to_all | solution.py:36
  273.3 0.1 dot_general.54
  273.4 1.2 fusion.6
  274.7 6.4 collective-permute-start.2
  281.1 51.4 %reduce-scatter.11.cloned.1.call-done = f32[8,1024]{1,0:T(8,128)} async-done(((f32[128,1024]{1,0:T(8,128)}), f32[8,1024]{1,0:T(8,128)}) %reduce-scatter.11.cloned.1.call-update) | async-done | bytes 32784 | tf_op jit(solution)/shard_map/reduce_scatter | solution.py:41
  332.6 2.0 bitcast_dynamic-update-slice_fusion.2
  334.6 14.1 %all_gather.17 = bf16[128,1024]{1,0:T(8,128)(2,1)S(1)} all-gather(bf16[8,1024]{1,0:T(8,128)(2,1)S(1)} %get-tuple-element.11), channel_id=1, replica_groups=mesh['patch'=32,'lag'=16] {'lag'}, dimensions={0}, use_global_device_ids=true | all-gather | bytes 278528 | tf_op jit(solution)/shard_map/all_gather | solution.py:47
  348.7 0.1 reshape.46
  348.8 19.8 %all_to_all.65 = bf16[32,4,1024]{2,1,0:T(4,128)(2,1)S(1)} all-to-all(bf16[32,4,1024]{2,1,0:T(4,128)(2,1)S(1)} %reshape.46), channel_id=1, replica_groups=mesh['patch'=32,'lag'=16] {'patch'}, dimensions={0} | all-to-all | bytes 524288 | tf_op jit(solution)/shard_map/all_to_all | solution.py:26
  368.6 0.8 gather_fusion.3
  369.4 0.2 broadcast_select_fusion.2
  369.6 16.0 %all_to_all.66 = bf16[32,4,1024]{2,1,0:T(4,128)(2,1)S(1)} all-to-all(bf16[32,4,1024]{2,1,0:T(4,128)(2,1)S(1)} %broadcast_select_fusion.2), channel_id=1, replica_groups=mesh['patch'=32,'lag'=16] {'patch'}, dimensions={0} | all-to-all | bytes 524288 | tf_op jit(solution)/shard_map/all_to_all | solution.py:36
  385.7 1.2 fusion.4
  387.0 6.4 collective-permute-start.3
  393.5 51.4 %reduce-scatter.13.cloned.1.call-done = f32[8,1024]{1,0:T(8,128)} async-done(((f32[128,1024]{1,0:T(8,128)}), f32[8,1024]{1,0:T(8,128)}) %reduce-scatter.13.cloned.1.call-update) | async-done | bytes 32784 | tf_op jit(solution)/shard_map/reduce_scatter | solution.py:41
  444.9 2.0 bitcast_dynamic-update-slice_fusion.1
  446.9 14.1 %all_gather.18 = bf16[128,1024]{1,0:T(8,128)(2,1)S(1)} all-gather(bf16[8,1024]{1,0:T(8,128)(2,1)S(1)} %get-tuple-element.13), channel_id=1, replica_groups=mesh['patch'=32,'lag'=16] {'lag'}, dimensions={0}, use_global_device_ids=true | all-gather | bytes 278528 | tf_op jit(solution)/shard_map/all_gather | solution.py:47
  461.1 0.1 reshape.47
  461.2 19.8 %all_to_all.67 = bf16[32,4,1024]{2,1,0:T(4,128)(2,1)S(1)} all-to-all(bf16[32,4,1024]{2,1,0:T(4,128)(2,1)S(1)} %reshape.47), channel_id=1, replica_groups=mesh['patch'=32,'lag'=16] {'patch'}, dimensions={0} | all-to-all | bytes 524288 | tf_op jit(solution)/shard_map/all_to_all | solution.py:26
  481.0 0.8 gather_fusion.4
  481.7 0.2 broadcast_select_fusion.1
  481.9 16.0 %all_to_all.68 = bf16[32,4,1024]{2,1,0:T(4,128)(2,1)S(1)} all-to-all(bf16[32,4,1024]{2,1,0:T(4,128)(2,1)S(1)} %broadcast_select_fusion.1), channel_id=1, replica_groups=mesh['patch'=32,'lag'=16] {'patch'}, dimensions={0} | all-to-all | bytes 524288 | tf_op jit(solution)/shard_map/all_to_all | solution.py:36
  498.1 1.2 fusion.2
  499.4 6.4 collective-permute-start.4
  505.8 51.4 %reduce-scatter.15.cloned.1.call-done = f32[8,1024]{1,0:T(8,128)} async-done(((f32[128,1024]{1,0:T(8,128)}), f32[8,1024]{1,0:T(8,128)}) %reduce-scatter.15.cloned.1.call-update) | async-done | bytes 32784 | tf_op jit(solution)/shard_map/reduce_scatter | solution.py:41
  557.2 2.0 bitcast_dynamic-update-slice_fusion
  559.2 14.1 %all_gather.19 = bf16[128,1024]{1,0:T(8,128)(2,1)S(1)} all-gather(bf16[8,1024]{1,0:T(8,128)(2,1)S(1)} %get-tuple-element.15), channel_id=1, replica_groups=mesh['patch'=32,'lag'=16] {'lag'}, dimensions={0}, use_global_device_ids=true | all-gather | bytes 278528 | tf_op jit(solution)/shard_map/all_gather | solution.py:47
  573.4 0.1 reshape.48
  573.5 19.8 %all_to_all.69 = bf16[32,4,1024]{2,1,0:T(4,128)(2,1)S(1)} all-to-all(bf16[32,4,1024]{2,1,0:T(4,128)(2,1)S(1)} %reshape.48), channel_id=1, replica_groups=mesh['patch'=32,'lag'=16] {'patch'}, dimensions={0} | all-to-all | bytes 524288 | tf_op jit(solution)/shard_map/all_to_all | solution.py:26
  593.3 0.8 gather_fusion.5
  594.1 0.2 broadcast_select_fusion
  594.3 16.0 %all_to_all.70 = bf16[32,4,1024]{2,1,0:T(4,128)(2,1)S(1)} all-to-all(bf16[32,4,1024]{2,1,0:T(4,128)(2,1)S(1)} %broadcast_select_fusion), channel_id=1, replica_groups=mesh['patch'=32,'lag'=16] {'patch'}, dimensions={0} | all-to-all | bytes 524288 | tf_op jit(solution)/shard_map/all_to_all | solution.py:36
  610.4 1.2 fusion
  611.7 57.9 %reduce-scatter.17.cloned.1.call-done = f32[8,1024]{1,0:T(8,128)} async-done(((f32[128,1024]{1,0:T(8,128)}), f32[8,1024]{1,0:T(8,128)}) %reduce-scatter.17.cloned.1.call-update) | async-done | bytes 32784 | tf_op jit(solution)/shard_map/reduce_scatter | solution.py:41
  669.6 2.6 fusion.13
  (34 shorter events, 0.7 us)
Async XLA Ops:
  6.5 41.3 %copy-start = (bf16[1,1024,1024]{2,1,0:T(8,128)(2,1)S(1)}, bf16[1,1024,1024]{2,1,0:T(8,128)(2,1)}, u32[]{:S(2)}) copy-start(bf16[1,1024,1024]{2,1,0:T(8,128)(2,1)} %param.8) | copy-start | bytes 6291460
  8.4 22.6 %all-to-all-start = ((bf16[32,4,1024]{2,1,0:T(4,128)(2,1)}), bf16[32,4,1024]{2,1,0:T(4,128)(2,1)S(1)}, u32[]{:S(2)}, u32[]{:S(2)}) async-start(bf16[32,4,1024]{2,1,0:T(4,128)(2,1)} %reshape_squeeze.3), calls=%async_computation | async-start | bytes 524288 | tf_op jit(solution)/shard_map/all_to_all | solution.py:26
  21.3 86.8 %reduce-scatter.7.cloned.1.call-start = ((), (), s32[]{:S(2)}) async-start(), calls=%async_computation.18 | async-start | bytes 557056 | tf_op jit(solution)/shard_map/reduce_scatter | solution.py:41
  47.8 1.4 copy-start.1
  47.8 60.3 %copy-start.2 = (bf16[6,8,1024]{2,1,0:T(8,128)(2,1)S(1)}, bf16[6,8,1024]{2,1,0:T(8,128)(2,1)}, u32[]{:S(2)}) copy-start(bf16[6,8,1024]{2,1,0:T(8,128)(2,1)} %param.10) | copy-start | bytes 294916
  49.2 171.1 %reduce-scatter.9.cloned.1.call-start = ((), (), s32[]{:S(2)}) async-start(), calls=%async_computation.19 | async-start | bytes 557056 | tf_op jit(solution)/shard_map/reduce_scatter | solution.py:41
  49.2 75.0 %collective-permute-start = (bf16[128,1024]{1,0:T(8,128)(2,1)S(1)}, bf16[128,1024]{1,0:T(8,128)(2,1)S(1)}, u32[]{:S(2)}, u32[]{:S(2)}) collective-permute-start(bf16[128,1024]{1,0:T(8,128)(2,1)S(1)} %bitcast.90), channel_id=1, source_target_pairs={{0,1},{1,2},{2,3},{3,4},{4,5},{5,6},{6,7},{7,8},{8,9},{9,10},{10,1... | collective-permute-start | bytes 786440 | tf_op jit(solution)/shard_map/ppermute | solution.py:12
  162.3 170.2 %reduce-scatter.11.cloned.1.call-start = ((), (), s32[]{:S(2)}) async-start(), calls=%async_computation.20 | async-start | bytes 557056 | tf_op jit(solution)/shard_map/reduce_scatter | solution.py:41
  162.4 74.0 %collective-permute-start.1 = (bf16[128,1024]{1,0:T(8,128)(2,1)S(1)}, bf16[128,1024]{1,0:T(8,128)(2,1)S(1)}, u32[]{:S(2)}, u32[]{:S(2)}) collective-permute-start(bf16[128,1024]{1,0:T(8,128)(2,1)S(1)} %broadcast_select_fusion.10), channel_id=1, source_target_pairs={{0,1},{1,2},{2,3},{3,4},{4,5},{5,6},{6,7},{7,8},{8,9},{9,10},{10,1... | collective-permute-start | bytes 786440 | tf_op jit(solution)/shard_map/ppermute | solution.py:12
  274.7 170.2 %reduce-scatter.13.cloned.1.call-start = ((), (), s32[]{:S(2)}) async-start(), calls=%async_computation.21 | async-start | bytes 557056 | tf_op jit(solution)/shard_map/reduce_scatter | solution.py:41
  274.7 74.0 %collective-permute-start.2 = (bf16[128,1024]{1,0:T(8,128)(2,1)S(1)}, bf16[128,1024]{1,0:T(8,128)(2,1)S(1)}, u32[]{:S(2)}, u32[]{:S(2)}) collective-permute-start(bf16[128,1024]{1,0:T(8,128)(2,1)S(1)} %broadcast_select_fusion.9), channel_id=1, source_target_pairs={{0,1},{1,2},{2,3},{3,4},{4,5},{5,6},{6,7},{7,8},{8,9},{9,10},{10,1... | collective-permute-start | bytes 786440 | tf_op jit(solution)/shard_map/ppermute | solution.py:12
  387.0 170.2 %reduce-scatter.15.cloned.1.call-start = ((), (), s32[]{:S(2)}) async-start(), calls=%async_computation.22 | async-start | bytes 557056 | tf_op jit(solution)/shard_map/reduce_scatter | solution.py:41
  387.0 74.0 %collective-permute-start.3 = (bf16[128,1024]{1,0:T(8,128)(2,1)S(1)}, bf16[128,1024]{1,0:T(8,128)(2,1)S(1)}, u32[]{:S(2)}, u32[]{:S(2)}) collective-permute-start(bf16[128,1024]{1,0:T(8,128)(2,1)S(1)} %broadcast_select_fusion.8), channel_id=1, source_target_pairs={{0,1},{1,2},{2,3},{3,4},{4,5},{5,6},{6,7},{7,8},{8,9},{9,10},{10,1... | collective-permute-start | bytes 786440 | tf_op jit(solution)/shard_map/ppermute | solution.py:12
  499.3 170.2 %reduce-scatter.17.cloned.1.call-start = ((), (), s32[]{:S(2)}) async-start(), calls=%async_computation.23 | async-start | bytes 557056 | tf_op jit(solution)/shard_map/reduce_scatter | solution.py:41
  499.4 74.0 %collective-permute-start.4 = (bf16[128,1024]{1,0:T(8,128)(2,1)S(1)}, bf16[128,1024]{1,0:T(8,128)(2,1)S(1)}, u32[]{:S(2)}, u32[]{:S(2)}) collective-permute-start(bf16[128,1024]{1,0:T(8,128)(2,1)S(1)} %broadcast_select_fusion.7), channel_id=1, source_target_pairs={{0,1},{1,2},{2,3},{3,4},{4,5},{5,6},{6,7},{7,8},{8,9},{9,10},{10,1... | collective-permute-start | bytes 786440 | tf_op jit(solution)/shard_map/ppermute | solution.py:12
  559.2 51.2 %copy-start.3 = (bf16[6,8,1024]{2,1,0:T(8,128)(2,1)}, bf16[6,8,1024]{2,1,0:T(8,128)(2,1)S(1)}, u32[]{:S(2)}) copy-start(bf16[6,8,1024]{2,1,0:T(8,128)(2,1)S(1)} %get-tuple-element.14) | copy-start | bytes 294916
Sparse Core Ops, SparseCore 0:
  49.3 58.7 reduce-scatter.6
  162.5 57.7 reduce-scatter.8
  274.8 57.7 reduce-scatter.10
  387.1 57.7 reduce-scatter.12
  499.4 57.7 reduce-scatter.14
  611.8 57.7 reduce-scatter.16
where the time goes:
time: 680 us; the launch traced here: 679 us
  waiting for transfers between devices  323 us (48%)
  blocking collectives  265 us (39%)
  starting transfers between devices  46.8 us (7%)
  matrix products  20 us (3%)
  between operations  13.7 us (2%)
  local copies, waits for them, and re-layouts  7.43 us (1%)
    reduce_scatter x6, waiting for transfers between devices, on_device(): lax.psum_scatter(partial_value, 'lag', scatter_dimension=0, tiled=True)  315 us
    all_to_all x5, blocking collectives, on_device(): lax.all_to_all(history_now.reshape(patch_count, block_rows, unknowns), 'p...  98.8 us
    all_to_all x6, blocking collectives, on_device(): lax.all_to_all(chosen, 'patch', split_axis=0, concat_axis=0, tiled=True)  96 us
    all_gather x5, blocking collectives, on_device(): latest = lax.all_gather(own_rows, 'lag', axis=0, tiled=True)  70.7 us
    ppermute x5, starting transfers between devices, passed_along(): return lax.ppermute(value, axis, pairs)  33.6 us
  transfers between devices with their start and end apart: 12, of which 7 were waited for; matrix products, arithmetic and copies ran while one was open for 2% of the time, Pallas kernels for 0%

commit v1 on v0

v1 whole, which is shorter than its diff:
```python
import jax
import jax.numpy as jnp
from jax import lax
from jax.sharding import Mesh, PartitionSpec as P

STEPS = 6
PATCH = ("x", "z")
LAG = ("y", "core")
F32, BF16 = jnp.float32, jnp.bfloat16


def swap(value, axes):
    return lax.all_to_all(value, axes, split_axis=0, concat_axis=0, tiled=True)


def shift(value):
    size = lax.axis_size(LAG)
    return lax.ppermute(value, LAG, [(i, i + 1) for i in range(size - 1)])


def dot(a, b):
    return jnp.dot(a, b, preferred_element_type=F32)


def on_device(history, coupling, inverse, cotangent, targets):
    history, tile, target_row = history[0], coupling[0], targets[0]
    patches, lags = lax.axis_size(PATCH), lax.axis_size(LAG)
    rows, width = history.shape
    piece, own, back = rows // patches, rows // lags, STEPS - 1
    core = lax.axis_index("core")
    chips = lags // 2

    spread = [swap(history.reshape(patches, piece, width), PATCH)]
    for _ in range(back):
        spread.append(shift(spread[-1]))

    chunks = swap(tile.reshape(lags, width // lags, width), LAG)
    first = lax.all_gather(chunks[0], LAG, axis=0, tiled=True)
    later = lax.all_gather(chunks[1:back], LAG, axis=0)
    tiles = [first] + [later[:, i].reshape(width, width) for i in range(back - 1)]

    stacked = jnp.stack(spread, axis=1).reshape(patches, STEPS * piece, width)
    routed = swap(jnp.take(stacked, target_row, axis=0), PATCH)
    terms = dot(routed.reshape(-1, width), tile).reshape(chips, 2, STEPS * own, width)

    mine = target_row[lax.axis_index(PATCH)].astype(BF16)
    note = jnp.full((chips, own, width), mine, BF16)
    kept = lax.dynamic_index_in_dim(terms, core, 1, keepdims=False)
    sent = lax.dynamic_index_in_dim(terms, 1 - core, 1, keepdims=False).astype(BF16)
    got = lax.ppermute(jnp.concatenate([sent, note], 1), "core", [(0, 1), (1, 0)])
    both = (kept + got[:, : STEPS * own].astype(F32)).astype(BF16)
    other = got[:, STEPS * own :]
    half = own // 2
    note0 = jnp.where(core == 0, note, other)[:, :half]
    note1 = jnp.where(core == 0, other, note)[:, :half]
    parts = swap(jnp.concatenate([both, note0, note1], 1), "y")
    base = jnp.sum(parts[:, : STEPS * own].astype(F32), axis=0)
    base = base.reshape(2, STEPS, piece, width).transpose(1, 0, 2, 3).reshape(STEPS, own, width)
    listed = parts[:, STEPS * own :: half, 0].reshape(lags).astype(jnp.int32)

    states, results = [], []
    for k in range(STEPS):
        total = base[k]
        for l in range(k, 0, -1):
            chosen = lax.dynamic_index_in_dim(states[k - l], listed[l - 1], 0, keepdims=False)
            total = total + dot(chosen, tiles[l - 1])
        residual = (cotangent[k].astype(F32) - total).astype(BF16)
        adjoint = dot(residual, inverse).astype(BF16)
        results.append(adjoint)
        if k + 1 < STEPS:
            copies = jnp.broadcast_to(adjoint[None], (patches,) + adjoint.shape)
            states.append(swap(copies, PATCH))
    return jnp.stack(results)


def solution(mesh):
    fine = Mesh(mesh.devices.reshape(4, 8, 8, 2), PATCH + LAG)
    placed = (P(LAG, None, PATCH), P(LAG, PATCH, None), P(PATCH, None), P(None, LAG, PATCH), P(LAG, None))
    return jax.shard_map(
        on_device, mesh=fine, in_specs=placed, out_specs=P(None, LAG, PATCH), check_vma=False
    )
```

time: 680 us -> 377 us (0.55)
  the two profiles are of different devices: /device:TPU:25 before, /device:TPU:64 now
where the time goes in v1:
time: 377 us; the launch traced here: 375 us
  blocking collectives  124 us (33%)
  waiting for transfers between devices  94.1 us (25%)
  starting transfers between devices  68.9 us (18%)
  matrix products  31.2 us (8%)
  local copies, waits for them, and re-layouts  27.6 us (7%)
  between operations  23.1 us (6%)
  other arithmetic  6.4 us (2%)
    all_to_all x3, blocking collectives, swap(): return lax.all_to_all(value, axes, split_axis=0, concat_axis=0, tiled=True)  124 us
    all_to_all x6, waiting for transfers between devices, swap(): return lax.all_to_all(value, axes, split_axis=0, concat_axis=0, tiled=True)  86.8 us
    dot_general x17, matrix products, dot(): return jnp.dot(a, b, preferred_element_type=F32)  31.2 us
    all_to_all x6, starting transfers between devices, swap(): return lax.all_to_all(value, axes, split_axis=0, concat_axis=0, tiled=True)  31.1 us
    ppermute x5, starting transfers between devices, shift(): return lax.ppermute(value, LAG, [(i, i + 1) for i in range(size - 1)])  27.7 us
    ppermute x1, starting transfers between devices, on_device(): lax.ppermute(jnp.concatenate([sent, note], 1), 'core', [(0, 1), (1, 0)])  10.1 us
  transfers between devices with their start and end apart: 14, of which 12 were waited for; matrix products, arithmetic and copies ran while one was open for 12% of the time, Pallas kernels for 0%

profile of v1, /device:TPU:64, one launch (start us, length us, event | category | flops | bytes accessed | tf_op | source)
XLA Modules:
  0.0 375.3 jit_solution(810853981047763228)
XLA Ops:
  6.5 57.0 %all_to_all.45 = bf16[16,64,1024]{2,1,0:T(8,128)(2,1)S(1)} all-to-all(bf16[16,64,1024]{2,1,0:T(8,128)(2,1)} %bitcast.264), channel_id=1, replica_groups=mesh['x'=4,'z'=8,'y'=8,'core'=2] {'y','core'}, dimensions={0} | all-to-all | bytes 4194304 | tf_op jit(solution)/shard_map/all_to_all | solution.py:13
  63.5 1.4 copy-done.8
  64.9 0.7 slice.141
  65.6 1.9 slice.143
  67.6 25.6 %all_to_all.46 = bf16[32,4,1024]{2,1,0:T(4,128)(2,1)S(1)} all-to-all(bf16[32,4,1024]{2,1,0:T(4,128)(2,1)S(1)} %reshape_squeeze.19), channel_id=1, replica_groups=mesh['x'=4,'z'=8,'y'=8,'core'=2] {'x','z'}, dimensions={0} | all-to-all | bytes 524288 | tf_op jit(solution)/shard_map/all_to_all | solution.py:13
  93.3 2.0 collective-permute-start
  95.3 1.2 collective-permute-done
  96.5 5.9 %collective-permute-start.1 = (bf16[32,4,1024]{2,1,0:T(4,128)(2,1)S(1)}, bf16[32,4,1024]{2,1,0:T(4,128)(2,1)S(1)}, u32[]{:S(2)}, u32[]{:S(2)}) collective-permute-start(bf16[32,4,1024]{2,1,0:T(4,128)(2,1)S(1)} %collective-permute-done), channel_id=1, source_target_pairs={{0,1},{1,2},{2,3},{3,4},{4,5},{5,6},{6,7},{7,8},{8,9},{9,10},{10,1... | collective-permute-start | bytes 786440 | tf_op jit(solution)/shard_map/ppermute | solution.py:18
  102.5 1.1 collective-permute-done.1
  103.6 6.7 %collective-permute-start.2 = (bf16[32,4,1024]{2,1,0:T(4,128)(2,1)S(1)}, bf16[32,4,1024]{2,1,0:T(4,128)(2,1)S(1)}, u32[]{:S(2)}, u32[]{:S(2)}) collective-permute-start(bf16[32,4,1024]{2,1,0:T(4,128)(2,1)S(1)} %collective-permute-done.1), channel_id=1, source_target_pairs={{0,1},{1,2},{2,3},{3,4},{4,5},{5,6},{6,7},{7,8},{8,9},{9,10},{10,1... | collective-permute-start | bytes 786440 | tf_op jit(solution)/shard_map/ppermute | solution.py:18
  110.4 1.0 collective-permute-done.2
  111.4 6.5 %collective-permute-start.3 = (bf16[32,4,1024]{2,1,0:T(4,128)(2,1)S(1)}, bf16[32,4,1024]{2,1,0:T(4,128)(2,1)S(1)}, u32[]{:S(2)}, u32[]{:S(2)}) collective-permute-start(bf16[32,4,1024]{2,1,0:T(4,128)(2,1)S(1)} %collective-permute-done.2), channel_id=1, source_target_pairs={{0,1},{1,2},{2,3},{3,4},{4,5},{5,6},{6,7},{7,8},{8,9},{9,10},{10,1... | collective-permute-start | bytes 786440 | tf_op jit(solution)/shard_map/ppermute | solution.py:18
  118.2 0.9 collective-permute-done.3
  119.1 6.5 %collective-permute-start.4 = (bf16[32,4,1024]{2,1,0:T(4,128)(2,1)S(1)}, bf16[32,4,1024]{2,1,0:T(4,128)(2,1)S(1)}, u32[]{:S(2)}, u32[]{:S(2)}) collective-permute-start(bf16[32,4,1024]{2,1,0:T(4,128)(2,1)S(1)} %collective-permute-done.3), channel_id=1, source_target_pairs={{0,1},{1,2},{2,3},{3,4},{4,5},{5,6},{6,7},{7,8},{8,9},{9,10},{10,1... | collective-permute-start | bytes 786440 | tf_op jit(solution)/shard_map/ppermute | solution.py:18
  125.9 0.9 collective-permute-done.4
  126.9 0.5 copy.9
  127.4 2.0 copy.10
  129.4 3.2 gather_fusion
  132.6 2.8 broadcast_select_fusion
  135.4 6.0 %all-to-all-start.1 = ((bf16[32,24,1024]{2,1,0:T(8,128)(2,1)}), bf16[32,24,1024]{2,1,0:T(8,128)(2,1)}, u32[]{:S(2)}, u32[]{:S(2)}) async-start(bf16[32,24,1024]{2,1,0:T(8,128)(2,1)} %broadcast_select_fusion), calls=%async_computation.1 | async-start | bytes 3145728 | tf_op jit(solution)/shard_map/all_to_all | solution.py:13
  141.5 0.6 fusion.154
  142.1 32.2 %all-to-all-done.1 = bf16[32,24,1024]{2,1,0:T(8,128)(2,1)} async-done(((bf16[32,24,1024]{2,1,0:T(8,128)(2,1)}), bf16[32,24,1024]{2,1,0:T(8,128)(2,1)}, u32[]{:S(2)}, u32[]{:S(2)}) %all-to-all-start.1) | async-done | bytes 1572896 | tf_op jit(solution)/shard_map/all_to_all | solution.py:13
  174.3 3.9 %fusion = f32[8,2,48,1024]{3,2,1,0:T(8,128)S(1)} fusion(bf16[8,2,48,1024]{3,2,1,0:T(8,128)(2,1)} %bitcast.11, bf16[1,1024,1024]{2,1,0:T(8,128)(2,1)} %param.6), kind=kOutput, calls=%fused_computation.1 | convolution fusion | flops 1610612736 | bytes 6815744 | tf_op jit(solution)/shard_map/dot_general | solution.py:22
  178.3 0.8 concatenate.6
  179.0 0.7 copy-done.9
  179.8 10.1 %collective-permute-start.5 = (bf16[8,56,1024]{2,1,0:T(8,128)(2,1)S(1)}, bf16[8,56,1024]{2,1,0:T(8,128)(2,1)}, u32[]{:S(2)}, u32[]{:S(2)}) collective-permute-start(bf16[8,56,1024]{2,1,0:T(8,128)(2,1)S(1)} %concatenate.6), channel_id=1, source_target_pairs={{0,1},{1,0},{2,3},{3,2},{4,5},{5,4},{6,7},{7,6},{8,9},{9,8},{10,11... | collective-permute-start | bytes 2752520 | tf_op jit(solution)/shard_map/ppermute | solution.py:50
  189.8 2.2 collective-permute-done.5
  192.0 0.9 slice.135
  192.9 0.7 broadcast_select_fusion.2
  193.7 1.9 fusion.12
  195.7 41.3 %all_to_all.47 = bf16[8,56,1024]{2,1,0:T(8,128)(2,1)S(1)} all-to-all(bf16[8,56,1024]{2,1,0:T(8,128)(2,1)S(1)} %pad_maximum_fusion), channel_id=1, replica_groups=mesh['x'=4,'z'=8,'y'=8,'core'=2] {'y'}, dimensions={0} | all-to-all | bytes 1835008 | tf_op jit(solution)/shard_map/all_to_all | solution.py:13
  237.2 0.7 fusion.152
  237.9 1.7 constant_dynamic-update-slice_fusion.4
  239.6 0.8 broadcast_in_dim.25
  240.4 5.4 %all-to-all-start.3 = ((bf16[32,8,1024]{2,1,0:T(8,128)(2,1)}), bf16[32,8,1024]{2,1,0:T(8,128)(2,1)S(1)}, u32[]{:S(2)}, u32[]{:S(2)}) async-start(bf16[32,8,1024]{2,1,0:T(8,128)(2,1)} %broadcast_in_dim.25), calls=%async_computation.3 | async-start | bytes 1048576 | tf_op jit(solution)/shard_map/all_to_all | solution.py:13
  246.2 0.7 fusion.153
  248.1 0.8 squeeze.117
  249.6 14.0 %all-to-all-done.3 = bf16[32,8,1024]{2,1,0:T(8,128)(2,1)S(1)} async-done(((bf16[32,8,1024]{2,1,0:T(8,128)(2,1)}), bf16[32,8,1024]{2,1,0:T(8,128)(2,1)S(1)}, u32[]{:S(2)}, u32[]{:S(2)}) %all-to-all-start.3) | async-done | bytes 524320 | tf_op jit(solution)/shard_map/all_to_all | solution.py:13
  263.6 2.9 constant_dynamic-update-slice_fusion.3
  266.5 0.9 broadcast_in_dim.26
  267.3 4.8 %all-to-all-start.5 = ((bf16[32,8,1024]{2,1,0:T(8,128)(2,1)}), bf16[32,8,1024]{2,1,0:T(8,128)(2,1)S(1)}, u32[]{:S(2)}, u32[]{:S(2)}) async-start(bf16[32,8,1024]{2,1,0:T(8,128)(2,1)} %broadcast_in_dim.26), calls=%async_computation.5 | async-start | bytes 1048576 | tf_op jit(solution)/shard_map/all_to_all | solution.py:13
  273.9 5.8 %fusion.151 = (bf16[16,1,64,1024]{3,2,1,0:T(8,128)(2,1)}, bf16[16,1,64,1024]{3,2,1,0:T(8,128)(2,1)}, bf16[16,1,64,1024]{3,2,1,0:T(8,128)(2,1)}, bf16[16,1,64,1024]{3,2,1,0:T(8,128)(2,1)S(1)}) fusion(bf16[16,4,64,1024]{3,2,1,0:T(8,128)(2,1)} %bitcast.261), kind=kLoop, calls=%fused_computation.137 | loop fusion | bytes 16777216 | tf_op jit(solution)/shard_map/slice | solution.py:40
  279.8 1.3 copy-done.1
  281.5 7.6 %all-to-all-done.5 = bf16[32,8,1024]{2,1,0:T(8,128)(2,1)S(1)} async-done(((bf16[32,8,1024]{2,1,0:T(8,128)(2,1)}), bf16[32,8,1024]{2,1,0:T(8,128)(2,1)S(1)}, u32[]{:S(2)}, u32[]{:S(2)}) %all-to-all-start.5) | async-done | bytes 524320 | tf_op jit(solution)/shard_map/all_to_all | solution.py:13
  289.1 2.9 constant_dynamic-update-slice_fusion.2
  292.0 0.9 broadcast_in_dim.48
  292.8 4.9 %all-to-all-start.6 = ((bf16[32,8,1024]{2,1,0:T(8,128)(2,1)}), bf16[32,8,1024]{2,1,0:T(8,128)(2,1)}, u32[]{:S(2)}, u32[]{:S(2)}) async-start(bf16[32,8,1024]{2,1,0:T(8,128)(2,1)} %broadcast_in_dim.48), calls=%async_computation.6 | async-start | bytes 1048576 | tf_op jit(solution)/shard_map/all_to_all | solution.py:13
  299.9 2.1 convolution_add_fusion.8
  302.1 0.4 convolution_add_fusion.7
  302.4 12.2 %all-to-all-done.6 = bf16[32,8,1024]{2,1,0:T(8,128)(2,1)} async-done(((bf16[32,8,1024]{2,1,0:T(8,128)(2,1)}), bf16[32,8,1024]{2,1,0:T(8,128)(2,1)}, u32[]{:S(2)}, u32[]{:S(2)}) %all-to-all-start.6) | async-done | bytes 524320 | tf_op jit(solution)/shard_map/all_to_all | solution.py:13
  314.6 2.9 constant_dynamic-update-slice_fusion.1
  317.5 0.9 broadcast_in_dim.49
  318.4 4.9 %all-to-all-start.7 = ((bf16[32,8,1024]{2,1,0:T(8,128)(2,1)}), bf16[32,8,1024]{2,1,0:T(8,128)(2,1)}, u32[]{:S(2)}, u32[]{:S(2)}) async-start(bf16[32,8,1024]{2,1,0:T(8,128)(2,1)} %broadcast_in_dim.49), calls=%async_computation.7 | async-start | bytes 1048576 | tf_op jit(solution)/shard_map/all_to_all | solution.py:13
  327.1 2.1 convolution_add_fusion.6
  329.9 1.1 convolution_add_fusion.4
  331.0 9.1 %all-to-all-done.7 = bf16[32,8,1024]{2,1,0:T(8,128)(2,1)} async-done(((bf16[32,8,1024]{2,1,0:T(8,128)(2,1)}), bf16[32,8,1024]{2,1,0:T(8,128)(2,1)}, u32[]{:S(2)}, u32[]{:S(2)}) %all-to-all-start.7) | async-done | bytes 524320 | tf_op jit(solution)/shard_map/all_to_all | solution.py:13
  340.1 2.9 constant_dynamic-update-slice_fusion
  343.0 0.9 broadcast_in_dim.50
  343.9 4.9 %all-to-all-start.8 = ((bf16[32,8,1024]{2,1,0:T(8,128)(2,1)}), bf16[32,8,1024]{2,1,0:T(8,128)(2,1)}, u32[]{:S(2)}, u32[]{:S(2)}) async-start(bf16[32,8,1024]{2,1,0:T(8,128)(2,1)} %broadcast_in_dim.50), calls=%async_computation.8 | async-start | bytes 1048576 | tf_op jit(solution)/shard_map/all_to_all | solution.py:13
  348.8 2.1 convolution_add_fusion.3
  351.7 1.1 convolution_add_fusion.1
  352.8 1.1 convolution_add_fusion
  353.9 11.7 %all-to-all-done.8 = bf16[32,8,1024]{2,1,0:T(8,128)(2,1)} async-done(((bf16[32,8,1024]{2,1,0:T(8,128)(2,1)}), bf16[32,8,1024]{2,1,0:T(8,128)(2,1)}, u32[]{:S(2)}, u32[]{:S(2)}) %all-to-all-start.8) | async-done | bytes 524320 | tf_op jit(solution)/shard_map/all_to_all | solution.py:13
  365.5 2.9 fusion.59
  (62 shorter events, 3.7 us)
Async XLA Ops:
  6.5 231.3 %copy-start = (bf16[1024,1024]{1,0:T(8,128)(2,1)S(1)}, bf16[1024,1024]{1,0:T(8,128)(2,1)}, u32[]{:S(2)}) copy-start(bf16[1024,1024]{1,0:T(8,128)(2,1)} %param.7) | copy-start | bytes 6291460
  6.5 243.0 %all-gather.5.cloned.1.call-start = ((), (), s32[]{:S(2)}) async-start(), calls=%async_computation.9 | async-start | bytes 2228224 | tf_op jit(solution)/shard_map/all_gather | solution.py:38
  6.5 61.0 %copy-start.10 = (bf16[1,128,1024]{2,1,0:T(8,128)(2,1)S(1)}, bf16[1,128,1024]{2,1,0:T(8,128)(2,1)}, u32[]{:S(2)}) copy-start(bf16[1,128,1024]{2,1,0:T(8,128)(2,1)} %param.5) | copy-start | bytes 786436
  63.5 1.4 copy-start.8
  64.9 37.6 %copy-start.16 = (s32[1,32]{1,0:T(1,128)S(1)}, s32[1,32]{1,0:T(1,128)}, u32[]{:S(2)}) copy-start(s32[1,32]{1,0:T(1,128)} %param.9) | copy-start | bytes 388
  65.6 208.3 %all-gather.7.cloned.1.call-start = ((), (), s32[]{:S(2)}) async-start(), calls=%async_computation.10 | async-start | bytes 8912896 | tf_op jit(solution)/shard_map/all_gather | solution.py:39
  93.3 3.2 collective-permute-start
  96.5 7.1 %collective-permute-start.1 = (bf16[32,4,1024]{2,1,0:T(4,128)(2,1)S(1)}, bf16[32,4,1024]{2,1,0:T(4,128)(2,1)S(1)}, u32[]{:S(2)}, u32[]{:S(2)}) collective-permute-start(bf16[32,4,1024]{2,1,0:T(4,128)(2,1)S(1)} %collective-permute-done), channel_id=1, source_target_pairs={{0,1},{1,2},{2,3},{3,4},{4,5},{5,6},{6,7},{7,8},{8,9},{9,10},{10,1... | collective-permute-start | bytes 786440 | tf_op jit(solution)/shard_map/ppermute | solution.py:18
  103.6 7.8 %collective-permute-start.2 = (bf16[32,4,1024]{2,1,0:T(4,128)(2,1)S(1)}, bf16[32,4,1024]{2,1,0:T(4,128)(2,1)S(1)}, u32[]{:S(2)}, u32[]{:S(2)}) collective-permute-start(bf16[32,4,1024]{2,1,0:T(4,128)(2,1)S(1)} %collective-permute-done.1), channel_id=1, source_target_pairs={{0,1},{1,2},{2,3},{3,4},{4,5},{5,6},{6,7},{7,8},{8,9},{9,10},{10,1... | collective-permute-start | bytes 786440 | tf_op jit(solution)/shard_map/ppermute | solution.py:18
  111.4 7.7 %collective-permute-start.3 = (bf16[32,4,1024]{2,1,0:T(4,128)(2,1)S(1)}, bf16[32,4,1024]{2,1,0:T(4,128)(2,1)S(1)}, u32[]{:S(2)}, u32[]{:S(2)}) collective-permute-start(bf16[32,4,1024]{2,1,0:T(4,128)(2,1)S(1)} %collective-permute-done.2), channel_id=1, source_target_pairs={{0,1},{1,2},{2,3},{3,4},{4,5},{5,6},{6,7},{7,8},{8,9},{9,10},{10,1... | collective-permute-start | bytes 786440 | tf_op jit(solution)/shard_map/ppermute | solution.py:18
  119.1 7.7 %collective-permute-start.4 = (bf16[32,4,1024]{2,1,0:T(4,128)(2,1)S(1)}, bf16[32,4,1024]{2,1,0:T(4,128)(2,1)S(1)}, u32[]{:S(2)}, u32[]{:S(2)}) collective-permute-start(bf16[32,4,1024]{2,1,0:T(4,128)(2,1)S(1)} %collective-permute-done.3), channel_id=1, source_target_pairs={{0,1},{1,2},{2,3},{3,4},{4,5},{5,6},{6,7},{7,8},{8,9},{9,10},{10,1... | collective-permute-start | bytes 786440 | tf_op jit(solution)/shard_map/ppermute | solution.py:18
  135.4 38.8 %all-to-all-start.1 = ((bf16[32,24,1024]{2,1,0:T(8,128)(2,1)}), bf16[32,24,1024]{2,1,0:T(8,128)(2,1)}, u32[]{:S(2)}, u32[]{:S(2)}) async-start(bf16[32,24,1024]{2,1,0:T(8,128)(2,1)} %broadcast_select_fusion), calls=%async_computation.1 | async-start | bytes 3145728 | tf_op jit(solution)/shard_map/all_to_all | solution.py:13
  178.1 1.6 copy-start.9
  179.8 12.3 %collective-permute-start.5 = (bf16[8,56,1024]{2,1,0:T(8,128)(2,1)S(1)}, bf16[8,56,1024]{2,1,0:T(8,128)(2,1)}, u32[]{:S(2)}, u32[]{:S(2)}) collective-permute-start(bf16[8,56,1024]{2,1,0:T(8,128)(2,1)S(1)} %concatenate.6), channel_id=1, source_target_pairs={{0,1},{1,0},{2,3},{3,2},{4,5},{5,4},{6,7},{7,6},{8,9},{9,8},{10,11... | collective-permute-start | bytes 2752520 | tf_op jit(solution)/shard_map/ppermute | solution.py:50
  240.4 23.2 %all-to-all-start.3 = ((bf16[32,8,1024]{2,1,0:T(8,128)(2,1)}), bf16[32,8,1024]{2,1,0:T(8,128)(2,1)S(1)}, u32[]{:S(2)}, u32[]{:S(2)}) async-start(bf16[32,8,1024]{2,1,0:T(8,128)(2,1)} %broadcast_in_dim.25), calls=%async_computation.3 | async-start | bytes 1048576 | tf_op jit(solution)/shard_map/all_to_all | solution.py:13
  263.6 9.7 %copy-start.14 = (f32[1,2,4,1024]{3,2,0,1:T(4,128)S(1)}, f32[1,2,4,1024]{3,2,0,1:T(4,128)}, u32[]{:S(2)}) copy-start(f32[1,2,4,1024]{3,2,0,1:T(4,128)} %get-tuple-element.12) | copy-start | bytes 98308
  267.3 21.8 %all-to-all-start.5 = ((bf16[32,8,1024]{2,1,0:T(8,128)(2,1)}), bf16[32,8,1024]{2,1,0:T(8,128)(2,1)S(1)}, u32[]{:S(2)}, u32[]{:S(2)}) async-start(bf16[32,8,1024]{2,1,0:T(8,128)(2,1)} %broadcast_in_dim.26), calls=%async_computation.5 | async-start | bytes 1048576 | tf_op jit(solution)/shard_map/all_to_all | solution.py:13
  279.7 1.4 copy-start.1
  279.7 9.4 %copy-start.15 = (bf16[6,8,1024]{2,1,0:T(8,128)(2,1)S(1)}, bf16[6,8,1024]{2,1,0:T(8,128)(2,1)}, u32[]{:S(2)}) copy-start(bf16[6,8,1024]{2,1,0:T(8,128)(2,1)} %param.8) | copy-start | bytes 294916
  289.1 10.0 %copy-start.13 = (f32[1,2,4,1024]{3,2,0,1:T(4,128)S(1)}, f32[1,2,4,1024]{3,2,0,1:T(4,128)}, u32[]{:S(2)}) copy-start(f32[1,2,4,1024]{3,2,0,1:T(4,128)} %get-tuple-element.11) | copy-start | bytes 98308
  292.8 21.8 %all-to-all-start.6 = ((bf16[32,8,1024]{2,1,0:T(8,128)(2,1)}), bf16[32,8,1024]{2,1,0:T(8,128)(2,1)}, u32[]{:S(2)}, u32[]{:S(2)}) async-start(bf16[32,8,1024]{2,1,0:T(8,128)(2,1)} %broadcast_in_dim.48), calls=%async_computation.6 | async-start | bytes 1048576 | tf_op jit(solution)/shard_map/all_to_all | solution.py:13
  299.8 2.2 copy-start.2
  314.6 11.1 %copy-start.12 = (f32[1,2,4,1024]{3,2,0,1:T(4,128)S(1)}, f32[1,2,4,1024]{3,2,0,1:T(4,128)}, u32[]{:S(2)}) copy-start(f32[1,2,4,1024]{3,2,0,1:T(4,128)} %get-tuple-element.9) | copy-start | bytes 98308
  314.6 11.2 %copy-start.11 = (f32[1,2,4,1024]{3,2,0,1:T(4,128)S(1)}, f32[1,2,4,1024]{3,2,0,1:T(4,128)}, u32[]{:S(2)}) copy-start(f32[1,2,4,1024]{3,2,0,1:T(4,128)} %get-tuple-element.10) | copy-start | bytes 98308
  318.4 21.7 %all-to-all-start.7 = ((bf16[32,8,1024]{2,1,0:T(8,128)(2,1)}), bf16[32,8,1024]{2,1,0:T(8,128)(2,1)}, u32[]{:S(2)}, u32[]{:S(2)}) async-start(bf16[32,8,1024]{2,1,0:T(8,128)(2,1)} %broadcast_in_dim.49), calls=%async_computation.7 | async-start | bytes 1048576 | tf_op jit(solution)/shard_map/all_to_all | solution.py:13
  327.1 2.2 copy-start.5
  327.1 2.8 copy-start.3
  343.9 21.7 %all-to-all-start.8 = ((bf16[32,8,1024]{2,1,0:T(8,128)(2,1)}), bf16[32,8,1024]{2,1,0:T(8,128)(2,1)}, u32[]{:S(2)}, u32[]{:S(2)}) async-start(bf16[32,8,1024]{2,1,0:T(8,128)(2,1)} %broadcast_in_dim.50), calls=%async_computation.8 | async-start | bytes 1048576 | tf_op jit(solution)/shard_map/all_to_all | solution.py:13
  348.8 2.2 copy-start.7
  348.8 2.8 copy-start.6
  351.0 1.7 copy-start.4
Sparse Core Ops, SparseCore 0:
  65.7 42.7 all-gather.4
  110.6 58.8 all-gather.6

commit v2 on v1

--- a/solution.py
+++ b/solution.py
@@ -13,11 +13,6 @@
     return lax.all_to_all(value, axes, split_axis=0, concat_axis=0, tiled=True)
 
 
-def shift(value):
-    size = lax.axis_size(LAG)
-    return lax.ppermute(value, LAG, [(i, i + 1) for i in range(size - 1)])
-
-
 def dot(a, b):
     return jnp.dot(a, b, preferred_element_type=F32)
 
@@ -30,33 +25,32 @@
     core = lax.axis_index("core")
     chips = lags // 2
 
-    spread = [swap(history.reshape(patches, piece, width), PATCH)]
-    for _ in range(back):
-        spread.append(shift(spread[-1]))
+    spread = swap(history.reshape(patches, piece, width), PATCH)
+    mine = target_row[lax.axis_index(PATCH)].astype(BF16)
+    note = jnp.stack([jnp.full((piece, width), mine, BF16), jnp.zeros((piece, width), BF16)])
+    known = lax.all_gather(jnp.concatenate([spread, note]), LAG, axis=0, tiled=True)
+    blocks = patches + 2
+    listed = known[patches::blocks, 0, 0].astype(jnp.int32)
 
-    chunks = swap(tile.reshape(lags, width // lags, width), LAG)
+    _, tile_after = lax.optimization_barrier((spread, tile))
+    chunks = swap(tile_after.reshape(lags, width // lags, width), LAG)
     first = lax.all_gather(chunks[0], LAG, axis=0, tiled=True)
     later = lax.all_gather(chunks[1:back], LAG, axis=0)
     tiles = [first] + [later[:, i].reshape(width, width) for i in range(back - 1)]
 
-    stacked = jnp.stack(spread, axis=1).reshape(patches, STEPS * piece, width)
-    routed = swap(jnp.take(stacked, target_row, axis=0), PATCH)
+    lag = lax.axis_index(LAG)
+    earlier = lag - jnp.arange(STEPS)
+    index = jnp.where(earlier >= 0, earlier * blocks + target_row[:, None], patches + 1)
+    chosen = known.at[index].get(mode="promise_in_bounds")
+    routed = swap(chosen.reshape(patches, STEPS * piece, width), PATCH)
     terms = dot(routed.reshape(-1, width), tile).reshape(chips, 2, STEPS * own, width)
 
-    mine = target_row[lax.axis_index(PATCH)].astype(BF16)
-    note = jnp.full((chips, own, width), mine, BF16)
     kept = lax.dynamic_index_in_dim(terms, core, 1, keepdims=False)
     sent = lax.dynamic_index_in_dim(terms, 1 - core, 1, keepdims=False).astype(BF16)
-    got = lax.ppermute(jnp.concatenate([sent, note], 1), "core", [(0, 1), (1, 0)])
-    both = (kept + got[:, : STEPS * own].astype(F32)).astype(BF16)
-    other = got[:, STEPS * own :]
-    half = own // 2
-    note0 = jnp.where(core == 0, note, other)[:, :half]
-    note1 = jnp.where(core == 0, other, note)[:, :half]
-    parts = swap(jnp.concatenate([both, note0, note1], 1), "y")
-    base = jnp.sum(parts[:, : STEPS * own].astype(F32), axis=0)
+    got = lax.ppermute(sent, "core", [(0, 1), (1, 0)])
+    both = (kept + got.astype(F32)).astype(BF16)
+    base = jnp.sum(swap(both, "y").astype(F32), axis=0)
     base = base.reshape(2, STEPS, piece, width).transpose(1, 0, 2, 3).reshape(STEPS, own, width)
-    listed = parts[:, STEPS * own :: half, 0].reshape(lags).astype(jnp.int32)
 
     states, results = [], []
     for k in range(STEPS):

time: 377 us -> 354 us (0.939)
  starting transfers between devices: 68.9 us -> 47.9 us
  waiting for transfers between devices: 94.1 us -> 106 us
  blocking collectives: 124 us -> 113 us
  matrix products: 31.2 us -> 27.4 us
    ppermute x6 -> x1, starting transfers between devices: 37.8 us -> 3.5 us  [on_device(): got = lax.ppermute(sent, 'core', [(0, 1), (1, 0)])]
    all_to_all x6 -> x7, waiting for transfers between devices: 86.8 us -> 103 us  [swap(): return lax.all_to_all(value, axes, split_axis=0, concat_axis=0, tiled=True)]
    all_to_all x6 -> x7, starting transfers between devices: 31.1 us -> 44.3 us  [swap(): return lax.all_to_all(value, axes, split_axis=0, concat_axis=0, tiled=True)]
    all_to_all x3 -> x2, blocking collectives: 124 us -> 113 us  [swap(): return lax.all_to_all(value, axes, split_axis=0, concat_axis=0, tiled=True)]
    ppermute x6 -> x1, waiting for transfers between devices: 7.27 us -> 2.21 us  [on_device(): got = lax.ppermute(sent, 'core', [(0, 1), (1, 0)])]
    dot_general x17, matrix products: 31.2 us -> 27.4 us  [dot(): return jnp.dot(a, b, preferred_element_type=F32)]
  transfers between devices with their start and end apart: 14 -> 11, of which waited for: 12 -> 8; matrix products, arithmetic and copies ran while one was open for 12% -> 12% of each run, Pallas kernels for 0% -> 0%
where the time goes in v2:
time: 354 us; the launch traced here: 352 us
  blocking collectives  113 us (32%)
  waiting for transfers between devices  106 us (30%)
  starting transfers between devices  47.9 us (14%)
  local copies, waits for them, and re-layouts  30.5 us (9%)
  matrix products  27.4 us (8%)
  between operations  22.7 us (6%)
  other arithmetic  5.05 us (1%)
    all_to_all x2, blocking collectives, swap(): return lax.all_to_all(value, axes, split_axis=0, concat_axis=0, tiled=True)  113 us
    all_to_all x7, waiting for transfers between devices, swap(): return lax.all_to_all(value, axes, split_axis=0, concat_axis=0, tiled=True)  103 us
    all_to_all x7, starting transfers between devices, swap(): return lax.all_to_all(value, axes, split_axis=0, concat_axis=0, tiled=True)  44.3 us
    dot_general x17, matrix products, dot(): return jnp.dot(a, b, preferred_element_type=F32)  27.4 us
  transfers between devices with their start and end apart: 11, of which 8 were waited for; matrix products, arithmetic and copies ran while one was open for 12% of the time, Pallas kernels for 0%

profile of v2, /device:TPU:64, one launch (start us, length us, event | category | flops | bytes accessed | tf_op | source)
XLA Modules:
  0.0 352.1 jit_solution(9957086020239160920)
XLA Ops:
  6.5 1.9 reshape_squeeze.15
  8.4 12.6 %all-to-all-start = ((bf16[32,4,1024]{2,1,0:T(4,128)(2,1)}), bf16[32,4,1024]{2,1,0:T(4,128)(2,1)S(1)}, u32[]{:S(2)}, u32[]{:S(2)}) async-start(bf16[32,4,1024]{2,1,0:T(4,128)(2,1)} %reshape_squeeze.15), calls=%async_computation | async-start | bytes 524288 | tf_op jit(solution)/shard_map/all_to_all | solution.py:13
  21.1 1.2 fusion.155
  22.3 0.7 pad.1.clone
  23.0 0.1 pad.2.clone
  23.1 10.2 %all-to-all-done = bf16[32,4,1024]{2,1,0:T(4,128)(2,1)S(1)} async-done(((bf16[32,4,1024]{2,1,0:T(4,128)(2,1)}), bf16[32,4,1024]{2,1,0:T(4,128)(2,1)S(1)}, u32[]{:S(2)}, u32[]{:S(2)}) %all-to-all-start) | async-done | bytes 262176 | tf_op jit(solution)/shard_map/all_to_all | solution.py:13
  33.3 0.9 maximum_maximum_fusion
  34.3 76.2 %all_to_all.45 = bf16[16,64,1024]{2,1,0:T(8,128)(2,1)S(1)} all-to-all(bf16[16,64,1024]{2,1,0:T(8,128)(2,1)} %bitcast.250), channel_id=1, replica_groups=mesh['x'=4,'z'=8,'y'=8,'core'=2] {'y','core'}, dimensions={0} | all-to-all | bytes 4194304 | tf_op jit(solution)/shard_map/all_to_all | solution.py:13
  110.6 1.3 copy-done.8
  111.9 0.7 slice.122
  112.6 1.9 slice.125
  114.6 0.1 compare_select_fusion
  114.6 0.1 reshape.149
  114.8 5.5 %gather_fusion = bf16[192,4,1024]{2,1,0:T(4,128)(2,1)} fusion(bf16[544,4,1024]{2,1,0:T(4,128)(2,1)} %all-gather.6.cloned.1.call-done, s32[1024]{0:T(1024)S(1)} %pad_clamp_fusion), kind=kCustom, calls=%fused_computation | custom fusion | bytes 3146496 | tf_op jit(solution)/shard_map/gather | solution.py:44
  120.3 3.5 reshape.138
  123.8 4.7 %all-to-all-start.1 = ((bf16[32,24,1024]{2,1,0:T(8,128)(2,1)}), bf16[32,24,1024]{2,1,0:T(8,128)(2,1)}, u32[]{:S(2)}, u32[]{:S(2)}) async-start(bf16[32,24,1024]{2,1,0:T(8,128)(2,1)} %reshape.138), calls=%async_computation.1 | async-start | bytes 3145728 | tf_op jit(solution)/shard_map/all_to_all | solution.py:13
  128.5 39.2 %all-to-all-done.1 = bf16[32,24,1024]{2,1,0:T(8,128)(2,1)} async-done(((bf16[32,24,1024]{2,1,0:T(8,128)(2,1)}), bf16[32,24,1024]{2,1,0:T(8,128)(2,1)}, u32[]{:S(2)}, u32[]{:S(2)}) %all-to-all-start.1) | async-done | bytes 1572896 | tf_op jit(solution)/shard_map/all_to_all | solution.py:13
  167.7 3.9 %fusion = f32[8,2,48,1024]{3,2,1,0:T(8,128)S(1)} fusion(bf16[8,2,48,1024]{3,2,1,0:T(8,128)(2,1)} %bitcast.3, bf16[1,1024,1024]{2,1,0:T(8,128)(2,1)} %param.6), kind=kOutput, calls=%fused_computation.1 | convolution fusion | flops 1610612736 | bytes 6815744 | tf_op jit(solution)/shard_map/dot_general | solution.py:17
  171.6 1.6 copy-done.9
  173.2 0.1 fusion.70
  173.3 3.5 collective-permute-start
  176.9 2.2 collective-permute-done
  179.1 1.9 fusion.12
  181.0 36.7 %all_to_all.46 = bf16[8,48,1024]{2,1,0:T(8,128)(2,1)S(1)} all-to-all(bf16[8,48,1024]{2,1,0:T(8,128)(2,1)S(1)} %fusion.12), channel_id=1, replica_groups=mesh['x'=4,'z'=8,'y'=8,'core'=2] {'y'}, dimensions={0} | all-to-all | bytes 1572864 | tf_op jit(solution)/shard_map/all_to_all | solution.py:13
  217.7 0.1 convert_reduce_fusion
  217.9 0.4 bitcast_dynamic-update-slice_fusion.4
  218.3 0.9 broadcast_in_dim.20
  219.2 7.3 %all-to-all-start.3 = ((bf16[32,8,1024]{2,1,0:T(8,128)(2,1)}), bf16[32,8,1024]{2,1,0:T(8,128)(2,1)S(1)}, u32[]{:S(2)}, u32[]{:S(2)}) async-start(bf16[32,8,1024]{2,1,0:T(8,128)(2,1)} %broadcast_in_dim.20), calls=%async_computation.3 | async-start | bytes 1048576 | tf_op jit(solution)/shard_map/all_to_all | solution.py:13
  226.5 0.7 slice_convert_fusion
  227.3 0.6 fusion.154
  229.8 13.7 %all-to-all-done.3 = bf16[32,8,1024]{2,1,0:T(8,128)(2,1)S(1)} async-done(((bf16[32,8,1024]{2,1,0:T(8,128)(2,1)}), bf16[32,8,1024]{2,1,0:T(8,128)(2,1)S(1)}, u32[]{:S(2)}, u32[]{:S(2)}) %all-to-all-start.3) | async-done | bytes 524320 | tf_op jit(solution)/shard_map/all_to_all | solution.py:13
  243.5 2.3 bitcast_dynamic-update-slice_fusion.3
  245.7 0.9 broadcast_in_dim.21
  246.6 4.9 %all-to-all-start.5 = ((bf16[32,8,1024]{2,1,0:T(8,128)(2,1)}), bf16[32,8,1024]{2,1,0:T(8,128)(2,1)S(1)}, u32[]{:S(2)}, u32[]{:S(2)}) async-start(bf16[32,8,1024]{2,1,0:T(8,128)(2,1)} %broadcast_in_dim.21), calls=%async_computation.5 | async-start | bytes 1048576 | tf_op jit(solution)/shard_map/all_to_all | solution.py:13
  253.2 5.8 %fusion.152 = (bf16[16,1,64,1024]{3,2,1,0:T(8,128)(2,1)}, bf16[16,1,64,1024]{3,2,1,0:T(8,128)(2,1)}, bf16[16,1,64,1024]{3,2,1,0:T(8,128)(2,1)}, bf16[16,1,64,1024]{3,2,1,0:T(8,128)(2,1)S(1)}) fusion(bf16[16,4,64,1024]{3,2,1,0:T(8,128)(2,1)} %bitcast.248), kind=kLoop, calls=%fused_computation.128 | loop fusion | bytes 16777216 | tf_op jit(solution)/shard_map/slice | solution.py:39
  259.0 1.4 copy-done.1
  260.4 0.4 convolution_add_fusion.9
  260.8 7.5 %all-to-all-done.5 = bf16[32,8,1024]{2,1,0:T(8,128)(2,1)S(1)} async-done(((bf16[32,8,1024]{2,1,0:T(8,128)(2,1)}), bf16[32,8,1024]{2,1,0:T(8,128)(2,1)S(1)}, u32[]{:S(2)}, u32[]{:S(2)}) %all-to-all-start.5) | async-done | bytes 524320 | tf_op jit(solution)/shard_map/all_to_all | solution.py:13
  268.3 2.3 bitcast_dynamic-update-slice_fusion.2
  270.6 0.9 broadcast_in_dim.22
  271.4 4.9 %all-to-all-start.6 = ((bf16[32,8,1024]{2,1,0:T(8,128)(2,1)}), bf16[32,8,1024]{2,1,0:T(8,128)(2,1)}, u32[]{:S(2)}, u32[]{:S(2)}) async-start(bf16[32,8,1024]{2,1,0:T(8,128)(2,1)} %broadcast_in_dim.22), calls=%async_computation.6 | async-start | bytes 1048576 | tf_op jit(solution)/shard_map/all_to_all | solution.py:13
  278.3 2.1 convolution_add_fusion.8
  280.4 0.1 copy-done.2
  280.5 0.4 convolution_add_fusion.7
  280.9 12.3 %all-to-all-done.6 = bf16[32,8,1024]{2,1,0:T(8,128)(2,1)} async-done(((bf16[32,8,1024]{2,1,0:T(8,128)(2,1)}), bf16[32,8,1024]{2,1,0:T(8,128)(2,1)}, u32[]{:S(2)}, u32[]{:S(2)}) %all-to-all-start.6) | async-done | bytes 524320 | tf_op jit(solution)/shard_map/all_to_all | solution.py:13
  293.2 2.3 bitcast_dynamic-update-slice_fusion.1
  295.4 0.9 broadcast_in_dim.23
  296.3 4.9 %all-to-all-start.7 = ((bf16[32,8,1024]{2,1,0:T(8,128)(2,1)}), bf16[32,8,1024]{2,1,0:T(8,128)(2,1)}, u32[]{:S(2)}, u32[]{:S(2)}) async-start(bf16[32,8,1024]{2,1,0:T(8,128)(2,1)} %broadcast_in_dim.23), calls=%async_computation.7 | async-start | bytes 1048576 | tf_op jit(solution)/shard_map/all_to_all | solution.py:13
  305.1 2.1 convolution_add_fusion.6
  307.3 0.1 copy-done.5
  307.3 0.4 convolution_add_fusion.5
  307.7 0.2 copy-done.3
  308.0 1.1 convolution_add_fusion.4
  309.1 8.9 %all-to-all-done.7 = bf16[32,8,1024]{2,1,0:T(8,128)(2,1)} async-done(((bf16[32,8,1024]{2,1,0:T(8,128)(2,1)}), bf16[32,8,1024]{2,1,0:T(8,128)(2,1)}, u32[]{:S(2)}, u32[]{:S(2)}) %all-to-all-start.7) | async-done | bytes 524320 | tf_op jit(solution)/shard_map/all_to_all | solution.py:13
  318.0 2.3 bitcast_dynamic-update-slice_fusion
  320.2 0.9 broadcast_in_dim.24
  321.1 4.9 %all-to-all-start.8 = ((bf16[32,8,1024]{2,1,0:T(8,128)(2,1)}), bf16[32,8,1024]{2,1,0:T(8,128)(2,1)}, u32[]{:S(2)}, u32[]{:S(2)}) async-start(bf16[32,8,1024]{2,1,0:T(8,128)(2,1)} %broadcast_in_dim.24), calls=%async_computation.8 | async-start | bytes 1048576 | tf_op jit(solution)/shard_map/all_to_all | solution.py:13
  326.1 2.1 convolution_add_fusion.3
  328.3 0.4 convolution_add_fusion.2
  328.6 0.2 copy-done.6
  328.9 1.1 convolution_add_fusion.1
  330.0 1.1 convolution_add_fusion
  331.1 11.6 %all-to-all-done.8 = bf16[32,8,1024]{2,1,0:T(8,128)(2,1)} async-done(((bf16[32,8,1024]{2,1,0:T(8,128)(2,1)}), bf16[32,8,1024]{2,1,0:T(8,128)(2,1)}, u32[]{:S(2)}, u32[]{:S(2)}) %all-to-all-start.8) | async-done | bytes 524320 | tf_op jit(solution)/shard_map/all_to_all | solution.py:13
  342.7 2.9 fusion.59
  (39 shorter events, 0.5 us)
Async XLA Ops:
  6.5 211.4 %copy-start = (bf16[1024,1024]{1,0:T(8,128)(2,1)S(1)}, bf16[1024,1024]{1,0:T(8,128)(2,1)}, u32[]{:S(2)}) copy-start(bf16[1024,1024]{1,0:T(8,128)(2,1)} %param.7) | copy-start | bytes 6291460
  8.4 24.9 %all-to-all-start = ((bf16[32,4,1024]{2,1,0:T(4,128)(2,1)}), bf16[32,4,1024]{2,1,0:T(4,128)(2,1)S(1)}, u32[]{:S(2)}, u32[]{:S(2)}) async-start(bf16[32,4,1024]{2,1,0:T(4,128)(2,1)} %reshape_squeeze.15), calls=%async_computation | async-start | bytes 524288 | tf_op jit(solution)/shard_map/all_to_all | solution.py:13
  21.0 93.7 %all-gather.6.cloned.1.call-start = ((), (), s32[]{:S(2)}) async-start(), calls=%async_computation.9 | async-start | bytes 4734976 | tf_op jit(solution)/shard_map/all_gather | solution.py:31
  34.3 195.5 %all-gather.8.cloned.1.call-start = ((), (), s32[]{:S(2)}) async-start(), calls=%async_computation.10 | async-start | bytes 2228224 | tf_op jit(solution)/shard_map/all_gather | solution.py:37
  34.3 80.2 %copy-start.12 = (s32[1,32]{1,0:T(1,128)S(1)}, s32[1,32]{1,0:T(1,128)}, u32[]{:S(2)}) copy-start(s32[1,32]{1,0:T(1,128)} %param.9) | copy-start | bytes 388
  110.6 1.3 copy-start.8
  112.6 140.6 %all-gather.10.cloned.1.call-start = ((), (), s32[]{:S(2)}) async-start(), calls=%async_computation.11 | async-start | bytes 8912896 | tf_op jit(solution)/shard_map/all_gather | solution.py:38
  123.8 43.9 %all-to-all-start.1 = ((bf16[32,24,1024]{2,1,0:T(8,128)(2,1)}), bf16[32,24,1024]{2,1,0:T(8,128)(2,1)}, u32[]{:S(2)}, u32[]{:S(2)}) async-start(bf16[32,24,1024]{2,1,0:T(8,128)(2,1)} %reshape.138), calls=%async_computation.1 | async-start | bytes 3145728 | tf_op jit(solution)/shard_map/all_to_all | solution.py:13
  171.6 1.7 copy-start.9
  173.3 5.7 %collective-permute-start = (bf16[8,48,1024]{2,1,0:T(8,128)(2,1)S(1)}, bf16[8,48,1024]{2,1,0:T(8,128)(2,1)}, u32[]{:S(2)}, u32[]{:S(2)}) collective-permute-start(bf16[8,48,1024]{2,1,0:T(8,128)(2,1)S(1)} %fusion.70), channel_id=1, source_target_pairs={{0,1},{1,0},{2,3},{3,2},{4,5},{5,4},{6,7},{7,6},{8,9},{9,8},{10,11... | collective-permute-start | bytes 2359304 | tf_op jit(solution)/shard_map/ppermute | solution.py:50
  181.0 36.9 %copy-start.10 = (bf16[6,8,1024]{2,1,0:T(8,128)(2,1)S(1)}, bf16[6,8,1024]{2,1,0:T(8,128)(2,1)}, u32[]{:S(2)}) copy-start(bf16[6,8,1024]{2,1,0:T(8,128)(2,1)} %param.8) | copy-start | bytes 294916
  219.2 24.3 %all-to-all-start.3 = ((bf16[32,8,1024]{2,1,0:T(8,128)(2,1)}), bf16[32,8,1024]{2,1,0:T(8,128)(2,1)S(1)}, u32[]{:S(2)}, u32[]{:S(2)}) async-start(bf16[32,8,1024]{2,1,0:T(8,128)(2,1)} %broadcast_in_dim.20), calls=%async_computation.3 | async-start | bytes 1048576 | tf_op jit(solution)/shard_map/all_to_all | solution.py:13
  246.6 21.7 %all-to-all-start.5 = ((bf16[32,8,1024]{2,1,0:T(8,128)(2,1)}), bf16[32,8,1024]{2,1,0:T(8,128)(2,1)S(1)}, u32[]{:S(2)}, u32[]{:S(2)}) async-start(bf16[32,8,1024]{2,1,0:T(8,128)(2,1)} %broadcast_in_dim.21), calls=%async_computation.5 | async-start | bytes 1048576 | tf_op jit(solution)/shard_map/all_to_all | solution.py:13
  259.0 1.4 copy-start.1
  271.4 21.7 %all-to-all-start.6 = ((bf16[32,8,1024]{2,1,0:T(8,128)(2,1)}), bf16[32,8,1024]{2,1,0:T(8,128)(2,1)}, u32[]{:S(2)}, u32[]{:S(2)}) async-start(bf16[32,8,1024]{2,1,0:T(8,128)(2,1)} %broadcast_in_dim.22), calls=%async_computation.6 | async-start | bytes 1048576 | tf_op jit(solution)/shard_map/all_to_all | solution.py:13
  278.2 2.2 copy-start.2
  296.3 21.7 %all-to-all-start.7 = ((bf16[32,8,1024]{2,1,0:T(8,128)(2,1)}), bf16[32,8,1024]{2,1,0:T(8,128)(2,1)}, u32[]{:S(2)}, u32[]{:S(2)}) async-start(bf16[32,8,1024]{2,1,0:T(8,128)(2,1)} %broadcast_in_dim.23), calls=%async_computation.7 | async-start | bytes 1048576 | tf_op jit(solution)/shard_map/all_to_all | solution.py:13
  305.1 2.2 copy-start.5
  305.1 2.8 copy-start.3
  320.2 8.4 %copy-start.11 = (bf16[6,8,1024]{2,1,0:T(8,128)(2,1)}, bf16[6,8,1024]{2,1,0:T(8,128)(2,1)S(1)}, u32[]{:S(2)}) copy-start(bf16[6,8,1024]{2,1,0:T(8,128)(2,1)S(1)} %get-tuple-element.30) | copy-start | bytes 294916
  321.1 21.6 %all-to-all-start.8 = ((bf16[32,8,1024]{2,1,0:T(8,128)(2,1)}), bf16[32,8,1024]{2,1,0:T(8,128)(2,1)}, u32[]{:S(2)}, u32[]{:S(2)}) async-start(bf16[32,8,1024]{2,1,0:T(8,128)(2,1)} %broadcast_in_dim.24), calls=%async_computation.8 | async-start | bytes 1048576 | tf_op jit(solution)/shard_map/all_to_all | solution.py:13
  326.0 2.2 copy-start.7
  326.0 2.8 copy-start.6
  328.3 1.7 copy-start.4
Sparse Core Ops, SparseCore 0:
  34.4 78.5 all-gather.5
  115.1 36.0 all-gather.7
  153.3 74.1 all-gather.9

commit v3 on v2

v3 whole, which is shorter than its diff:
```python
import jax
import jax.numpy as jnp
from jax import lax
from jax.sharding import Mesh, PartitionSpec as P

STEPS = 6
PATCH = ("x", "z")
LAG = ("y", "core")
F32, BF16 = jnp.float32, jnp.bfloat16


def swap(value, axes):
    return lax.all_to_all(value, axes, split_axis=0, concat_axis=0, tiled=True)


def dot(a, b):
    return jnp.dot(a, b, preferred_element_type=F32)


def on_device(history, coupling, inverse, cotangent, targets):
    history, tile, target_row = history[0], coupling[0], targets[0]
    patches, lags = lax.axis_size(PATCH), lax.axis_size(LAG)
    rows, width = history.shape
    piece, own, back = rows // patches, rows // lags, STEPS - 1
    core, lag = lax.axis_index("core"), lax.axis_index(LAG)
    chips = lags // 2

    spread = swap(history.reshape(patches, piece, width), PATCH)
    mine = target_row[lax.axis_index(PATCH)].astype(BF16)
    note = jnp.stack([jnp.full((piece, width), mine, BF16), jnp.zeros((piece, width), BF16)])
    known = lax.all_gather(jnp.concatenate([spread, note]), LAG, axis=0, tiled=True)
    blocks = patches + 2
    listed = known[patches::blocks, 0, 0].astype(jnp.int32)

    third = 352
    moved1 = lax.ppermute(tile[third : 2 * third], LAG, [(i, i + back) for i in range(back)])
    moved2 = lax.ppermute(tile[width - third :], LAG, [(i, i + 2 * back) for i in range(back)])
    first = swap(spread.at[target_row].get(mode="promise_in_bounds"), PATCH)
    moved1, moved2, _ = lax.optimization_barrier((moved1, moved2, first))
    share = jnp.where(lag < back, tile[:third], jnp.where(lag < 2 * back, moved1, moved2))
    shares = lax.all_gather(share, LAG, axis=0)

    def tile_of(l):
        last = shares[l - 1 + 2 * back][3 * third - width :]
        return jnp.concatenate([shares[l - 1], shares[l - 1 + back], last])

    first = dot(first.reshape(rows, width), tile).astype(BF16)
    total = jnp.sum(swap(first.reshape(lags, own, width), LAG).astype(F32), axis=0)

    def solve(k, total):
        residual = (cotangent[k].astype(F32) - total).astype(BF16)
        return dot(residual, inverse).astype(BF16)

    results = [solve(0, total)]

    earlier = lag - jnp.arange(1, STEPS)
    index = jnp.where(earlier >= 0, earlier * blocks + target_row[:, None], patches + 1)
    chosen = known.at[index].get(mode="promise_in_bounds")
    held = own // piece
    ahead = jnp.broadcast_to(results[0].reshape(1, held, piece, width), (patches, held, piece, width))
    routed = swap(jnp.concatenate([ahead, chosen], axis=1), PATCH)
    states = [routed[:, :held].reshape(patches, own, width)]
    terms = dot(routed[:, held:].reshape(-1, width), tile).reshape(chips, 2, back * own, width)
    kept = lax.dynamic_index_in_dim(terms, core, 1, keepdims=False)
    sent = lax.dynamic_index_in_dim(terms, 1 - core, 1, keepdims=False).astype(BF16)
    got = lax.ppermute(sent, "core", [(0, 1), (1, 0)])
    both = (kept + got.astype(F32)).astype(BF16)
    base = jnp.sum(swap(both, "y").astype(F32), axis=0)
    base = base.reshape(held, back, piece, width).transpose(1, 0, 2, 3).reshape(back, own, width)

    tiles = [tile_of(l) for l in range(1, STEPS)]
    for k in range(1, STEPS):
        total = base[k - 1]
        for l in range(k, 0, -1):
            state = lax.dynamic_index_in_dim(states[k - l], listed[l - 1], 0, keepdims=False)
            total = total + dot(state, tiles[l - 1])
        results.append(solve(k, total))
        if k + 1 < STEPS:
            copies = jnp.broadcast_to(results[k][None], (patches, own, width))
            states.append(swap(copies, PATCH))
    return jnp.stack(results)


def solution(mesh):
    fine = Mesh(mesh.devices.reshape(4, 8, 8, 2), PATCH + LAG)
    placed = (P(LAG, None, PATCH), P(LAG, PATCH, None), P(PATCH, None), P(None, LAG, PATCH), P(LAG, None))

    return jax.shard_map(on_device, mesh=fine, in_specs=placed, out_specs=P(None, LAG, PATCH), check_vma=False)
```

time: 354 us -> 344 us (0.972)
  blocking collectives: 113 us -> 0 us
  waiting for transfers between devices: 106 us -> 166 us
  starting transfers between devices: 47.9 us -> 65.1 us
  matrix products: 27.4 us -> 37.6 us
  local copies, waits for them, and re-layouts: 30.5 us -> 39.3 us
  other arithmetic: 5.05 us -> 10.3 us
    all_to_all x2 -> x0, blocking collectives: 113 us -> none  [swap(): return lax.all_to_all(value, axes, split_axis=0, concat_axis=0, tiled=True)]
    ppermute x0 -> x2, waiting for transfers between devices: none -> 44.9 us  [the longest x1 44.9 us: on_device(): lax.ppermute(tile[width - third:], LAG, [(i, i + 2 * back) for i in range...]
    all_to_all x7 -> x9, waiting for transfers between devices: 103 us -> 119 us  [swap(): return lax.all_to_all(value, axes, split_axis=0, concat_axis=0, tiled=True)]
    dot_general x17 -> x18, matrix products: 27.4 us -> 37.6 us  [dot(): return jnp.dot(a, b, preferred_element_type=F32)]
    all_to_all x7 -> x9, starting transfers between devices: 44.3 us -> 54 us  [swap(): return lax.all_to_all(value, axes, split_axis=0, concat_axis=0, tiled=True)]
    ppermute x0 -> x2, starting transfers between devices: none -> 9.15 us  [the longest x1 6.98 us: on_device(): lax.ppermute(tile[width - third:], LAG, [(i, i + 2 * back) for i in range...]
    slice x4 -> x6, local copies, waits for them, and re-layouts: 8.4 us -> 15.5 us  [the longest x1 5.64 us: tile_of(): return jnp.concatenate([shares[l - 1], shares[l - 1 + back], last])]
    squeeze x6 -> x5, local copies, waits for them, and re-layouts: 0.09 us -> 6.15 us  [on_device(): total = base[k - 1]]
  transfers between devices with their start and end apart: 11 -> 14, of which waited for: 8 -> 10; matrix products, arithmetic and copies ran while one was open for 12% -> 17% of each run, Pallas kernels for 0% -> 0%
where the time goes in v3:
time: 344 us; the launch traced here: 341 us
  waiting for transfers between devices  166 us (48%)
  starting transfers between devices  65.1 us (19%)
  local copies, waits for them, and re-layouts  39.3 us (11%)
  matrix products  37.6 us (11%)
  between operations  23.1 us (7%)
  other arithmetic  10.3 us (3%)
    all_to_all x9, waiting for transfers between devices, swap(): return lax.all_to_all(value, axes, split_axis=0, concat_axis=0, tiled=True)  119 us
    all_to_all x9, starting transfers between devices, swap(): return lax.all_to_all(value, axes, split_axis=0, concat_axis=0, tiled=True)  54 us
    ppermute x1, waiting for transfers between devices, on_device(): lax.ppermute(tile[width - third:], LAG, [(i, i + 2 * back) for i in range...  44.9 us
    dot_general x18, matrix products, dot(): return jnp.dot(a, b, preferred_element_type=F32)  37.6 us
    ppermute x1, starting transfers between devices, on_device(): lax.ppermute(tile[width - third:], LAG, [(i, i + 2 * back) for i in range...  6.98 us
  transfers between devices with their start and end apart: 14, of which 10 were waited for; matrix products, arithmetic and copies ran while one was open for 17% of the time, Pallas kernels for 0%

profile of v3, /device:TPU:64, one launch (start us, length us, event | category | flops | bytes accessed | tf_op | source)
XLA Modules:
  0.0 341.4 jit_solution(7315044827145891743)
XLA Ops:
  6.5 1.9 reshape_squeeze.3
  8.4 12.7 %all-to-all-start = ((bf16[32,4,1024]{2,1,0:T(4,128)(2,1)}), bf16[32,4,1024]{2,1,0:T(4,128)(2,1)S(1)}, u32[]{:S(2)}, u32[]{:S(2)}) async-start(bf16[32,4,1024]{2,1,0:T(4,128)(2,1)} %reshape_squeeze.3), calls=%async_computation | async-start | bytes 524288 | tf_op jit(solution)/shard_map/all_to_all | solution.py:13
  21.2 1.2 fusion.121
  23.3 10.2 %all-to-all-done = bf16[32,4,1024]{2,1,0:T(4,128)(2,1)S(1)} async-done(((bf16[32,4,1024]{2,1,0:T(4,128)(2,1)}), bf16[32,4,1024]{2,1,0:T(4,128)(2,1)S(1)}, u32[]{:S(2)}, u32[]{:S(2)}) %all-to-all-start) | async-done | bytes 262176 | tf_op jit(solution)/shard_map/all_to_all | solution.py:13
  33.4 0.9 maximum_maximum_fusion
  34.4 2.6 slice_bitcast_fusion
  37.0 7.0 %collective-permute-start.2 = (bf16[352,1024]{1,0:T(8,128)(2,1)}, bf16[352,1024]{1,0:T(8,128)(2,1)S(1)}, u32[]{:S(2)}, u32[]{:S(2)}) collective-permute-start(bf16[352,1024]{1,0:T(8,128)(2,1)} %get-tuple-element.24), channel_id=1, source_target_pairs={{0,10},{1,11},{2,12},{3,13},{4,14},{16,26},{17,27},{18,28},{19,29}... | collective-permute-start | bytes 2162696 | tf_op jit(solution)/shard_map/ppermute | solution.py:37
  44.0 2.2 collective-permute-start.1
  46.1 1.4 gather_fusion
  47.6 4.6 %all-to-all-start.1 = ((bf16[32,4,1024]{2,1,0:T(4,128)(2,1)}), bf16[32,4,1024]{2,1,0:T(4,128)(2,1)S(1)}, u32[]{:S(2)}, u32[]{:S(2)}) async-start(bf16[32,4,1024]{2,1,0:T(4,128)(2,1)} %gather_fusion), calls=%async_computation.1 | async-start | bytes 524288 | tf_op jit(solution)/shard_map/all_to_all | solution.py:13
  52.2 44.9 %collective-permute-done.2 = bf16[352,1024]{1,0:T(8,128)(2,1)S(1)} collective-permute-done((bf16[352,1024]{1,0:T(8,128)(2,1)}, bf16[352,1024]{1,0:T(8,128)(2,1)S(1)}, u32[]{:S(2)}, u32[]{:S(2)}) %collective-permute-start.2) | collective-permute-done | bytes 720928 | tf_op jit(solution)/shard_map/ppermute | solution.py:37
  97.1 2.3 bitcast_select_fusion
  99.5 2.8 fusion.14
  102.3 6.5 %all-to-all-start.2 = ((bf16[16,8,1024]{2,1,0:T(8,128)(2,1)}), bf16[16,8,1024]{2,1,0:T(8,128)(2,1)S(1)}, u32[]{:S(2)}, u32[]{:S(2)}) async-start(bf16[16,8,1024]{2,1,0:T(8,128)(2,1)} %fusion.14), calls=%async_computation.2 | async-start | bytes 524288 | tf_op jit(solution)/shard_map/all_to_all | solution.py:13
  109.1 10.9 %all-to-all-done.2 = bf16[16,8,1024]{2,1,0:T(8,128)(2,1)S(1)} async-done(((bf16[16,8,1024]{2,1,0:T(8,128)(2,1)}), bf16[16,8,1024]{2,1,0:T(8,128)(2,1)S(1)}, u32[]{:S(2)}, u32[]{:S(2)}) %all-to-all-start.2) | async-done | bytes 262176 | tf_op jit(solution)/shard_map/all_to_all | solution.py:13
  120.1 1.7 bitcast_dynamic-update-slice_fusion.4
  121.8 4.0 %gather_fusion.1 = bf16[160,4,1024]{2,1,0:T(4,128)(2,1)S(1)} fusion(bf16[544,4,1024]{2,1,0:T(4,128)(2,1)} %all-gather.4.cloned.1.call-done, s32[1024]{0:T(1024)S(1)} %pad_clamp_fusion), kind=kCustom, calls=%fused_computation.1 | custom fusion | bytes 2622080 | tf_op jit(solution)/shard_map/gather | solution.py:58
  126.1 2.4 pad_maximum_fusion.4
  128.5 4.9 %all-to-all-start.3 = ((bf16[32,7,4,1024]{3,2,1,0:T(4,128)(2,1)}), bf16[32,7,4,1024]{3,2,1,0:T(4,128)(2,1)}, u32[]{:S(2)}, u32[]{:S(2)}) async-start(bf16[32,7,4,1024]{3,2,1,0:T(4,128)(2,1)} %pad_maximum_fusion.4), calls=%async_computation.3 | async-start | bytes 3670016 | tf_op jit(solution)/shard_map/all_to_all | solution.py:13
  133.4 45.3 %all-to-all-done.3 = bf16[32,7,4,1024]{3,2,1,0:T(4,128)(2,1)} async-done(((bf16[32,7,4,1024]{3,2,1,0:T(4,128)(2,1)}), bf16[32,7,4,1024]{3,2,1,0:T(4,128)(2,1)}, u32[]{:S(2)}, u32[]{:S(2)}) %all-to-all-start.3) | async-done | bytes 1835040 | tf_op jit(solution)/shard_map/all_to_all | solution.py:13
  178.7 1.8 slice.224
  180.5 1.2 dot_general.73
  181.7 3.5 %fusion.6 = f32[8,2,40,1024]{3,2,1,0:T(8,128)S(1)} fusion(bf16[8,2,40,1024]{3,2,1,0:T(8,128)(2,1)} %dot_general.73, bf16[1,1024,1024]{2,1,0:T(8,128)(2,1)} %param.6), kind=kOutput, calls=%fused_computation.12 | convolution fusion | flops 1342177280 | bytes 6029312 | tf_op jit(solution)/shard_map/dot_general | solution.py:17
  185.2 1.5 copy-done.1
  186.8 1.9 collective-permute-start
  188.8 2.1 collective-permute-done
  190.8 2.4 fusion.10
  193.2 3.5 %all-to-all-start.4 = ((bf16[8,40,1024]{2,1,0:T(8,128)(2,1)}), bf16[8,40,1024]{2,1,0:T(8,128)(2,1)S(1)}, u32[]{:S(2)}, u32[]{:S(2)}) async-start(bf16[8,40,1024]{2,1,0:T(8,128)(2,1)} %fusion.10), calls=%async_computation.4 | async-start | bytes 1310720 | tf_op jit(solution)/shard_map/all_to_all | solution.py:13
  200.2 1.3 slice.226
  201.4 0.9 reshape.180
  202.3 15.2 %all-to-all-done.4 = bf16[8,40,1024]{2,1,0:T(8,128)(2,1)S(1)} async-done(((bf16[8,40,1024]{2,1,0:T(8,128)(2,1)}), bf16[8,40,1024]{2,1,0:T(8,128)(2,1)S(1)}, u32[]{:S(2)}, u32[]{:S(2)}) %all-to-all-start.4) | async-done | bytes 655392 | tf_op jit(solution)/shard_map/all_to_all | solution.py:13
  219.0 3.6 %slice_bitcast_fusion.2 = (bf16[320,1024]{1,0:T(8,128)(2,1)}, bf16[320,1024]{1,0:T(8,128)(2,1)}, bf16[320,1024]{1,0:T(8,128)(2,1)}, bf16[320,1024]{1,0:T(8,128)(2,1)}, bf16[320,1024]{1,0:T(8,128)(2,1)}) fusion(bf16[16,352,1024]{2,1,0:T(8,128)(2,1)} %bitcast.192), kind=kLoop, calls=%fused_computation.60 | loop fusion | bytes 6553600 | tf_op jit(solution)/shard_map/slice | solution.py:44
  222.6 5.6 %fusion.118 = (bf16[352,1024]{1,0:T(8,128)(2,1)}, bf16[352,1024]{1,0:T(8,128)(2,1)}, bf16[352,1024]{1,0:T(8,128)(2,1)}, bf16[352,1024]{1,0:T(8,128)(2,1)}, bf16[...) fusion(bf16[5632,1024]{1,0:T(8,128)(2,1)} %all-gather.6.cloned., ...), kind=kLoop, calls=%fused_computation.149 | loop fusion | bytes 14417920 | tf_op jit(solution)/shard_map/slice | solution.py:45
  228.2 2.4 bitcast_dynamic-update-slice_fusion.3
  230.6 0.9 broadcast_in_dim.24
  231.5 7.0 %all-to-all-start.5 = ((bf16[32,8,1024]{2,1,0:T(8,128)(2,1)}), bf16[32,8,1024]{2,1,0:T(8,128)(2,1)}, u32[]{:S(2)}, u32[]{:S(2)}) async-start(bf16[32,8,1024]{2,1,0:T(8,128)(2,1)} %broadcast_in_dim.24), calls=%async_computation.5 | async-start | bytes 1048576 | tf_op jit(solution)/shard_map/all_to_all | solution.py:13
  240.4 1.4 squeeze.148
  241.8 2.5 convolution_add_fusion.12
  244.3 12.1 %all-to-all-done.5 = bf16[32,8,1024]{2,1,0:T(8,128)(2,1)} async-done(((bf16[32,8,1024]{2,1,0:T(8,128)(2,1)}), bf16[32,8,1024]{2,1,0:T(8,128)(2,1)}, u32[]{:S(2)}, u32[]{:S(2)}) %all-to-all-start.5) | async-done | bytes 524320 | tf_op jit(solution)/shard_map/all_to_all | solution.py:13
  256.4 2.4 bitcast_dynamic-update-slice_fusion.2
  258.8 0.9 broadcast_in_dim.25
  259.6 4.9 %all-to-all-start.6 = ((bf16[32,8,1024]{2,1,0:T(8,128)(2,1)}), bf16[32,8,1024]{2,1,0:T(8,128)(2,1)}, u32[]{:S(2)}, u32[]{:S(2)}) async-start(bf16[32,8,1024]{2,1,0:T(8,128)(2,1)} %broadcast_in_dim.25), calls=%async_computation.6 | async-start | bytes 1048576 | tf_op jit(solution)/shard_map/all_to_all | solution.py:13
  266.4 1.4 squeeze.154
  267.8 2.1 convolution_add_fusion.10
  270.0 1.7 convolution_add_fusion.9
  271.7 10.2 %all-to-all-done.6 = bf16[32,8,1024]{2,1,0:T(8,128)(2,1)} async-done(((bf16[32,8,1024]{2,1,0:T(8,128)(2,1)}), bf16[32,8,1024]{2,1,0:T(8,128)(2,1)}, u32[]{:S(2)}, u32[]{:S(2)}) %all-to-all-start.6) | async-done | bytes 524320 | tf_op jit(solution)/shard_map/all_to_all | solution.py:13
  281.9 2.4 bitcast_dynamic-update-slice_fusion.1
  284.3 0.9 broadcast_in_dim.48
  285.2 4.9 %all-to-all-start.7 = ((bf16[32,8,1024]{2,1,0:T(8,128)(2,1)}), bf16[32,8,1024]{2,1,0:T(8,128)(2,1)}, u32[]{:S(2)}, u32[]{:S(2)}) async-start(bf16[32,8,1024]{2,1,0:T(8,128)(2,1)} %broadcast_in_dim.48), calls=%async_computation.7 | async-start | bytes 1048576 | tf_op jit(solution)/shard_map/all_to_all | solution.py:13
  292.0 1.4 squeeze.161
  293.4 2.1 convolution_add_fusion.7
  295.5 1.2 convolution_add_fusion.6
  297.1 1.7 convolution_add_fusion.5
  298.8 8.3 %all-to-all-done.7 = bf16[32,8,1024]{2,1,0:T(8,128)(2,1)} async-done(((bf16[32,8,1024]{2,1,0:T(8,128)(2,1)}), bf16[32,8,1024]{2,1,0:T(8,128)(2,1)}, u32[]{:S(2)}, u32[]{:S(2)}) %all-to-all-start.7) | async-done | bytes 524320 | tf_op jit(solution)/shard_map/all_to_all | solution.py:13
  307.1 2.4 bitcast_dynamic-update-slice_fusion
  309.5 0.9 broadcast_in_dim.49
  310.4 4.9 %all-to-all-start.8 = ((bf16[32,8,1024]{2,1,0:T(8,128)(2,1)}), bf16[32,8,1024]{2,1,0:T(8,128)(2,1)}, u32[]{:S(2)}, u32[]{:S(2)}) async-start(bf16[32,8,1024]{2,1,0:T(8,128)(2,1)} %broadcast_in_dim.49), calls=%async_computation.8 | async-start | bytes 1048576 | tf_op jit(solution)/shard_map/all_to_all | solution.py:13
  316.9 1.4 squeeze.169
  318.3 2.1 fusion.22
  320.5 1.2 convolution_add_fusion.3
  322.0 1.2 convolution_add_fusion.2
  323.5 1.7 convolution_add_fusion.1
  325.3 6.9 %all-to-all-done.8 = bf16[32,8,1024]{2,1,0:T(8,128)(2,1)} async-done(((bf16[32,8,1024]{2,1,0:T(8,128)(2,1)}), bf16[32,8,1024]{2,1,0:T(8,128)(2,1)}, u32[]{:S(2)}, u32[]{:S(2)}) %all-to-all-start.8) | async-done | bytes 524320 | tf_op jit(solution)/shard_map/all_to_all | solution.py:13
  332.1 2.4 fusion.31
  (69 shorter events, 5.5 us)
Async XLA Ops:
  6.5 113.5 %copy-start = (bf16[1024,1024]{1,0:T(8,128)(2,1)S(1)}, bf16[1024,1024]{1,0:T(8,128)(2,1)}, u32[]{:S(2)}) copy-start(bf16[1024,1024]{1,0:T(8,128)(2,1)} %param.7) | copy-start | bytes 6291460
  8.4 37.7 %copy-start.20 = (s32[1,32]{1,0:T(1,128)S(1)}, s32[1,32]{1,0:T(1,128)}, u32[]{:S(2)}) copy-start(s32[1,32]{1,0:T(1,128)} %param.9) | copy-start | bytes 388
  8.4 25.0 %all-to-all-start = ((bf16[32,4,1024]{2,1,0:T(4,128)(2,1)}), bf16[32,4,1024]{2,1,0:T(4,128)(2,1)S(1)}, u32[]{:S(2)}, u32[]{:S(2)}) async-start(bf16[32,4,1024]{2,1,0:T(4,128)(2,1)} %reshape_squeeze.3), calls=%async_computation | async-start | bytes 524288 | tf_op jit(solution)/shard_map/all_to_all | solution.py:13
  21.2 100.6 %all-gather.4.cloned.1.call-start = ((), (), s32[]{:S(2)}) async-start(), calls=%async_computation.9 | async-start | bytes 4734976 | tf_op jit(solution)/shard_map/all_gather | solution.py:31
  37.0 60.1 %collective-permute-start.2 = (bf16[352,1024]{1,0:T(8,128)(2,1)}, bf16[352,1024]{1,0:T(8,128)(2,1)S(1)}, u32[]{:S(2)}, u32[]{:S(2)}) collective-permute-start(bf16[352,1024]{1,0:T(8,128)(2,1)} %get-tuple-element.24), channel_id=1, source_target_pairs={{0,10},{1,11},{2,12},{3,13},{4,14},{16,26},{17,27},{18,28},{19,29}... | collective-permute-start | bytes 2162696 | tf_op jit(solution)/shard_map/ppermute | solution.py:37
  44.0 53.2 %collective-permute-start.1 = (bf16[352,1024]{1,0:T(8,128)(2,1)}, bf16[352,1024]{1,0:T(8,128)(2,1)}, u32[]{:S(2)}, u32[]{:S(2)}) collective-permute-start(bf16[352,1024]{1,0:T(8,128)(2,1)} %get-tuple-element.25), channel_id=1, source_target_pairs={{0,5},{1,6},{2,7},{3,8},{4,9},{16,21},{17,22},{18,23},{19,24},{20,... | collective-permute-start | bytes 2162696 | tf_op jit(solution)/shard_map/ppermute | solution.py:36
  47.6 49.5 %all-to-all-start.1 = ((bf16[32,4,1024]{2,1,0:T(4,128)(2,1)}), bf16[32,4,1024]{2,1,0:T(4,128)(2,1)S(1)}, u32[]{:S(2)}, u32[]{:S(2)}) async-start(bf16[32,4,1024]{2,1,0:T(4,128)(2,1)} %gather_fusion), calls=%async_computation.1 | async-start | bytes 524288 | tf_op jit(solution)/shard_map/all_to_all | solution.py:13
  52.2 166.8 %all-gather.6.cloned.1.call-start = ((), (), s32[]{:S(2)}) async-start(), calls=%async_computation.10 | async-start | bytes 12255232 | tf_op jit(solution)/shard_map/all_gather | solution.py:41
  102.3 17.7 %all-to-all-start.2 = ((bf16[16,8,1024]{2,1,0:T(8,128)(2,1)}), bf16[16,8,1024]{2,1,0:T(8,128)(2,1)S(1)}, u32[]{:S(2)}, u32[]{:S(2)}) async-start(bf16[16,8,1024]{2,1,0:T(8,128)(2,1)} %fusion.14), calls=%async_computation.2 | async-start | bytes 524288 | tf_op jit(solution)/shard_map/all_to_all | solution.py:13
  128.5 50.2 %all-to-all-start.3 = ((bf16[32,7,4,1024]{3,2,1,0:T(4,128)(2,1)}), bf16[32,7,4,1024]{3,2,1,0:T(4,128)(2,1)}, u32[]{:S(2)}, u32[]{:S(2)}) async-start(bf16[32,7,4,1024]{3,2,1,0:T(4,128)(2,1)} %pad_maximum_fusion.4), calls=%async_computation.3 | async-start | bytes 3670016 | tf_op jit(solution)/shard_map/all_to_all | solution.py:13
  185.2 1.5 copy-start.1
  186.8 4.0 %collective-permute-start = (bf16[8,40,1024]{2,1,0:T(8,128)(2,1)S(1)}, bf16[8,40,1024]{2,1,0:T(8,128)(2,1)S(1)}, u32[]{:S(2)}, u32[]{:S(2)}) collective-permute-start(bf16[8,40,1024]{2,1,0:T(8,128)(2,1)S(1)} %fusion.32), channel_id=1, source_target_pairs={{0,1},{1,0},{2,3},{3,2},{4,5},{5,4},{6,7},{7,6},{8,9},{9,8},{10,11... | collective-permute-start | bytes 1966088 | tf_op jit(solution)/shard_map/ppermute | solution.py:66
  193.2 24.3 %all-to-all-start.4 = ((bf16[8,40,1024]{2,1,0:T(8,128)(2,1)}), bf16[8,40,1024]{2,1,0:T(8,128)(2,1)S(1)}, u32[]{:S(2)}, u32[]{:S(2)}) async-start(bf16[8,40,1024]{2,1,0:T(8,128)(2,1)} %fusion.10), calls=%async_computation.4 | async-start | bytes 1310720 | tf_op jit(solution)/shard_map/all_to_all | solution.py:13
  231.5 24.9 %all-to-all-start.5 = ((bf16[32,8,1024]{2,1,0:T(8,128)(2,1)}), bf16[32,8,1024]{2,1,0:T(8,128)(2,1)}, u32[]{:S(2)}, u32[]{:S(2)}) async-start(bf16[32,8,1024]{2,1,0:T(8,128)(2,1)} %broadcast_in_dim.24), calls=%async_computation.5 | async-start | bytes 1048576 | tf_op jit(solution)/shard_map/all_to_all | solution.py:13
  259.6 22.3 %all-to-all-start.6 = ((bf16[32,8,1024]{2,1,0:T(8,128)(2,1)}), bf16[32,8,1024]{2,1,0:T(8,128)(2,1)}, u32[]{:S(2)}, u32[]{:S(2)}) async-start(bf16[32,8,1024]{2,1,0:T(8,128)(2,1)} %broadcast_in_dim.25), calls=%async_computation.6 | async-start | bytes 1048576 | tf_op jit(solution)/shard_map/all_to_all | solution.py:13
  267.8 2.1 copy-start.2
  267.8 2.1 copy-start.5
  267.8 2.2 copy-start.14
  285.2 21.9 %all-to-all-start.7 = ((bf16[32,8,1024]{2,1,0:T(8,128)(2,1)}), bf16[32,8,1024]{2,1,0:T(8,128)(2,1)}, u32[]{:S(2)}, u32[]{:S(2)}) async-start(bf16[32,8,1024]{2,1,0:T(8,128)(2,1)} %broadcast_in_dim.48), calls=%async_computation.7 | async-start | bytes 1048576 | tf_op jit(solution)/shard_map/all_to_all | solution.py:13
  293.3 2.1 copy-start.8
  293.4 2.1 copy-start.10
  293.4 2.2 copy-start.17
  295.5 1.3 copy-start.3
  295.5 1.3 copy-start.6
  295.5 1.5 copy-start.15
  310.4 21.8 %all-to-all-start.8 = ((bf16[32,8,1024]{2,1,0:T(8,128)(2,1)}), bf16[32,8,1024]{2,1,0:T(8,128)(2,1)}, u32[]{:S(2)}, u32[]{:S(2)}) async-start(bf16[32,8,1024]{2,1,0:T(8,128)(2,1)} %broadcast_in_dim.49), calls=%async_computation.8 | async-start | bytes 1048576 | tf_op jit(solution)/shard_map/all_to_all | solution.py:13
  318.3 2.1 copy-start.12
  318.3 2.1 copy-start.13
  318.3 2.2 copy-start.19
  320.5 1.3 copy-start.9
  320.5 1.3 copy-start.11
  320.5 1.5 copy-start.18
  322.0 1.3 copy-start.4
  322.0 1.3 copy-start.7
  322.0 1.5 copy-start.16
Sparse Core Ops, SparseCore 0:
  34.5 71.7 all-gather.3
  108.4 66.5 all-gather.5

commit v4 on v3

--- a/solution.py
+++ b/solution.py
@@ -36,16 +36,16 @@
     moved1 = lax.ppermute(tile[third : 2 * third], LAG, [(i, i + back) for i in range(back)])
     moved2 = lax.ppermute(tile[width - third :], LAG, [(i, i + 2 * back) for i in range(back)])
     first = swap(spread.at[target_row].get(mode="promise_in_bounds"), PATCH)
-    moved1, moved2, _ = lax.optimization_barrier((moved1, moved2, first))
+    first = dot(first.reshape(rows, width), tile).astype(BF16)
+    total = jnp.sum(swap(first.reshape(lags, own, width), LAG).astype(F32), axis=0)
+    moved1, moved2, _ = lax.optimization_barrier((moved1, moved2, total))
     share = jnp.where(lag < back, tile[:third], jnp.where(lag < 2 * back, moved1, moved2))
     shares = lax.all_gather(share, LAG, axis=0)
 
-    def tile_of(l):
-        last = shares[l - 1 + 2 * back][3 * third - width :]
-        return jnp.concatenate([shares[l - 1], shares[l - 1 + back], last])
-
-    first = dot(first.reshape(rows, width), tile).astype(BF16)
-    total = jnp.sum(swap(first.reshape(lags, own, width), LAG).astype(F32), axis=0)
+    def tile_of(l, after):
+        ready, _ = lax.optimization_barrier((shares, after))
+        last = ready[l - 1 + 2 * back][3 * third - width :]
+        return jnp.concatenate([ready[l - 1], ready[l - 1 + back], last])
 
     def solve(k, total):
         residual = (cotangent[k].astype(F32) - total).astype(BF16)
@@ -60,15 +60,19 @@
     ahead = jnp.broadcast_to(results[0].reshape(1, held, piece, width), (patches, held, piece, width))
     routed = swap(jnp.concatenate([ahead, chosen], axis=1), PATCH)
     states = [routed[:, :held].reshape(patches, own, width)]
-    terms = dot(routed[:, held:].reshape(-1, width), tile).reshape(chips, 2, back * own, width)
-    kept = lax.dynamic_index_in_dim(terms, core, 1, keepdims=False)
-    sent = lax.dynamic_index_in_dim(terms, 1 - core, 1, keepdims=False).astype(BF16)
-    got = lax.ppermute(sent, "core", [(0, 1), (1, 0)])
-    both = (kept + got.astype(F32)).astype(BF16)
-    base = jnp.sum(swap(both, "y").astype(F32), axis=0)
+    routed = routed.reshape(chips, 2, -1, STEPS + 1, piece, width)
+
+    def terms(which):
+        part = lax.dynamic_index_in_dim(routed, which, 1, keepdims=False)
+        return dot(part[:, :, held:].reshape(-1, width), tile).reshape(chips, back * own, width)
+
+    got = lax.ppermute(terms(1 - core).astype(BF16), "core", [(0, 1), (1, 0)])
+    both = (terms(core) + got.astype(F32)).astype(BF16)
+    parts = swap(both, "y")
+    base = jnp.sum(parts.astype(F32), axis=0)
     base = base.reshape(held, back, piece, width).transpose(1, 0, 2, 3).reshape(back, own, width)
 
-    tiles = [tile_of(l) for l in range(1, STEPS)]
+    tiles = [tile_of(1, both)]
     for k in range(1, STEPS):
         total = base[k - 1]
         for l in range(k, 0, -1):
@@ -76,6 +80,7 @@
             total = total + dot(state, tiles[l - 1])
         results.append(solve(k, total))
         if k + 1 < STEPS:
+            tiles.append(tile_of(k + 1, results[k]))
             copies = jnp.broadcast_to(results[k][None], (patches, own, width))
             states.append(swap(copies, PATCH))
     return jnp.stack(results)

time: 344 us -> 350 us (1.017)
  waiting for transfers between devices: 166 us -> 147 us
  starting transfers between devices: 65.1 us -> 78.6 us
  local copies, waits for them, and re-layouts: 39.3 us -> 52.1 us
    ppermute x1, waiting for transfers between devices: 44.9 us -> 0.01 us  [on_device(): lax.ppermute(tile[width - third:], LAG, [(i, i + 2 * back) for i in range...]
    all_to_all x9, waiting for transfers between devices: 119 us -> 147 us  [swap(): return lax.all_to_all(value, axes, split_axis=0, concat_axis=0, tiled=True)]
    all_to_all x9, starting transfers between devices: 54 us -> 68.1 us  [swap(): return lax.all_to_all(value, axes, split_axis=0, concat_axis=0, tiled=True)]
    squeeze x0 -> x6, local copies, waits for them, and re-layouts: none -> 11.2 us  [the longest x5 9.02 us: tile_of(): return jnp.concatenate([ready[l - 1], ready[l - 1 + back], last])]
    slice x3 -> x7, local copies, waits for them, and re-layouts: 11 us -> 8.77 us  [the longest x5 6.54 us: tile_of(): last = ready[l - 1 + 2 * back][3 * third - width:]]
    dot_general x18 -> x19, matrix products: 37.6 us -> 38.5 us  [dot(): return jnp.dot(a, b, preferred_element_type=F32)]
  transfers between devices with their start and end apart: 14 -> 14, of which waited for: 10 -> 8; matrix products, arithmetic and copies ran while one was open for 17% -> 20% of each run, Pallas kernels for 0% -> 0%
where the time goes in v4:
time: 350 us; the launch traced here: 348 us
  waiting for transfers between devices  147 us (42%)
  starting transfers between devices  78.6 us (22%)
  local copies, waits for them, and re-layouts  52.1 us (15%)
  matrix products  38.5 us (11%)
  between operations  23.4 us (7%)
  other arithmetic  8.38 us (2%)
    all_to_all x9, waiting for transfers between devices, swap(): return lax.all_to_all(value, axes, split_axis=0, concat_axis=0, tiled=True)  147 us
    all_to_all x9, starting transfers between devices, swap(): return lax.all_to_all(value, axes, split_axis=0, concat_axis=0, tiled=True)  68.1 us
    dot_general x19, matrix products, dot(): return jnp.dot(a, b, preferred_element_type=F32)  38.5 us
    squeeze x5, local copies, waits for them, and re-layouts, tile_of(): return jnp.concatenate([ready[l - 1], ready[l - 1 + back], last])  9.02 us
  transfers between devices with their start and end apart: 14, of which 8 were waited for; matrix products, arithmetic and copies ran while one was open for 20% of the time, Pallas kernels for 0%

profile of v4, /device:TPU:64, one launch (start us, length us, event | category | flops | bytes accessed | tf_op | source)
XLA Modules:
  0.0 347.7 jit_solution(7950523728410557443)
XLA Ops:
  6.5 1.9 reshape_squeeze.3
  8.4 12.6 %all-to-all-start = ((bf16[32,4,1024]{2,1,0:T(4,128)(2,1)}), bf16[32,4,1024]{2,1,0:T(4,128)(2,1)S(1)}, u32[]{:S(2)}, u32[]{:S(2)}) async-start(bf16[32,4,1024]{2,1,0:T(4,128)(2,1)} %reshape_squeeze.3), calls=%async_computation | async-start | bytes 524288 | tf_op jit(solution)/shard_map/all_to_all | solution.py:13
  21.2 1.2 fusion.123
  23.1 10.2 %all-to-all-done = bf16[32,4,1024]{2,1,0:T(4,128)(2,1)S(1)} async-done(((bf16[32,4,1024]{2,1,0:T(4,128)(2,1)}), bf16[32,4,1024]{2,1,0:T(4,128)(2,1)S(1)}, u32[]{:S(2)}, u32[]{:S(2)}) %all-to-all-start) | async-done | bytes 262176 | tf_op jit(solution)/shard_map/all_to_all | solution.py:13
  35.0 1.5 gather_fusion
  36.4 4.6 %all-to-all-start.1 = ((bf16[32,4,1024]{2,1,0:T(4,128)(2,1)}), bf16[32,4,1024]{2,1,0:T(4,128)(2,1)S(1)}, u32[]{:S(2)}, u32[]{:S(2)}) async-start(bf16[32,4,1024]{2,1,0:T(4,128)(2,1)} %gather_fusion), calls=%async_computation.1 | async-start | bytes 524288 | tf_op jit(solution)/shard_map/all_to_all | solution.py:13
  41.0 2.6 slice_bitcast_fusion.10
  43.6 2.6 collective-permute-start.1
  46.2 6.0 %collective-permute-start.2 = (bf16[352,1024]{1,0:T(8,128)(2,1)}, bf16[352,1024]{1,0:T(8,128)(2,1)}, u32[]{:S(2)}, u32[]{:S(2)}) collective-permute-start(bf16[352,1024]{1,0:T(8,128)(2,1)} %get-tuple-element.29), channel_id=1, source_target_pairs={{0,10},{1,11},{2,12},{3,13},{4,14},{16,26},{17,27},{18,28},{19,29}... | collective-permute-start | bytes 2162696 | tf_op jit(solution)/shard_map/ppermute | solution.py:37
  52.5 2.8 fusion.18
  55.3 7.3 %all-to-all-start.2 = ((bf16[16,8,1024]{2,1,0:T(8,128)(2,1)}), bf16[16,8,1024]{2,1,0:T(8,128)(2,1)S(1)}, u32[]{:S(2)}, u32[]{:S(2)}) async-start(bf16[16,8,1024]{2,1,0:T(8,128)(2,1)} %fusion.18), calls=%async_computation.2 | async-start | bytes 524288 | tf_op jit(solution)/shard_map/all_to_all | solution.py:13
  62.8 48.7 %all-to-all-done.2 = bf16[16,8,1024]{2,1,0:T(8,128)(2,1)S(1)} async-done(((bf16[16,8,1024]{2,1,0:T(8,128)(2,1)}), bf16[16,8,1024]{2,1,0:T(8,128)(2,1)S(1)}, u32[]{:S(2)}, u32[]{:S(2)}) %all-to-all-start.2) | async-done | bytes 262176 | tf_op jit(solution)/shard_map/all_to_all | solution.py:13
  111.5 2.1 bitcast_select_fusion
  113.9 1.7 bitcast_dynamic-update-slice_fusion.4
  115.6 4.0 %gather_fusion.1 = bf16[160,4,1024]{2,1,0:T(4,128)(2,1)S(1)} fusion(bf16[544,4,1024]{2,1,0:T(4,128)(2,1)} %all-gather.4.cloned.1.call-done, s32[1024]{0:T(1024)S(1)} %pad_clamp_fusion), kind=kCustom, calls=%fused_computation.1 | custom fusion | bytes 2622080 | tf_op jit(solution)/shard_map/gather | solution.py:58
  119.8 2.4 pad_maximum_fusion.4
  122.3 10.4 %all-to-all-start.3 = ((bf16[32,7,4,1024]{3,2,1,0:T(4,128)(2,1)}), bf16[32,7,4,1024]{3,2,1,0:T(4,128)(2,1)}, u32[]{:S(2)}, u32[]{:S(2)}) async-start(bf16[32,7,4,1024]{3,2,1,0:T(4,128)(2,1)} %pad_maximum_fusion.4), calls=%async_computation.3 | async-start | bytes 3670016 | tf_op jit(solution)/shard_map/all_to_all | solution.py:13
  132.7 44.1 %all-to-all-done.3 = bf16[32,7,4,1024]{3,2,1,0:T(4,128)(2,1)} async-done(((bf16[32,7,4,1024]{3,2,1,0:T(4,128)(2,1)}), bf16[32,7,4,1024]{3,2,1,0:T(4,128)(2,1)}, u32[]{:S(2)}, u32[]{:S(2)}) %all-to-all-start.3) | async-done | bytes 1835040 | tf_op jit(solution)/shard_map/all_to_all | solution.py:13
  176.7 2.2 dynamic-slice_bitcast_fusion
  179.0 1.1 slice.219
  180.1 2.2 dot_general.80
  182.3 3.6 %fusion.12 = bf16[8,40,1024]{2,1,0:T(8,128)(2,1)} fusion(bf16[8,40,1024]{2,1,0:T(8,128)(2,1)} %dot_general.80, bf16[1,1024,1024]{2,1,0:T(8,128)(2,1)} %param.6), kind=kOutput, calls=%fused_computation.19 | convolution fusion | flops 671416320 | bytes 3407872 | tf_op jit(solution)/shard_map/dot_general | solution.py:17
  185.9 1.9 collective-permute-start
  188.9 1.5 dot_general.78
  190.4 3.4 add_convert_fusion
  193.9 6.6 %all-to-all-start.4 = ((bf16[8,40,1024]{2,1,0:T(8,128)(2,1)}), bf16[8,40,1024]{2,1,0:T(8,128)(2,1)S(1)}, u32[]{:S(2)}, u32[]{:S(2)}) async-start(bf16[8,40,1024]{2,1,0:T(8,128)(2,1)} %add_convert_fusion), calls=%async_computation.4 | async-start | bytes 1310720 | tf_op jit(solution)/shard_map/all_to_all | solution.py:13
  203.7 1.3 slice.221
  206.0 15.5 %all-to-all-done.4 = bf16[8,40,1024]{2,1,0:T(8,128)(2,1)S(1)} async-done(((bf16[8,40,1024]{2,1,0:T(8,128)(2,1)}), bf16[8,40,1024]{2,1,0:T(8,128)(2,1)S(1)}, u32[]{:S(2)}, u32[]{:S(2)}) %all-to-all-start.4) | async-done | bytes 655392 | tf_op jit(solution)/shard_map/all_to_all | solution.py:13
  222.9 2.0 slice_bitcast_fusion.16
  224.9 1.4 slice_bitcast_fusion.9
  226.3 2.4 bitcast_dynamic-update-slice_fusion.3
  229.6 6.9 %all-to-all-start.5 = ((bf16[32,8,1024]{2,1,0:T(8,128)(2,1)}), bf16[32,8,1024]{2,1,0:T(8,128)(2,1)}, u32[]{:S(2)}, u32[]{:S(2)}) async-start(bf16[32,8,1024]{2,1,0:T(8,128)(2,1)} %broadcast_in_dim.24), calls=%async_computation.5 | async-start | bytes 1048576 | tf_op jit(solution)/shard_map/all_to_all | solution.py:13
  244.1 1.4 squeeze.151
  245.4 1.4 squeeze.157
  246.8 1.4 squeeze.164
  248.2 1.4 squeeze.172
  249.6 1.1 slice_bitcast_fusion.15
  250.7 1.7 slice_bitcast_fusion.7
  253.5 1.7 convolution_add_fusion.12
  255.2 2.4 bitcast_dynamic-update-slice_fusion.2
  258.5 9.8 %all-to-all-start.6 = ((bf16[32,8,1024]{2,1,0:T(8,128)(2,1)}), bf16[32,8,1024]{2,1,0:T(8,128)(2,1)}, u32[]{:S(2)}, u32[]{:S(2)}) async-start(bf16[32,8,1024]{2,1,0:T(8,128)(2,1)} %broadcast_in_dim.25), calls=%async_computation.6 | async-start | bytes 1048576 | tf_op jit(solution)/shard_map/all_to_all | solution.py:13
  268.3 1.1 slice_bitcast_fusion.14
  269.5 1.7 slice_bitcast_fusion.5
  271.2 1.3 convolution_add_fusion.10
  273.2 1.7 convolution_add_fusion.9
  274.9 10.7 %all-to-all-done.6 = bf16[32,8,1024]{2,1,0:T(8,128)(2,1)} async-done(((bf16[32,8,1024]{2,1,0:T(8,128)(2,1)}), bf16[32,8,1024]{2,1,0:T(8,128)(2,1)}, u32[]{:S(2)}, u32[]{:S(2)}) %all-to-all-start.6) | async-done | bytes 524320 | tf_op jit(solution)/shard_map/all_to_all | solution.py:13
  285.6 2.4 bitcast_dynamic-update-slice_fusion.1
  288.9 4.9 %all-to-all-start.7 = ((bf16[32,8,1024]{2,1,0:T(8,128)(2,1)}), bf16[32,8,1024]{2,1,0:T(8,128)(2,1)}, u32[]{:S(2)}, u32[]{:S(2)}) async-start(bf16[32,8,1024]{2,1,0:T(8,128)(2,1)} %broadcast_in_dim.48), calls=%async_computation.7 | async-start | bytes 1048576 | tf_op jit(solution)/shard_map/all_to_all | solution.py:13
  293.8 1.1 slice_bitcast_fusion.13
  294.9 1.7 slice_bitcast_fusion.3
  297.8 1.3 convolution_add_fusion.7
  299.3 1.2 convolution_add_fusion.6
  300.8 1.7 convolution_add_fusion.5
  302.5 8.4 %all-to-all-done.7 = bf16[32,8,1024]{2,1,0:T(8,128)(2,1)} async-done(((bf16[32,8,1024]{2,1,0:T(8,128)(2,1)}), bf16[32,8,1024]{2,1,0:T(8,128)(2,1)}, u32[]{:S(2)}, u32[]{:S(2)}) %all-to-all-start.7) | async-done | bytes 524320 | tf_op jit(solution)/shard_map/all_to_all | solution.py:13
  310.9 2.4 bitcast_dynamic-update-slice_fusion
  313.3 2.6 slice_bitcast_fusion.1
  316.7 4.9 %all-to-all-start.8 = ((bf16[32,8,1024]{2,1,0:T(8,128)(2,1)}), bf16[32,8,1024]{2,1,0:T(8,128)(2,1)}, u32[]{:S(2)}, u32[]{:S(2)}) async-start(bf16[32,8,1024]{2,1,0:T(8,128)(2,1)} %broadcast_in_dim.49), calls=%async_computation.8 | async-start | bytes 1048576 | tf_op jit(solution)/shard_map/all_to_all | solution.py:13
  321.7 1.1 slice_bitcast_fusion.12
  322.8 1.9 fusion.26
  324.8 1.2 convolution_add_fusion.3
  326.3 1.2 convolution_add_fusion.2
  327.9 1.7 convolution_add_fusion.1
  329.6 9.0 %all-to-all-done.8 = bf16[32,8,1024]{2,1,0:T(8,128)(2,1)} async-done(((bf16[32,8,1024]{2,1,0:T(8,128)(2,1)}), bf16[32,8,1024]{2,1,0:T(8,128)(2,1)}, u32[]{:S(2)}, u32[]{:S(2)}) %all-to-all-start.8) | async-done | bytes 524320 | tf_op jit(solution)/shard_map/all_to_all | solution.py:13
  338.5 2.4 fusion.35
  (101 shorter events, 15.8 us)
Async XLA Ops:
  6.5 107.3 %copy-start = (bf16[1024,1024]{1,0:T(8,128)(2,1)S(1)}, bf16[1024,1024]{1,0:T(8,128)(2,1)}, u32[]{:S(2)}) copy-start(bf16[1024,1024]{1,0:T(8,128)(2,1)} %param.7) | copy-start | bytes 6291460
  8.4 24.9 %all-to-all-start = ((bf16[32,4,1024]{2,1,0:T(4,128)(2,1)}), bf16[32,4,1024]{2,1,0:T(4,128)(2,1)S(1)}, u32[]{:S(2)}, u32[]{:S(2)}) async-start(bf16[32,4,1024]{2,1,0:T(4,128)(2,1)} %reshape_squeeze.3), calls=%async_computation | async-start | bytes 524288 | tf_op jit(solution)/shard_map/all_to_all | solution.py:13
  21.0 94.6 %all-gather.4.cloned.1.call-start = ((), (), s32[]{:S(2)}) async-start(), calls=%async_computation.9 | async-start | bytes 4734976 | tf_op jit(solution)/shard_map/all_gather | solution.py:31
  36.4 16.1 %all-to-all-start.1 = ((bf16[32,4,1024]{2,1,0:T(4,128)(2,1)}), bf16[32,4,1024]{2,1,0:T(4,128)(2,1)S(1)}, u32[]{:S(2)}, u32[]{:S(2)}) async-start(bf16[32,4,1024]{2,1,0:T(4,128)(2,1)} %gather_fusion), calls=%async_computation.1 | async-start | bytes 524288 | tf_op jit(solution)/shard_map/all_to_all | solution.py:13
  43.6 67.9 %collective-permute-start.1 = (bf16[352,1024]{1,0:T(8,128)(2,1)}, bf16[352,1024]{1,0:T(8,128)(2,1)S(1)}, u32[]{:S(2)}, u32[]{:S(2)}) collective-permute-start(bf16[352,1024]{1,0:T(8,128)(2,1)} %get-tuple-element.30), channel_id=1, source_target_pairs={{0,5},{1,6},{2,7},{3,8},{4,9},{16,21},{17,22},{18,23},{19,24},{20,... | collective-permute-start | bytes 2162696 | tf_op jit(solution)/shard_map/ppermute | solution.py:36
  46.2 65.3 %collective-permute-start.2 = (bf16[352,1024]{1,0:T(8,128)(2,1)}, bf16[352,1024]{1,0:T(8,128)(2,1)}, u32[]{:S(2)}, u32[]{:S(2)}) collective-permute-start(bf16[352,1024]{1,0:T(8,128)(2,1)} %get-tuple-element.29), channel_id=1, source_target_pairs={{0,10},{1,11},{2,12},{3,13},{4,14},{16,26},{17,27},{18,28},{19,29}... | collective-permute-start | bytes 2162696 | tf_op jit(solution)/shard_map/ppermute | solution.py:37
  55.3 58.3 %copy-start.31 = (s32[1,32]{1,0:T(1,128)S(1)}, s32[1,32]{1,0:T(1,128)}, u32[]{:S(2)}) copy-start(s32[1,32]{1,0:T(1,128)} %param.9) | copy-start | bytes 388
  55.3 56.1 %all-to-all-start.2 = ((bf16[16,8,1024]{2,1,0:T(8,128)(2,1)}), bf16[16,8,1024]{2,1,0:T(8,128)(2,1)S(1)}, u32[]{:S(2)}, u32[]{:S(2)}) async-start(bf16[16,8,1024]{2,1,0:T(8,128)(2,1)} %fusion.18), calls=%async_computation.2 | async-start | bytes 524288 | tf_op jit(solution)/shard_map/all_to_all | solution.py:13
  62.7 160.2 %all-gather.6.cloned.1.call-start = ((), (), s32[]{:S(2)}) async-start(), calls=%async_computation.10 | async-start | bytes 12255232 | tf_op jit(solution)/shard_map/all_gather | solution.py:43
  122.3 54.5 %all-to-all-start.3 = ((bf16[32,7,4,1024]{3,2,1,0:T(4,128)(2,1)}), bf16[32,7,4,1024]{3,2,1,0:T(4,128)(2,1)}, u32[]{:S(2)}, u32[]{:S(2)}) async-start(bf16[32,7,4,1024]{3,2,1,0:T(4,128)(2,1)} %pad_maximum_fusion.4), calls=%async_computation.3 | async-start | bytes 3670016 | tf_op jit(solution)/shard_map/all_to_all | solution.py:13
  185.9 4.5 %collective-permute-start = (bf16[8,40,1024]{2,1,0:T(8,128)(2,1)}, bf16[8,40,1024]{2,1,0:T(8,128)(2,1)}, u32[]{:S(2)}, u32[]{:S(2)}) collective-permute-start(bf16[8,40,1024]{2,1,0:T(8,128)(2,1)} %fusion.12), channel_id=1, source_target_pairs={{0,1},{1,0},{2,3},{3,2},{4,5},{5,4},{6,7},{7,6},{8,9},{9,8},{10,11... | collective-permute-start | bytes 1966088 | tf_op jit(solution)/shard_map/ppermute | solution.py:69
  193.9 27.6 %all-to-all-start.4 = ((bf16[8,40,1024]{2,1,0:T(8,128)(2,1)}), bf16[8,40,1024]{2,1,0:T(8,128)(2,1)S(1)}, u32[]{:S(2)}, u32[]{:S(2)}) async-start(bf16[8,40,1024]{2,1,0:T(8,128)(2,1)} %add_convert_fusion), calls=%async_computation.4 | async-start | bytes 1310720 | tf_op jit(solution)/shard_map/all_to_all | solution.py:13
  229.6 25.6 %all-to-all-start.5 = ((bf16[32,8,1024]{2,1,0:T(8,128)(2,1)}), bf16[32,8,1024]{2,1,0:T(8,128)(2,1)}, u32[]{:S(2)}, u32[]{:S(2)}) async-start(bf16[32,8,1024]{2,1,0:T(8,128)(2,1)} %broadcast_in_dim.24), calls=%async_computation.5 | async-start | bytes 1048576 | tf_op jit(solution)/shard_map/all_to_all | solution.py:13
  249.6 3.9 %copy-start.30 = (f32[8,1024]{1,0:T(8,128)S(1)}, f32[8,1024]{1,0:T(8,128)}, u32[]{:S(2)}) copy-start(f32[8,1024]{1,0:T(8,128)} %squeeze.151) | copy-start | bytes 98308
  250.7 1.7 copy-start.19
  252.4 0.9 copy-start.1
  252.4 1.1 copy-start.5
  258.5 27.2 %all-to-all-start.6 = ((bf16[32,8,1024]{2,1,0:T(8,128)(2,1)}), bf16[32,8,1024]{2,1,0:T(8,128)(2,1)}, u32[]{:S(2)}, u32[]{:S(2)}) async-start(bf16[32,8,1024]{2,1,0:T(8,128)(2,1)} %broadcast_in_dim.25), calls=%async_computation.6 | async-start | bytes 1048576 | tf_op jit(solution)/shard_map/all_to_all | solution.py:13
  268.3 2.9 copy-start.29
  269.5 3.1 copy-start.23
  271.1 1.4 copy-start.9
  271.2 1.4 copy-start.12
  271.2 1.6 copy-start.2
  271.2 1.8 copy-start.6
  271.2 2.0 copy-start.20
  288.9 22.0 %all-to-all-start.7 = ((bf16[32,8,1024]{2,1,0:T(8,128)(2,1)}), bf16[32,8,1024]{2,1,0:T(8,128)(2,1)}, u32[]{:S(2)}, u32[]{:S(2)}) async-start(bf16[32,8,1024]{2,1,0:T(8,128)(2,1)} %broadcast_in_dim.48), calls=%async_computation.7 | async-start | bytes 1048576 | tf_op jit(solution)/shard_map/all_to_all | solution.py:13
  293.8 4.0 %copy-start.28 = (f32[8,1024]{1,0:T(8,128)S(1)}, f32[8,1024]{1,0:T(8,128)}, u32[]{:S(2)}) copy-start(f32[8,1024]{1,0:T(8,128)} %squeeze.164) | copy-start | bytes 98308
  294.9 1.7 copy-start.26
  296.6 0.9 copy-start.15
  296.6 1.1 copy-start.17
  297.7 1.3 copy-start.10
  297.7 1.3 copy-start.13
  297.7 1.5 copy-start.24
  299.3 1.3 copy-start.3
  299.3 1.3 copy-start.7
  299.3 1.5 copy-start.21
  316.7 21.8 %all-to-all-start.8 = ((bf16[32,8,1024]{2,1,0:T(8,128)(2,1)}), bf16[32,8,1024]{2,1,0:T(8,128)(2,1)}, u32[]{:S(2)}, u32[]{:S(2)}) async-start(bf16[32,8,1024]{2,1,0:T(8,128)(2,1)} %broadcast_in_dim.49), calls=%async_computation.8 | async-start | bytes 1048576 | tf_op jit(solution)/shard_map/all_to_all | solution.py:13
  322.8 1.9 copy-start.16
  322.8 1.9 copy-start.18
  322.8 2.0 copy-start.27
  324.8 1.3 copy-start.11
  324.8 1.3 copy-start.14
  324.8 1.5 copy-start.25
  326.3 1.3 copy-start.4
  326.3 1.3 copy-start.8
  326.3 1.5 copy-start.22
Sparse Core Ops, SparseCore 0:
  34.4 76.4 all-gather.3
  113.7 73.6 all-gather.5

commit v5 on v4

--- a/solution.py
+++ b/solution.py
@@ -38,7 +38,14 @@
     first = swap(spread.at[target_row].get(mode="promise_in_bounds"), PATCH)
     first = dot(first.reshape(rows, width), tile).astype(BF16)
     total = jnp.sum(swap(first.reshape(lags, own, width), LAG).astype(F32), axis=0)
-    moved1, moved2, _ = lax.optimization_barrier((moved1, moved2, total))
+
+    def solve(k, total):
+        residual = (cotangent[k].astype(F32) - total).astype(BF16)
+        return dot(residual, inverse).astype(BF16)
+
+    results = [solve(0, total)]
+
+    moved1, moved2, _ = lax.optimization_barrier((moved1, moved2, results[0]))
     share = jnp.where(lag < back, tile[:third], jnp.where(lag < 2 * back, moved1, moved2))
     shares = lax.all_gather(share, LAG, axis=0)
 
@@ -47,12 +54,6 @@
         last = ready[l - 1 + 2 * back][3 * third - width :]
         return jnp.concatenate([ready[l - 1], ready[l - 1 + back], last])
 
-    def solve(k, total):
-        residual = (cotangent[k].astype(F32) - total).astype(BF16)
-        return dot(residual, inverse).astype(BF16)
-
-    results = [solve(0, total)]
-
     earlier = lag - jnp.arange(1, STEPS)
     index = jnp.where(earlier >= 0, earlier * blocks + target_row[:, None], patches + 1)
     chosen = known.at[index].get(mode="promise_in_bounds")
@@ -60,14 +61,12 @@
     ahead = jnp.broadcast_to(results[0].reshape(1, held, piece, width), (patches, held, piece, width))
     routed = swap(jnp.concatenate([ahead, chosen], axis=1), PATCH)
     states = [routed[:, :held].reshape(patches, own, width)]
-    routed = routed.reshape(chips, 2, -1, STEPS + 1, piece, width)
-
-    def terms(which):
-        part = lax.dynamic_index_in_dim(routed, which, 1, keepdims=False)
-        return dot(part[:, :, held:].reshape(-1, width), tile).reshape(chips, back * own, width)
-
-    got = lax.ppermute(terms(1 - core).astype(BF16), "core", [(0, 1), (1, 0)])
-    both = (terms(core) + got.astype(F32)).astype(BF16)
+    terms = dot(routed[:, held:].reshape(-1, width), tile).astype(BF16)
+    terms = terms.reshape(chips, 2, back * own, width)
+    kept = lax.dynamic_index_in_dim(terms, core, 1, keepdims=False)
+    sent = lax.dynamic_index_in_dim(terms, 1 - core, 1, keepdims=False)
+    got = lax.ppermute(sent, "core", [(0, 1), (1, 0)])
+    both = (kept.astype(F32) + got.astype(F32)).astype(BF16)
     parts = swap(both, "y")
     base = jnp.sum(parts.astype(F32), axis=0)
     base = base.reshape(held, back, piece, width).transpose(1, 0, 2, 3).reshape(back, own, width)

time: 350 us -> 347 us (level)
  blocking collectives: 0 us -> 15.8 us
  waiting for transfers between devices: 147 us -> 138 us
  starting transfers between devices: 78.6 us -> 73.4 us
  local copies, waits for them, and re-layouts: 52.1 us -> 47.3 us
  matrix products: 38.5 us -> 35 us
    all_to_all x9 -> x8, waiting for transfers between devices: 147 us -> 100 us  [swap(): return lax.all_to_all(value, axes, split_axis=0, concat_axis=0, tiled=True)]
    ppermute x1, waiting for transfers between devices: 0.01 us -> 23.6 us  [on_device(): lax.ppermute(tile[width - third:], LAG, [(i, i + 2 * back) for i in range...]
    all_to_all x0 -> x1, blocking collectives: none -> 15.8 us  [swap(): return lax.all_to_all(value, axes, split_axis=0, concat_axis=0, tiled=True)]
    ppermute x1, waiting for transfers between devices: 0.01 us -> 11.7 us  [on_device(): lax.ppermute(tile[third:2 * third], LAG, [(i, i + back) for i in range(ba...]
    all_to_all x9 -> x8, starting transfers between devices: 68.1 us -> 62.9 us  [swap(): return lax.all_to_all(value, axes, split_axis=0, concat_axis=0, tiled=True)]
    dot_general x2 -> x0, local copies, waits for them, and re-layouts: 3.69 us -> none  [dot(): return jnp.dot(a, b, preferred_element_type=F32)]
    dot_general x19 -> x18, matrix products: 38.5 us -> 35 us  [dot(): return jnp.dot(a, b, preferred_element_type=F32)]
  transfers between devices with their start and end apart: 14 -> 13, of which waited for: 8 -> 10; matrix products, arithmetic and copies ran while one was open for 20% -> 19% of each run, Pallas kernels for 0% -> 0%
where the time goes in v5:
time: 347 us; the launch traced here: 344 us
  waiting for transfers between devices  138 us (40%)
  starting transfers between devices  73.4 us (21%)
  local copies, waits for them, and re-layouts  47.3 us (14%)
  matrix products  35 us (10%)
  between operations  23.7 us (7%)
  blocking collectives  15.8 us (5%)
  other arithmetic  10.6 us (3%)
    all_to_all x8, waiting for transfers between devices, swap(): return lax.all_to_all(value, axes, split_axis=0, concat_axis=0, tiled=True)  100 us
    all_to_all x8, starting transfers between devices, swap(): return lax.all_to_all(value, axes, split_axis=0, concat_axis=0, tiled=True)  62.9 us
    dot_general x18, matrix products, dot(): return jnp.dot(a, b, preferred_element_type=F32)  35 us
    ppermute x1, waiting for transfers between devices, on_device(): lax.ppermute(tile[width - third:], LAG, [(i, i + 2 * back) for i in range...  23.6 us
    all_to_all x1, blocking collectives, swap(): return lax.all_to_all(value, axes, split_axis=0, concat_axis=0, tiled=True)  15.8 us
    ppermute x1, waiting for transfers between devices, on_device(): lax.ppermute(tile[third:2 * third], LAG, [(i, i + back) for i in range(ba...  11.7 us
    squeeze x5, local copies, waits for them, and re-layouts, tile_of(): return jnp.concatenate([ready[l - 1], ready[l - 1 + back], last])  9.02 us
  transfers between devices with their start and end apart: 13, of which 10 were waited for; matrix products, arithmetic and copies ran while one was open for 19% of the time, Pallas kernels for 0%

profile of v5, /device:TPU:64, one launch (start us, length us, event | category | flops | bytes accessed | tf_op | source)
XLA Modules:
  0.0 344.0 jit_solution(823162782063833985)
XLA Ops:
  6.5 1.9 reshape_squeeze.3
  8.4 12.6 %all-to-all-start = ((bf16[32,4,1024]{2,1,0:T(4,128)(2,1)}), bf16[32,4,1024]{2,1,0:T(4,128)(2,1)S(1)}, u32[]{:S(2)}, u32[]{:S(2)}) async-start(bf16[32,4,1024]{2,1,0:T(4,128)(2,1)} %reshape_squeeze.3), calls=%async_computation | async-start | bytes 524288 | tf_op jit(solution)/shard_map/all_to_all | solution.py:13
  21.2 1.2 fusion.122
  23.1 10.2 %all-to-all-done = bf16[32,4,1024]{2,1,0:T(4,128)(2,1)S(1)} async-done(((bf16[32,4,1024]{2,1,0:T(4,128)(2,1)}), bf16[32,4,1024]{2,1,0:T(4,128)(2,1)S(1)}, u32[]{:S(2)}, u32[]{:S(2)}) %all-to-all-start) | async-done | bytes 262176 | tf_op jit(solution)/shard_map/all_to_all | solution.py:13
  35.7 15.8 %all_to_all.45 = bf16[32,4,1024]{2,1,0:T(4,128)(2,1)S(1)} all-to-all(bf16[32,4,1024]{2,1,0:T(4,128)(2,1)S(1)} %gather_fusion), channel_id=1, replica_groups=mesh['x'=4,'z'=8,'y'=8,'core'=2] {'x','z'}, dimensions={0} | all-to-all | bytes 524288 | tf_op jit(solution)/shard_map/all_to_all | solution.py:13
  51.7 2.8 fusion.17
  54.4 7.2 %all-to-all-start.2 = ((bf16[16,8,1024]{2,1,0:T(8,128)(2,1)}), bf16[16,8,1024]{2,1,0:T(8,128)(2,1)S(1)}, u32[]{:S(2)}, u32[]{:S(2)}) async-start(bf16[16,8,1024]{2,1,0:T(8,128)(2,1)} %fusion.17), calls=%async_computation.2 | async-start | bytes 524288 | tf_op jit(solution)/shard_map/all_to_all | solution.py:13
  61.7 2.6 slice_bitcast_fusion.10
  64.3 4.4 %collective-permute-start.1 = (bf16[352,1024]{1,0:T(8,128)(2,1)}, bf16[352,1024]{1,0:T(8,128)(2,1)S(1)}, u32[]{:S(2)}, u32[]{:S(2)}) collective-permute-start(bf16[352,1024]{1,0:T(8,128)(2,1)} %get-tuple-element.30), channel_id=1, source_target_pairs={{0,5},{1,6},{2,7},{3,8},{4,9},{16,21},{17,22},{18,23},{19,24},{20,... | collective-permute-start | bytes 2162696 | tf_op jit(solution)/shard_map/ppermute | solution.py:36
  68.8 4.0 %collective-permute-start.2 = (bf16[352,1024]{1,0:T(8,128)(2,1)}, bf16[352,1024]{1,0:T(8,128)(2,1)}, u32[]{:S(2)}, u32[]{:S(2)}) collective-permute-start(bf16[352,1024]{1,0:T(8,128)(2,1)} %get-tuple-element.29), channel_id=1, source_target_pairs={{0,10},{1,11},{2,12},{3,13},{4,14},{16,26},{17,27},{18,28},{19,29}... | collective-permute-start | bytes 2162696 | tf_op jit(solution)/shard_map/ppermute | solution.py:37
  72.8 3.2 all-to-all-done.2
  76.0 1.7 bitcast_dynamic-update-slice_fusion.4
  77.8 11.7 %collective-permute-done.1 = bf16[352,1024]{1,0:T(8,128)(2,1)S(1)} collective-permute-done((bf16[352,1024]{1,0:T(8,128)(2,1)}, bf16[352,1024]{1,0:T(8,128)(2,1)S(1)}, u32[]{:S(2)}, u32[]{:S(2)}) %collective-permute-start.1) | collective-permute-done | bytes 720928 | tf_op jit(solution)/shard_map/ppermute | solution.py:36
  89.5 23.6 %collective-permute-done.2 = bf16[352,1024]{1,0:T(8,128)(2,1)} collective-permute-done((bf16[352,1024]{1,0:T(8,128)(2,1)}, bf16[352,1024]{1,0:T(8,128)(2,1)}, u32[]{:S(2)}, u32[]{:S(2)}) %collective-permute-start.2) | collective-permute-done | bytes 720928 | tf_op jit(solution)/shard_map/ppermute | solution.py:37
  113.1 2.1 bitcast_select_fusion
  115.5 4.0 %gather_fusion.1 = bf16[160,4,1024]{2,1,0:T(4,128)(2,1)S(1)} fusion(bf16[544,4,1024]{2,1,0:T(4,128)(2,1)} %all-gather.4.cloned.1.call-done, s32[1024]{0:T(1024)S(1)} %pad_clamp_fusion), kind=kCustom, calls=%fused_computation.1 | custom fusion | bytes 2622080 | tf_op jit(solution)/shard_map/gather | solution.py:59
  119.7 2.5 pad_maximum_fusion.4
  122.2 9.4 %all-to-all-start.3 = ((bf16[32,7,4,1024]{3,2,1,0:T(4,128)(2,1)}), bf16[32,7,4,1024]{3,2,1,0:T(4,128)(2,1)}, u32[]{:S(2)}, u32[]{:S(2)}) async-start(bf16[32,7,4,1024]{3,2,1,0:T(4,128)(2,1)} %pad_maximum_fusion.4), calls=%async_computation.3 | async-start | bytes 3670016 | tf_op jit(solution)/shard_map/all_to_all | solution.py:13
  131.6 44.0 %all-to-all-done.3 = bf16[32,7,4,1024]{3,2,1,0:T(4,128)(2,1)} async-done(((bf16[32,7,4,1024]{3,2,1,0:T(4,128)(2,1)}), bf16[32,7,4,1024]{3,2,1,0:T(4,128)(2,1)}, u32[]{:S(2)}, u32[]{:S(2)}) %all-to-all-start.3) | async-done | bytes 1835040 | tf_op jit(solution)/shard_map/all_to_all | solution.py:13
  175.6 1.8 slice.214
  177.4 1.2 reshape.182
  178.6 3.5 %fusion.10 = bf16[640,1024]{1,0:T(8,128)(2,1)S(1)} fusion(bf16[640,1024]{1,0:T(8,128)(2,1)} %reshape.182, bf16[1,1024,1024]{2,1,0:T(8,128)(2,1)} %param.6), kind=kOutput, calls=%fused_computation.17 | convolution fusion | flops 1342832640 | bytes 4718592 | tf_op jit(solution)/shard_map/dot_general | solution.py:17
  183.1 1.9 collective-permute-start
  185.0 2.4 collective-permute-done
  187.4 2.2 fusion.13
  189.6 7.1 %all-to-all-start.4 = ((bf16[8,40,1024]{2,1,0:T(8,128)(2,1)}), bf16[8,40,1024]{2,1,0:T(8,128)(2,1)S(1)}, u32[]{:S(2)}, u32[]{:S(2)}) async-start(bf16[8,40,1024]{2,1,0:T(8,128)(2,1)} %fusion.13), calls=%async_computation.4 | async-start | bytes 1310720 | tf_op jit(solution)/shard_map/all_to_all | solution.py:13
  200.1 1.3 slice.216
  202.3 15.0 %all-to-all-done.4 = bf16[8,40,1024]{2,1,0:T(8,128)(2,1)S(1)} async-done(((bf16[8,40,1024]{2,1,0:T(8,128)(2,1)}), bf16[8,40,1024]{2,1,0:T(8,128)(2,1)S(1)}, u32[]{:S(2)}, u32[]{:S(2)}) %all-to-all-start.4) | async-done | bytes 655392 | tf_op jit(solution)/shard_map/all_to_all | solution.py:13
  218.8 2.0 slice_bitcast_fusion.16
  220.8 1.4 slice_bitcast_fusion.9
  222.2 2.4 bitcast_dynamic-update-slice_fusion.3
  225.5 7.0 %all-to-all-start.5 = ((bf16[32,8,1024]{2,1,0:T(8,128)(2,1)}), bf16[32,8,1024]{2,1,0:T(8,128)(2,1)}, u32[]{:S(2)}, u32[]{:S(2)}) async-start(bf16[32,8,1024]{2,1,0:T(8,128)(2,1)} %broadcast_in_dim.24), calls=%async_computation.5 | async-start | bytes 1048576 | tf_op jit(solution)/shard_map/all_to_all | solution.py:13
  240.3 1.4 squeeze.148
  241.7 1.4 squeeze.154
  243.0 1.4 squeeze.161
  244.4 1.4 squeeze.169
  245.8 1.1 slice_bitcast_fusion.15
  247.0 1.7 slice_bitcast_fusion.7
  249.7 1.7 convolution_add_fusion.12
  251.5 2.4 bitcast_dynamic-update-slice_fusion.2
  254.7 9.8 %all-to-all-start.6 = ((bf16[32,8,1024]{2,1,0:T(8,128)(2,1)}), bf16[32,8,1024]{2,1,0:T(8,128)(2,1)}, u32[]{:S(2)}, u32[]{:S(2)}) async-start(bf16[32,8,1024]{2,1,0:T(8,128)(2,1)} %broadcast_in_dim.25), calls=%async_computation.6 | async-start | bytes 1048576 | tf_op jit(solution)/shard_map/all_to_all | solution.py:13
  264.6 1.1 slice_bitcast_fusion.14
  265.7 1.7 slice_bitcast_fusion.5
  267.5 1.3 convolution_add_fusion.10
  269.5 1.7 convolution_add_fusion.9
  271.2 10.7 %all-to-all-done.6 = bf16[32,8,1024]{2,1,0:T(8,128)(2,1)} async-done(((bf16[32,8,1024]{2,1,0:T(8,128)(2,1)}), bf16[32,8,1024]{2,1,0:T(8,128)(2,1)}, u32[]{:S(2)}, u32[]{:S(2)}) %all-to-all-start.6) | async-done | bytes 524320 | tf_op jit(solution)/shard_map/all_to_all | solution.py:13
  281.9 2.4 bitcast_dynamic-update-slice_fusion.1
  285.1 4.9 %all-to-all-start.7 = ((bf16[32,8,1024]{2,1,0:T(8,128)(2,1)}), bf16[32,8,1024]{2,1,0:T(8,128)(2,1)}, u32[]{:S(2)}, u32[]{:S(2)}) async-start(bf16[32,8,1024]{2,1,0:T(8,128)(2,1)} %broadcast_in_dim.48), calls=%async_computation.7 | async-start | bytes 1048576 | tf_op jit(solution)/shard_map/all_to_all | solution.py:13
  290.0 1.1 slice_bitcast_fusion.13
  291.2 1.7 slice_bitcast_fusion.3
  294.0 1.3 convolution_add_fusion.7
  295.5 1.2 convolution_add_fusion.6
  297.1 1.7 convolution_add_fusion.5
  298.8 8.4 %all-to-all-done.7 = bf16[32,8,1024]{2,1,0:T(8,128)(2,1)} async-done(((bf16[32,8,1024]{2,1,0:T(8,128)(2,1)}), bf16[32,8,1024]{2,1,0:T(8,128)(2,1)}, u32[]{:S(2)}, u32[]{:S(2)}) %all-to-all-start.7) | async-done | bytes 524320 | tf_op jit(solution)/shard_map/all_to_all | solution.py:13
  307.2 2.4 bitcast_dynamic-update-slice_fusion
  309.5 2.6 slice_bitcast_fusion.1
  313.0 4.9 %all-to-all-start.8 = ((bf16[32,8,1024]{2,1,0:T(8,128)(2,1)}), bf16[32,8,1024]{2,1,0:T(8,128)(2,1)}, u32[]{:S(2)}, u32[]{:S(2)}) async-start(bf16[32,8,1024]{2,1,0:T(8,128)(2,1)} %broadcast_in_dim.49), calls=%async_computation.8 | async-start | bytes 1048576 | tf_op jit(solution)/shard_map/all_to_all | solution.py:13
  317.9 1.1 slice_bitcast_fusion.12
  319.1 1.9 fusion.25
  321.0 1.2 convolution_add_fusion.3
  322.6 1.2 convolution_add_fusion.2
  324.1 1.7 convolution_add_fusion.1
  325.8 9.0 %all-to-all-done.8 = bf16[32,8,1024]{2,1,0:T(8,128)(2,1)} async-done(((bf16[32,8,1024]{2,1,0:T(8,128)(2,1)}), bf16[32,8,1024]{2,1,0:T(8,128)(2,1)}, u32[]{:S(2)}, u32[]{:S(2)}) %all-to-all-start.8) | async-done | bytes 524320 | tf_op jit(solution)/shard_map/all_to_all | solution.py:13
  334.8 2.4 fusion.34
  (98 shorter events, 16.1 us)
Async XLA Ops:
  6.5 69.5 %copy-start = (bf16[1024,1024]{1,0:T(8,128)(2,1)S(1)}, bf16[1024,1024]{1,0:T(8,128)(2,1)}, u32[]{:S(2)}) copy-start(bf16[1024,1024]{1,0:T(8,128)(2,1)} %param.7) | copy-start | bytes 6291460
  8.4 24.9 %all-to-all-start = ((bf16[32,4,1024]{2,1,0:T(4,128)(2,1)}), bf16[32,4,1024]{2,1,0:T(4,128)(2,1)S(1)}, u32[]{:S(2)}, u32[]{:S(2)}) async-start(bf16[32,4,1024]{2,1,0:T(4,128)(2,1)} %reshape_squeeze.3), calls=%async_computation | async-start | bytes 524288 | tf_op jit(solution)/shard_map/all_to_all | solution.py:13
  21.0 94.5 %all-gather.4.cloned.1.call-start = ((), (), s32[]{:S(2)}) async-start(), calls=%async_computation.9 | async-start | bytes 4734976 | tf_op jit(solution)/shard_map/all_gather | solution.py:31
  54.4 21.6 %all-to-all-start.2 = ((bf16[16,8,1024]{2,1,0:T(8,128)(2,1)}), bf16[16,8,1024]{2,1,0:T(8,128)(2,1)S(1)}, u32[]{:S(2)}, u32[]{:S(2)}) async-start(bf16[16,8,1024]{2,1,0:T(8,128)(2,1)} %fusion.17), calls=%async_computation.2 | async-start | bytes 524288 | tf_op jit(solution)/shard_map/all_to_all | solution.py:13
  61.6 157.1 %all-gather.6.cloned.1.call-start = ((), (), s32[]{:S(2)}) async-start(), calls=%async_computation.10 | async-start | bytes 12255232 | tf_op jit(solution)/shard_map/all_gather | solution.py:50
  64.3 25.2 %collective-permute-start.1 = (bf16[352,1024]{1,0:T(8,128)(2,1)}, bf16[352,1024]{1,0:T(8,128)(2,1)S(1)}, u32[]{:S(2)}, u32[]{:S(2)}) collective-permute-start(bf16[352,1024]{1,0:T(8,128)(2,1)} %get-tuple-element.30), channel_id=1, source_target_pairs={{0,5},{1,6},{2,7},{3,8},{4,9},{16,21},{17,22},{18,23},{19,24},{20,... | collective-permute-start | bytes 2162696 | tf_op jit(solution)/shard_map/ppermute | solution.py:36
  68.8 44.3 %collective-permute-start.2 = (bf16[352,1024]{1,0:T(8,128)(2,1)}, bf16[352,1024]{1,0:T(8,128)(2,1)}, u32[]{:S(2)}, u32[]{:S(2)}) collective-permute-start(bf16[352,1024]{1,0:T(8,128)(2,1)} %get-tuple-element.29), channel_id=1, source_target_pairs={{0,10},{1,11},{2,12},{3,13},{4,14},{16,26},{17,27},{18,28},{19,29}... | collective-permute-start | bytes 2162696 | tf_op jit(solution)/shard_map/ppermute | solution.py:37
  77.8 37.5 %copy-start.31 = (s32[1,32]{1,0:T(1,128)S(1)}, s32[1,32]{1,0:T(1,128)}, u32[]{:S(2)}) copy-start(s32[1,32]{1,0:T(1,128)} %param.9) | copy-start | bytes 388
  122.2 53.4 %all-to-all-start.3 = ((bf16[32,7,4,1024]{3,2,1,0:T(4,128)(2,1)}), bf16[32,7,4,1024]{3,2,1,0:T(4,128)(2,1)}, u32[]{:S(2)}, u32[]{:S(2)}) async-start(bf16[32,7,4,1024]{3,2,1,0:T(4,128)(2,1)} %pad_maximum_fusion.4), calls=%async_computation.3 | async-start | bytes 3670016 | tf_op jit(solution)/shard_map/all_to_all | solution.py:13
  183.1 4.3 %collective-permute-start = (bf16[8,40,1024]{2,1,0:T(8,128)(2,1)}, bf16[8,40,1024]{2,1,0:T(8,128)(2,1)}, u32[]{:S(2)}, u32[]{:S(2)}) collective-permute-start(bf16[8,40,1024]{2,1,0:T(8,128)(2,1)} %dynamic-slice_bitcast_fusion), channel_id=1, source_target_pairs={{0,1},{1,0},{2,3},{3,2},{4,5},{5,4},{6,7},{7,6},{8,9},{9,8},{10,11... | collective-permute-start | bytes 1966088 | tf_op jit(solution)/shard_map/ppermute | solution.py:68
  189.6 27.7 %all-to-all-start.4 = ((bf16[8,40,1024]{2,1,0:T(8,128)(2,1)}), bf16[8,40,1024]{2,1,0:T(8,128)(2,1)S(1)}, u32[]{:S(2)}, u32[]{:S(2)}) async-start(bf16[8,40,1024]{2,1,0:T(8,128)(2,1)} %fusion.13), calls=%async_computation.4 | async-start | bytes 1310720 | tf_op jit(solution)/shard_map/all_to_all | solution.py:13
  225.5 26.0 %all-to-all-start.5 = ((bf16[32,8,1024]{2,1,0:T(8,128)(2,1)}), bf16[32,8,1024]{2,1,0:T(8,128)(2,1)}, u32[]{:S(2)}, u32[]{:S(2)}) async-start(bf16[32,8,1024]{2,1,0:T(8,128)(2,1)} %broadcast_in_dim.24), calls=%async_computation.5 | async-start | bytes 1048576 | tf_op jit(solution)/shard_map/all_to_all | solution.py:13
  245.8 3.9 %copy-start.30 = (f32[8,1024]{1,0:T(8,128)S(1)}, f32[8,1024]{1,0:T(8,128)}, u32[]{:S(2)}) copy-start(f32[8,1024]{1,0:T(8,128)} %squeeze.148) | copy-start | bytes 98308
  246.9 1.7 copy-start.19
  248.6 0.9 copy-start.1
  248.6 1.1 copy-start.5
  254.7 27.2 %all-to-all-start.6 = ((bf16[32,8,1024]{2,1,0:T(8,128)(2,1)}), bf16[32,8,1024]{2,1,0:T(8,128)(2,1)}, u32[]{:S(2)}, u32[]{:S(2)}) async-start(bf16[32,8,1024]{2,1,0:T(8,128)(2,1)} %broadcast_in_dim.25), calls=%async_computation.6 | async-start | bytes 1048576 | tf_op jit(solution)/shard_map/all_to_all | solution.py:13
  264.6 2.9 copy-start.29
  265.7 3.1 copy-start.23
  267.4 1.4 copy-start.9
  267.4 1.4 copy-start.12
  267.4 1.6 copy-start.2
  267.4 1.8 copy-start.6
  267.4 2.0 copy-start.20
  285.1 22.0 %all-to-all-start.7 = ((bf16[32,8,1024]{2,1,0:T(8,128)(2,1)}), bf16[32,8,1024]{2,1,0:T(8,128)(2,1)}, u32[]{:S(2)}, u32[]{:S(2)}) async-start(bf16[32,8,1024]{2,1,0:T(8,128)(2,1)} %broadcast_in_dim.48), calls=%async_computation.7 | async-start | bytes 1048576 | tf_op jit(solution)/shard_map/all_to_all | solution.py:13
  290.0 4.0 %copy-start.28 = (f32[8,1024]{1,0:T(8,128)S(1)}, f32[8,1024]{1,0:T(8,128)}, u32[]{:S(2)}) copy-start(f32[8,1024]{1,0:T(8,128)} %squeeze.161) | copy-start | bytes 98308
  291.2 1.7 copy-start.26
  292.9 0.9 copy-start.15
  292.9 1.1 copy-start.17
  294.0 1.3 copy-start.10
  294.0 1.3 copy-start.13
  294.0 1.5 copy-start.24
  295.5 1.3 copy-start.3
  295.5 1.3 copy-start.7
  295.5 1.5 copy-start.21
  313.0 21.8 %all-to-all-start.8 = ((bf16[32,8,1024]{2,1,0:T(8,128)(2,1)}), bf16[32,8,1024]{2,1,0:T(8,128)(2,1)}, u32[]{:S(2)}, u32[]{:S(2)}) async-start(bf16[32,8,1024]{2,1,0:T(8,128)(2,1)} %broadcast_in_dim.49), calls=%async_computation.8 | async-start | bytes 1048576 | tf_op jit(solution)/shard_map/all_to_all | solution.py:13
  319.0 1.9 copy-start.16
  319.0 1.9 copy-start.18
  319.0 2.0 copy-start.27
  321.0 1.3 copy-start.11
  321.0 1.3 copy-start.14
  321.0 1.5 copy-start.25
  322.6 1.3 copy-start.4
  322.6 1.3 copy-start.8
  322.6 1.5 copy-start.22
Sparse Core Ops, SparseCore 0:
  34.4 66.5 all-gather.3
  115.3 73.5 all-gather.5

commit v6 on v5

--- a/solution.py
+++ b/solution.py
@@ -45,7 +45,8 @@
 
     results = [solve(0, total)]
 
-    moved1, moved2, _ = lax.optimization_barrier((moved1, moved2, results[0]))
+    lower = core == 0
+    moved1, moved2, lower, _ = lax.optimization_barrier((moved1, moved2, lower, results[0]))
     share = jnp.where(lag < back, tile[:third], jnp.where(lag < 2 * back, moved1, moved2))
     shares = lax.all_gather(share, LAG, axis=0)
 
@@ -63,8 +64,8 @@
     states = [routed[:, :held].reshape(patches, own, width)]
     terms = dot(routed[:, held:].reshape(-1, width), tile).astype(BF16)
     terms = terms.reshape(chips, 2, back * own, width)
-    kept = lax.dynamic_index_in_dim(terms, core, 1, keepdims=False)
-    sent = lax.dynamic_index_in_dim(terms, 1 - core, 1, keepdims=False)
+    kept = jnp.where(lower, terms[:, 0], terms[:, 1])
+    sent = jnp.where(lower, terms[:, 1], terms[:, 0])
     got = lax.ppermute(sent, "core", [(0, 1), (1, 0)])
     both = (kept.astype(F32) + got.astype(F32)).astype(BF16)
     parts = swap(both, "y")
@@ -79,7 +80,7 @@
             total = total + dot(state, tiles[l - 1])
         results.append(solve(k, total))
         if k + 1 < STEPS:
-            tiles.append(tile_of(k + 1, results[k]))
+            tiles.append(tile_of(k + 1, results[k - 1]))
             copies = jnp.broadcast_to(results[k][None], (patches, own, width))
             states.append(swap(copies, PATCH))
     return jnp.stack(results)

time: 347 us -> 335 us (0.965)
  blocking collectives: 15.8 us -> 70.5 us
  waiting for transfers between devices: 138 us -> 95.9 us
  starting transfers between devices: 73.4 us -> 57.2 us
  local copies, waits for them, and re-layouts: 47.3 us -> 40.9 us
    all_to_all x1 -> x2, blocking collectives: 15.8 us -> 70.5 us  [swap(): return lax.all_to_all(value, axes, split_axis=0, concat_axis=0, tiled=True)]
    all_to_all x8 -> x7, waiting for transfers between devices: 100 us -> 58.2 us  [swap(): return lax.all_to_all(value, axes, split_axis=0, concat_axis=0, tiled=True)]
    all_to_all x8 -> x7, starting transfers between devices: 62.9 us -> 46.6 us  [swap(): return lax.all_to_all(value, axes, split_axis=0, concat_axis=0, tiled=True)]
  transfers between devices with their start and end apart: 13 -> 12, of which waited for: 10 -> 10; matrix products, arithmetic and copies ran while one was open for 19% -> 18% of each run, Pallas kernels for 0% -> 0%
where the time goes in v6:
time: 335 us; the launch traced here: 333 us
  waiting for transfers between devices  95.9 us (29%)
  blocking collectives  70.5 us (21%)
  starting transfers between devices  57.2 us (17%)
  local copies, waits for them, and re-layouts  40.9 us (12%)
  matrix products  36.3 us (11%)
  between operations  23.5 us (7%)
  other arithmetic  8.32 us (2%)
    all_to_all x2, blocking collectives, swap(): return lax.all_to_all(value, axes, split_axis=0, concat_axis=0, tiled=True)  70.5 us
    all_to_all x7, waiting for transfers between devices, swap(): return lax.all_to_all(value, axes, split_axis=0, concat_axis=0, tiled=True)  58.2 us
    all_to_all x7, starting transfers between devices, swap(): return lax.all_to_all(value, axes, split_axis=0, concat_axis=0, tiled=True)  46.6 us
    dot_general x18, matrix products, dot(): return jnp.dot(a, b, preferred_element_type=F32)  36.3 us
    ppermute x1, waiting for transfers between devices, on_device(): lax.ppermute(tile[width - third:], LAG, [(i, i + 2 * back) for i in range...  23.6 us
    ppermute x1, waiting for transfers between devices, on_device(): lax.ppermute(tile[third:2 * third], LAG, [(i, i + back) for i in range(ba...  11.8 us
    squeeze x5, local copies, waits for them, and re-layouts, tile_of(): return jnp.concatenate([ready[l - 1], ready[l - 1 + back], last])  10.8 us
  transfers between devices with their start and end apart: 12, of which 10 were waited for; matrix products, arithmetic and copies ran while one was open for 18% of the time, Pallas kernels for 0%

profile of v6, /device:TPU:64, one launch (start us, length us, event | category | flops | bytes accessed | tf_op | source)
XLA Modules:
  0.0 332.5 jit_solution(17620388536535539190)
XLA Ops:
  6.5 1.9 reshape_squeeze.3
  8.4 12.6 %all-to-all-start = ((bf16[32,4,1024]{2,1,0:T(4,128)(2,1)}), bf16[32,4,1024]{2,1,0:T(4,128)(2,1)S(1)}, u32[]{:S(2)}, u32[]{:S(2)}) async-start(bf16[32,4,1024]{2,1,0:T(4,128)(2,1)} %reshape_squeeze.3), calls=%async_computation | async-start | bytes 524288 | tf_op jit(solution)/shard_map/all_to_all | solution.py:13
  21.1 1.2 fusion.124
  23.1 10.2 %all-to-all-done = bf16[32,4,1024]{2,1,0:T(4,128)(2,1)S(1)} async-done(((bf16[32,4,1024]{2,1,0:T(4,128)(2,1)}), bf16[32,4,1024]{2,1,0:T(4,128)(2,1)S(1)}, u32[]{:S(2)}, u32[]{:S(2)}) %all-to-all-start) | async-done | bytes 262176 | tf_op jit(solution)/shard_map/all_to_all | solution.py:13
  33.3 0.9 maximum_maximum_fusion
  35.7 15.8 %all_to_all.45 = bf16[32,4,1024]{2,1,0:T(4,128)(2,1)S(1)} all-to-all(bf16[32,4,1024]{2,1,0:T(4,128)(2,1)S(1)} %gather_fusion), channel_id=1, replica_groups=mesh['x'=4,'z'=8,'y'=8,'core'=2] {'x','z'}, dimensions={0} | all-to-all | bytes 524288 | tf_op jit(solution)/shard_map/all_to_all | solution.py:13
  51.6 2.7 fusion.17
  54.4 7.2 %all-to-all-start.2 = ((bf16[16,8,1024]{2,1,0:T(8,128)(2,1)}), bf16[16,8,1024]{2,1,0:T(8,128)(2,1)S(1)}, u32[]{:S(2)}, u32[]{:S(2)}) async-start(bf16[16,8,1024]{2,1,0:T(8,128)(2,1)} %fusion.17), calls=%async_computation.2 | async-start | bytes 524288 | tf_op jit(solution)/shard_map/all_to_all | solution.py:13
  61.6 2.6 slice_bitcast_fusion.10
  64.3 4.4 %collective-permute-start = (bf16[352,1024]{1,0:T(8,128)(2,1)}, bf16[352,1024]{1,0:T(8,128)(2,1)S(1)}, u32[]{:S(2)}, u32[]{:S(2)}) collective-permute-start(bf16[352,1024]{1,0:T(8,128)(2,1)} %get-tuple-element.32), channel_id=1, source_target_pairs={{0,5},{1,6},{2,7},{3,8},{4,9},{16,21},{17,22},{18,23},{19,24},{20,... | collective-permute-start | bytes 2162696 | tf_op jit(solution)/shard_map/ppermute | solution.py:36
  68.7 3.9 %collective-permute-start.1 = (bf16[352,1024]{1,0:T(8,128)(2,1)}, bf16[352,1024]{1,0:T(8,128)(2,1)}, u32[]{:S(2)}, u32[]{:S(2)}) collective-permute-start(bf16[352,1024]{1,0:T(8,128)(2,1)} %get-tuple-element.31), channel_id=1, source_target_pairs={{0,10},{1,11},{2,12},{3,13},{4,14},{16,26},{17,27},{18,28},{19,29}... | collective-permute-start | bytes 2162696 | tf_op jit(solution)/shard_map/ppermute | solution.py:37
  72.6 3.3 all-to-all-done.2
  76.0 1.7 bitcast_dynamic-update-slice_fusion.4
  77.7 11.8 %collective-permute-done = bf16[352,1024]{1,0:T(8,128)(2,1)S(1)} collective-permute-done((bf16[352,1024]{1,0:T(8,128)(2,1)}, bf16[352,1024]{1,0:T(8,128)(2,1)S(1)}, u32[]{:S(2)}, u32[]{:S(2)}) %collective-permute-start) | collective-permute-done | bytes 720928 | tf_op jit(solution)/shard_map/ppermute | solution.py:36
  89.5 23.6 %collective-permute-done.1 = bf16[352,1024]{1,0:T(8,128)(2,1)} collective-permute-done((bf16[352,1024]{1,0:T(8,128)(2,1)}, bf16[352,1024]{1,0:T(8,128)(2,1)}, u32[]{:S(2)}, u32[]{:S(2)}) %collective-permute-start.1) | collective-permute-done | bytes 720928 | tf_op jit(solution)/shard_map/ppermute | solution.py:37
  113.1 2.1 bitcast_select_fusion.1
  115.5 4.0 %gather_fusion.1 = bf16[160,4,1024]{2,1,0:T(4,128)(2,1)S(1)} fusion(bf16[544,4,1024]{2,1,0:T(4,128)(2,1)} %all-gather.4.cloned.1.call-done, s32[1024]{0:T(1024)S(1)} %pad_clamp_fusion), kind=kCustom, calls=%fused_computation.1 | custom fusion | bytes 2622080 | tf_op jit(solution)/shard_map/gather | solution.py:60
  119.7 1.2 pad_maximum_fusion.4
  120.9 54.7 %all_to_all.46 = bf16[32,7,4,1024]{3,2,1,0:T(4,128)(2,1)S(1)} all-to-all(bf16[32,7,4,1024]{3,2,1,0:T(4,128)(2,1)S(1)} %pad_maximum_fusion.4), channel_id=1, replica_groups=mesh['x'=4,'z'=8,'y'=8,'core'=2] {'x','z'}, dimensions={0} | all-to-all | bytes 3670016 | tf_op jit(solution)/shard_map/all_to_all | solution.py:13
  175.5 1.3 copy-done.1
  177.2 1.2 reshape.186
  178.5 3.6 %fusion.10 = bf16[640,1024]{1,0:T(8,128)(2,1)S(1)} fusion(bf16[640,1024]{1,0:T(8,128)(2,1)} %reshape.186, bf16[1,1024,1024]{2,1,0:T(8,128)(2,1)} %param.6), kind=kOutput, calls=%fused_computation.17 | convolution fusion | flops 1342832640 | bytes 4718592 | tf_op jit(solution)/shard_map/dot_general | solution.py:17
  182.1 2.1 collective-permute-start.2
  184.2 2.3 collective-permute-done.2
  186.5 1.2 fusion.13
  187.7 6.9 %all-to-all-start.4 = ((bf16[8,40,1024]{2,1,0:T(8,128)(2,1)}), bf16[8,40,1024]{2,1,0:T(8,128)(2,1)S(1)}, u32[]{:S(2)}, u32[]{:S(2)}) async-start(bf16[8,40,1024]{2,1,0:T(8,128)(2,1)} %fusion.13), calls=%async_computation.4 | async-start | bytes 1310720 | tf_op jit(solution)/shard_map/all_to_all | solution.py:13
  205.7 0.9 reshape.189
  206.6 8.7 %all-to-all-done.4 = bf16[8,40,1024]{2,1,0:T(8,128)(2,1)S(1)} async-done(((bf16[8,40,1024]{2,1,0:T(8,128)(2,1)}), bf16[8,40,1024]{2,1,0:T(8,128)(2,1)S(1)}, u32[]{:S(2)}, u32[]{:S(2)}) %all-to-all-start.4) | async-done | bytes 655392 | tf_op jit(solution)/shard_map/all_to_all | solution.py:13
  218.5 1.4 slice_bitcast_fusion.9
  219.9 2.0 slice_bitcast_fusion.16
  221.9 2.4 bitcast_dynamic-update-slice_fusion.3
  224.3 0.9 broadcast_in_dim.24
  225.2 5.1 %all-to-all-start.5 = ((bf16[32,8,1024]{2,1,0:T(8,128)(2,1)}), bf16[32,8,1024]{2,1,0:T(8,128)(2,1)}, u32[]{:S(2)}, u32[]{:S(2)}) async-start(bf16[32,8,1024]{2,1,0:T(8,128)(2,1)} %broadcast_in_dim.24), calls=%async_computation.5 | async-start | bytes 1048576 | tf_op jit(solution)/shard_map/all_to_all | solution.py:13
  230.3 1.1 slice_bitcast_fusion.15
  231.5 1.7 slice_bitcast_fusion.7
  233.2 1.7 convolution_add_fusion.12
  234.9 2.5 slice_bitcast_fusion.5
  237.5 10.7 %all-to-all-done.5 = bf16[32,8,1024]{2,1,0:T(8,128)(2,1)} async-done(((bf16[32,8,1024]{2,1,0:T(8,128)(2,1)}), bf16[32,8,1024]{2,1,0:T(8,128)(2,1)}, u32[]{:S(2)}, u32[]{:S(2)}) %all-to-all-start.5) | async-done | bytes 524320 | tf_op jit(solution)/shard_map/all_to_all | solution.py:13
  248.2 2.4 bitcast_dynamic-update-slice_fusion.2
  251.4 4.9 %all-to-all-start.6 = ((bf16[32,8,1024]{2,1,0:T(8,128)(2,1)}), bf16[32,8,1024]{2,1,0:T(8,128)(2,1)}, u32[]{:S(2)}, u32[]{:S(2)}) async-start(bf16[32,8,1024]{2,1,0:T(8,128)(2,1)} %broadcast_in_dim.25), calls=%async_computation.6 | async-start | bytes 1048576 | tf_op jit(solution)/shard_map/all_to_all | solution.py:13
  256.3 1.1 slice_bitcast_fusion.14
  257.5 2.0 convolution_add_fusion.10
  259.7 1.7 convolution_add_fusion.9
  261.4 2.5 slice_bitcast_fusion.3
  263.9 9.3 %all-to-all-done.6 = bf16[32,8,1024]{2,1,0:T(8,128)(2,1)} async-done(((bf16[32,8,1024]{2,1,0:T(8,128)(2,1)}), bf16[32,8,1024]{2,1,0:T(8,128)(2,1)}, u32[]{:S(2)}, u32[]{:S(2)}) %all-to-all-start.6) | async-done | bytes 524320 | tf_op jit(solution)/shard_map/all_to_all | solution.py:13
  273.3 2.4 bitcast_dynamic-update-slice_fusion.1
  275.7 0.9 broadcast_in_dim.48
  276.5 4.9 %all-to-all-start.7 = ((bf16[32,8,1024]{2,1,0:T(8,128)(2,1)}), bf16[32,8,1024]{2,1,0:T(8,128)(2,1)}, u32[]{:S(2)}, u32[]{:S(2)}) async-start(bf16[32,8,1024]{2,1,0:T(8,128)(2,1)} %broadcast_in_dim.48), calls=%async_computation.7 | async-start | bytes 1048576 | tf_op jit(solution)/shard_map/all_to_all | solution.py:13
  281.4 1.1 slice_bitcast_fusion.13
  283.4 1.9 convolution_add_fusion.7
  285.4 1.2 convolution_add_fusion.6
  287.0 1.7 convolution_add_fusion.5
  288.7 2.6 slice_bitcast_fusion.1
  291.2 7.1 %all-to-all-done.7 = bf16[32,8,1024]{2,1,0:T(8,128)(2,1)} async-done(((bf16[32,8,1024]{2,1,0:T(8,128)(2,1)}), bf16[32,8,1024]{2,1,0:T(8,128)(2,1)}, u32[]{:S(2)}, u32[]{:S(2)}) %all-to-all-start.7) | async-done | bytes 524320 | tf_op jit(solution)/shard_map/all_to_all | solution.py:13
  298.3 2.4 bitcast_dynamic-update-slice_fusion
  300.7 0.9 broadcast_in_dim.49
  301.6 4.9 %all-to-all-start.8 = ((bf16[32,8,1024]{2,1,0:T(8,128)(2,1)}), bf16[32,8,1024]{2,1,0:T(8,128)(2,1)}, u32[]{:S(2)}, u32[]{:S(2)}) async-start(bf16[32,8,1024]{2,1,0:T(8,128)(2,1)} %broadcast_in_dim.49), calls=%async_computation.8 | async-start | bytes 1048576 | tf_op jit(solution)/shard_map/all_to_all | solution.py:13
  306.5 1.1 slice_bitcast_fusion.12
  307.7 1.9 fusion.25
  309.6 1.2 convolution_add_fusion.3
  311.2 1.2 convolution_add_fusion.2
  312.7 1.7 convolution_add_fusion.1
  314.4 8.9 %all-to-all-done.8 = bf16[32,8,1024]{2,1,0:T(8,128)(2,1)} async-done(((bf16[32,8,1024]{2,1,0:T(8,128)(2,1)}), bf16[32,8,1024]{2,1,0:T(8,128)(2,1)}, u32[]{:S(2)}, u32[]{:S(2)}) %all-to-all-start.8) | async-done | bytes 524320 | tf_op jit(solution)/shard_map/all_to_all | solution.py:13
  323.3 2.4 fusion.34
  (88 shorter events, 10.9 us)
Async XLA Ops:
  6.5 69.4 %copy-start = (bf16[1024,1024]{1,0:T(8,128)(2,1)S(1)}, bf16[1024,1024]{1,0:T(8,128)(2,1)}, u32[]{:S(2)}) copy-start(bf16[1024,1024]{1,0:T(8,128)(2,1)} %param.7) | copy-start | bytes 6291460
  8.4 24.9 %all-to-all-start = ((bf16[32,4,1024]{2,1,0:T(4,128)(2,1)}), bf16[32,4,1024]{2,1,0:T(4,128)(2,1)S(1)}, u32[]{:S(2)}, u32[]{:S(2)}) async-start(bf16[32,4,1024]{2,1,0:T(4,128)(2,1)} %reshape_squeeze.3), calls=%async_computation | async-start | bytes 524288 | tf_op jit(solution)/shard_map/all_to_all | solution.py:13
  21.0 94.4 %all-gather.4.cloned.1.call-start = ((), (), s32[]{:S(2)}) async-start(), calls=%async_computation.9 | async-start | bytes 4734976 | tf_op jit(solution)/shard_map/all_gather | solution.py:31
  54.4 21.6 %all-to-all-start.2 = ((bf16[16,8,1024]{2,1,0:T(8,128)(2,1)}), bf16[16,8,1024]{2,1,0:T(8,128)(2,1)S(1)}, u32[]{:S(2)}, u32[]{:S(2)}) async-start(bf16[16,8,1024]{2,1,0:T(8,128)(2,1)} %fusion.17), calls=%async_computation.2 | async-start | bytes 524288 | tf_op jit(solution)/shard_map/all_to_all | solution.py:13
  61.6 156.9 %all-gather.6.cloned.1.call-start = ((), (), s32[]{:S(2)}) async-start(), calls=%async_computation.10 | async-start | bytes 12255232 | tf_op jit(solution)/shard_map/all_gather | solution.py:51
  64.3 25.2 %collective-permute-start = (bf16[352,1024]{1,0:T(8,128)(2,1)}, bf16[352,1024]{1,0:T(8,128)(2,1)S(1)}, u32[]{:S(2)}, u32[]{:S(2)}) collective-permute-start(bf16[352,1024]{1,0:T(8,128)(2,1)} %get-tuple-element.32), channel_id=1, source_target_pairs={{0,5},{1,6},{2,7},{3,8},{4,9},{16,21},{17,22},{18,23},{19,24},{20,... | collective-permute-start | bytes 2162696 | tf_op jit(solution)/shard_map/ppermute | solution.py:36
  68.7 44.4 %collective-permute-start.1 = (bf16[352,1024]{1,0:T(8,128)(2,1)}, bf16[352,1024]{1,0:T(8,128)(2,1)}, u32[]{:S(2)}, u32[]{:S(2)}) collective-permute-start(bf16[352,1024]{1,0:T(8,128)(2,1)} %get-tuple-element.31), channel_id=1, source_target_pairs={{0,10},{1,11},{2,12},{3,13},{4,14},{16,26},{17,27},{18,28},{19,29}... | collective-permute-start | bytes 2162696 | tf_op jit(solution)/shard_map/ppermute | solution.py:37
  77.7 37.5 %copy-start.26 = (s32[1,32]{1,0:T(1,128)S(1)}, s32[1,32]{1,0:T(1,128)}, u32[]{:S(2)}) copy-start(s32[1,32]{1,0:T(1,128)} %param.9) | copy-start | bytes 388
  175.5 1.3 copy-start.1
  182.1 23.5 %slice-start = ((bf16[32,7,4,1024]{3,2,1,0:T(4,128)(2,1)}), bf16[32,2,4,1024]{3,2,1,0:T(4,128)(2,1)S(1)}, s32[]{:S(2)}) async-start(bf16[32,7,4,1024]{3,2,1,0:T(4,128)(2,1)} %copy-done.1), calls=%async_computation.11 | async-start | bytes 1048576 | tf_op jit(solution)/shard_map/slice | solution.py:64
  182.1 4.4 %collective-permute-start.2 = (bf16[8,40,1024]{2,1,0:T(8,128)(2,1)S(1)}, bf16[8,40,1024]{2,1,0:T(8,128)(2,1)S(1)}, u32[]{:S(2)}, u32[]{:S(2)}) collective-permute-start(bf16[8,40,1024]{2,1,0:T(8,128)(2,1)S(1)} %fusion.35), channel_id=1, source_target_pairs={{0,1},{1,0},{2,3},{3,2},{4,5},{5,4},{6,7},{7,6},{8,9},{9,8},{10,11... | collective-permute-start | bytes 1966088 | tf_op jit(solution)/shard_map/ppermute | solution.py:69
  187.7 27.6 %all-to-all-start.4 = ((bf16[8,40,1024]{2,1,0:T(8,128)(2,1)}), bf16[8,40,1024]{2,1,0:T(8,128)(2,1)S(1)}, u32[]{:S(2)}, u32[]{:S(2)}) async-start(bf16[8,40,1024]{2,1,0:T(8,128)(2,1)} %fusion.13), calls=%async_computation.4 | async-start | bytes 1310720 | tf_op jit(solution)/shard_map/all_to_all | solution.py:13
  225.2 23.0 %all-to-all-start.5 = ((bf16[32,8,1024]{2,1,0:T(8,128)(2,1)}), bf16[32,8,1024]{2,1,0:T(8,128)(2,1)}, u32[]{:S(2)}, u32[]{:S(2)}) async-start(bf16[32,8,1024]{2,1,0:T(8,128)(2,1)} %broadcast_in_dim.24), calls=%async_computation.5 | async-start | bytes 1048576 | tf_op jit(solution)/shard_map/all_to_all | solution.py:13
  230.3 2.9 copy-start.25
  231.5 3.5 %copy-start.16 = (bf16[320,1024]{1,0:T(8,128)(2,1)}, bf16[320,1024]{1,0:T(8,128)(2,1)S(1)}, u32[]{:S(2)}) copy-start(bf16[320,1024]{1,0:T(8,128)(2,1)S(1)} %slice_bitcast_fusion.15) | copy-start | bytes 1966084
  233.2 1.8 copy-start.2
  233.2 1.8 copy-start.6
  251.4 21.9 %all-to-all-start.6 = ((bf16[32,8,1024]{2,1,0:T(8,128)(2,1)}), bf16[32,8,1024]{2,1,0:T(8,128)(2,1)}, u32[]{:S(2)}, u32[]{:S(2)}) async-start(bf16[32,8,1024]{2,1,0:T(8,128)(2,1)} %broadcast_in_dim.25), calls=%async_computation.6 | async-start | bytes 1048576 | tf_op jit(solution)/shard_map/all_to_all | solution.py:13
  257.5 2.0 copy-start.20
  257.5 2.0 copy-start.3
  257.5 2.0 copy-start.7
  257.5 2.2 copy-start.17
  276.5 21.8 %all-to-all-start.7 = ((bf16[32,8,1024]{2,1,0:T(8,128)(2,1)}), bf16[32,8,1024]{2,1,0:T(8,128)(2,1)}, u32[]{:S(2)}, u32[]{:S(2)}) async-start(bf16[32,8,1024]{2,1,0:T(8,128)(2,1)} %broadcast_in_dim.48), calls=%async_computation.7 | async-start | bytes 1048576 | tf_op jit(solution)/shard_map/all_to_all | solution.py:13
  282.6 0.9 copy-start.23
  283.4 1.9 copy-start.10
  283.4 1.9 copy-start.12
  283.4 2.0 copy-start.21
  285.4 1.3 copy-start.4
  285.4 1.3 copy-start.8
  285.4 1.5 copy-start.18
  301.6 21.7 %all-to-all-start.8 = ((bf16[32,8,1024]{2,1,0:T(8,128)(2,1)}), bf16[32,8,1024]{2,1,0:T(8,128)(2,1)}, u32[]{:S(2)}, u32[]{:S(2)}) async-start(bf16[32,8,1024]{2,1,0:T(8,128)(2,1)} %broadcast_in_dim.49), calls=%async_computation.8 | async-start | bytes 1048576 | tf_op jit(solution)/shard_map/all_to_all | solution.py:13
  307.6 1.9 copy-start.14
  307.6 1.9 copy-start.15
  307.6 2.0 copy-start.24
  309.6 1.3 copy-start.11
  309.6 1.3 copy-start.13
  309.6 1.5 copy-start.22
  311.2 1.3 copy-start.5
  311.2 1.3 copy-start.9
  311.2 1.5 copy-start.19
Sparse Core Ops, SparseCore 0:
  34.4 66.5 all-gather.3
  115.3 73.5 all-gather.5

commit v7 on v6

--- a/solution.py
+++ b/solution.py
@@ -62,15 +62,23 @@
     ahead = jnp.broadcast_to(results[0].reshape(1, held, piece, width), (patches, held, piece, width))
     routed = swap(jnp.concatenate([ahead, chosen], axis=1), PATCH)
     states = [routed[:, :held].reshape(patches, own, width)]
-    terms = dot(routed[:, held:].reshape(-1, width), tile).astype(BF16)
-    terms = terms.reshape(chips, 2, back * own, width)
-    kept = jnp.where(lower, terms[:, 0], terms[:, 1])
-    sent = jnp.where(lower, terms[:, 1], terms[:, 0])
+    soon, late = held + 2, STEPS + 1
+
+    def terms(rows_of, first, last):
+        return dot(rows_of[:, first:last].reshape(-1, width), tile).astype(BF16)
+
+    def per_step(summed, count):
+        return list(summed.reshape(held, count, piece, width).transpose(1, 0, 2, 3).reshape(count, own, width))
+
+    near = terms(routed, held, soon).reshape(chips, 2, -1, width)
+    kept = jnp.where(lower, near[:, 0], near[:, 1])
+    sent = jnp.where(lower, near[:, 1], near[:, 0])
     got = lax.ppermute(sent, "core", [(0, 1), (1, 0)])
     both = (kept.astype(F32) + got.astype(F32)).astype(BF16)
     parts = swap(both, "y")
-    base = jnp.sum(parts.astype(F32), axis=0)
-    base = base.reshape(held, back, piece, width).transpose(1, 0, 2, 3).reshape(back, own, width)
+    base = per_step(jnp.sum(parts.astype(F32), axis=0), 2)
+    after, _ = lax.optimization_barrier((routed, sent))
+    far = lax.psum_scatter(terms(after, soon, late), LAG, scatter_dimension=0, tiled=True)
 
     tiles = [tile_of(1, both)]
     for k in range(1, STEPS):
@@ -79,6 +87,9 @@
             state = lax.dynamic_index_in_dim(states[k - l], listed[l - 1], 0, keepdims=False)
             total = total + dot(state, tiles[l - 1])
         results.append(solve(k, total))
+        if k == 2:
+            far, _ = lax.optimization_barrier((far, results[k]))
+            base += per_step(far.astype(F32), back - 2)
         if k + 1 < STEPS:
             tiles.append(tile_of(k + 1, results[k - 1]))
             copies = jnp.broadcast_to(results[k][None], (patches, own, width))

time: 335 us -> 344 us (1.027)
  the two profiles are of different devices: /device:TPU:64 before, /device:TPU:89 now
where the time goes in v7:
time: 344 us; the launch traced here: 341 us
  waiting for transfers between devices  85.6 us (25%)
  starting transfers between devices  73.9 us (21%)
  blocking collectives  63.7 us (19%)
  local copies, waits for them, and re-layouts  47.6 us (14%)
  matrix products  39.3 us (11%)
  between operations  22.5 us (7%)
  other arithmetic  8.85 us (3%)
    all_to_all x7, starting transfers between devices, swap(): return lax.all_to_all(value, axes, split_axis=0, concat_axis=0, tiled=True)  68.9 us
    all_to_all x2, blocking collectives, swap(): return lax.all_to_all(value, axes, split_axis=0, concat_axis=0, tiled=True)  63.7 us
    dot_general x19, matrix products, dot(): return jnp.dot(a, b, preferred_element_type=F32)  39.3 us
    all_to_all x7, waiting for transfers between devices, swap(): return lax.all_to_all(value, axes, split_axis=0, concat_axis=0, tiled=True)  37.1 us
    ppermute x1, waiting for transfers between devices, on_device(): lax.ppermute(tile[third:2 * third], LAG, [(i, i + back) for i in range(ba...  29.4 us
    reduce_scatter x1, waiting for transfers between devices, on_device(): lax.psum_scatter(terms(after, soon, late), LAG, scatter_dimension=0, tile...  17.6 us
    squeeze x5, local copies, waits for them, and re-layouts, tile_of(): return jnp.concatenate([ready[l - 1], ready[l - 1 + back], last])  10.7 us
    slice x5, local copies, waits for them, and re-layouts, tile_of(): last = ready[l - 1 + 2 * back][3 * third - width:]  8.22 us
  transfers between devices with their start and end apart: 13, of which 8 were waited for; matrix products, arithmetic and copies ran while one was open for 24% of the time, Pallas kernels for 0%

profile of v7, /device:TPU:89, one launch (start us, length us, event | category | flops | bytes accessed | tf_op | source)
XLA Modules:
  0.0 341.5 jit_solution(6194956990372748947)
XLA Ops:
  6.5 1.9 reshape_squeeze.3
  8.4 12.0 %all-to-all-start = ((bf16[32,4,1024]{2,1,0:T(4,128)(2,1)}), bf16[32,4,1024]{2,1,0:T(4,128)(2,1)S(1)}, u32[]{:S(2)}, u32[]{:S(2)}) async-start(bf16[32,4,1024]{2,1,0:T(4,128)(2,1)} %reshape_squeeze.3), calls=%async_computation | async-start | bytes 524288 | tf_op jit(solution)/shard_map/all_to_all | solution.py:13
  20.5 1.2 fusion.131
  22.6 9.6 %all-to-all-done = bf16[32,4,1024]{2,1,0:T(4,128)(2,1)S(1)} async-done(((bf16[32,4,1024]{2,1,0:T(4,128)(2,1)}), bf16[32,4,1024]{2,1,0:T(4,128)(2,1)S(1)}, u32[]{:S(2)}, u32[]{:S(2)}) %all-to-all-start) | async-done | bytes 262176 | tf_op jit(solution)/shard_map/all_to_all | solution.py:13
  34.6 14.6 %all_to_all.45 = bf16[32,4,1024]{2,1,0:T(4,128)(2,1)S(1)} all-to-all(bf16[32,4,1024]{2,1,0:T(4,128)(2,1)S(1)} %gather_fusion), channel_id=1, replica_groups=mesh['x'=4,'z'=8,'y'=8,'core'=2] {'x','z'}, dimensions={0} | all-to-all | bytes 524288 | tf_op jit(solution)/shard_map/all_to_all | solution.py:13
  49.3 2.8 fusion.21
  52.1 9.9 %all-to-all-start.2 = ((bf16[16,8,1024]{2,1,0:T(8,128)(2,1)}), bf16[16,8,1024]{2,1,0:T(8,128)(2,1)S(1)}, u32[]{:S(2)}, u32[]{:S(2)}) async-start(bf16[16,8,1024]{2,1,0:T(8,128)(2,1)} %fusion.21), calls=%async_computation.2 | async-start | bytes 524288 | tf_op jit(solution)/shard_map/all_to_all | solution.py:13
  62.0 2.6 slice_bitcast_fusion.10
  64.6 1.3 collective-permute-start
  65.9 1.6 collective-permute-start.1
  67.5 6.3 %all-to-all-done.2 = bf16[16,8,1024]{2,1,0:T(8,128)(2,1)S(1)} async-done(((bf16[16,8,1024]{2,1,0:T(8,128)(2,1)}), bf16[16,8,1024]{2,1,0:T(8,128)(2,1)S(1)}, u32[]{:S(2)}, u32[]{:S(2)}) %all-to-all-start.2) | async-done | bytes 262176 | tf_op jit(solution)/shard_map/all_to_all | solution.py:13
  73.8 1.7 bitcast_dynamic-update-slice_fusion.4
  75.5 29.4 %collective-permute-done = bf16[352,1024]{1,0:T(8,128)(2,1)S(1)} collective-permute-done((bf16[352,1024]{1,0:T(8,128)(2,1)}, bf16[352,1024]{1,0:T(8,128)(2,1)S(1)}, u32[]{:S(2)}, u32[]{:S(2)}) %collective-permute-start) | collective-permute-done | bytes 720928 | tf_op jit(solution)/shard_map/ppermute | solution.py:36
  104.9 2.1 bitcast_select_fusion
  107.3 4.0 %gather_fusion.1 = bf16[160,4,1024]{2,1,0:T(4,128)(2,1)S(1)} fusion(bf16[544,4,1024]{2,1,0:T(4,128)(2,1)} %all-gather.4.cloned.1.call-done, s32[1024]{0:T(1024)S(1)} %pad_clamp_fusion), kind=kCustom, calls=%fused_computation.1 | custom fusion | bytes 2622080 | tf_op jit(solution)/shard_map/gather | solution.py:60
  111.5 1.2 pad_maximum_fusion.4
  112.7 49.1 %all_to_all.46 = bf16[32,7,4,1024]{3,2,1,0:T(4,128)(2,1)S(1)} all-to-all(bf16[32,7,4,1024]{3,2,1,0:T(4,128)(2,1)S(1)} %pad_maximum_fusion.4), channel_id=1, replica_groups=mesh['x'=4,'z'=8,'y'=8,'core'=2] {'x','z'}, dimensions={0} | all-to-all | bytes 3670016 | tf_op jit(solution)/shard_map/all_to_all | solution.py:13
  161.8 1.2 copy-done.1
  164.6 2.5 fusion.15
  167.1 2.1 collective-permute-start.2
  169.2 1.5 collective-permute-done.2
  171.5 20.7 %all-to-all-start.4 = ((bf16[8,16,1024]{2,1,0:T(8,128)(2,1)}), bf16[8,16,1024]{2,1,0:T(8,128)(2,1)}, u32[]{:S(2)}, u32[]{:S(2)}) async-start(bf16[8,16,1024]{2,1,0:T(8,128)(2,1)} %fusion.39), calls=%async_computation.4 | async-start | bytes 524288 | tf_op jit(solution)/shard_map/all_to_all | solution.py:13
  202.6 1.0 reshape.197
  203.6 1.1 reshape.198
  204.6 3.7 %fusion.12 = bf16[384,1024]{1,0:T(8,128)(2,1)} fusion(bf16[384,1024]{1,0:T(8,128)(2,1)} %reshape.198, bf16[1,1024,1024]{2,1,0:T(8,128)(2,1)} %param.6), kind=kOutput, calls=%fused_computation.19 | convolution fusion | flops 805699584 | bytes 3670016 | tf_op jit(solution)/shard_map/dot_general | solution.py:17
  208.4 1.0 convert_reduce_fusion
  210.7 1.4 slice_bitcast_fusion.9
  212.1 2.0 slice_bitcast_fusion.16
  214.1 2.4 bitcast_dynamic-update-slice_fusion.3
  217.4 4.8 %all-to-all-start.5 = ((bf16[32,8,1024]{2,1,0:T(8,128)(2,1)}), bf16[32,8,1024]{2,1,0:T(8,128)(2,1)}, u32[]{:S(2)}, u32[]{:S(2)}) async-start(bf16[32,8,1024]{2,1,0:T(8,128)(2,1)} %broadcast_in_dim.24), calls=%async_computation.5 | async-start | bytes 1048576 | tf_op jit(solution)/shard_map/all_to_all | solution.py:13
  222.1 1.1 slice_bitcast_fusion.15
  223.3 1.7 slice_bitcast_fusion.7
  225.0 1.7 convolution_add_fusion.12
  226.8 2.5 slice_bitcast_fusion.5
  229.3 8.6 %all-to-all-done.5 = bf16[32,8,1024]{2,1,0:T(8,128)(2,1)} async-done(((bf16[32,8,1024]{2,1,0:T(8,128)(2,1)}), bf16[32,8,1024]{2,1,0:T(8,128)(2,1)}, u32[]{:S(2)}, u32[]{:S(2)}) %all-to-all-start.5) | async-done | bytes 524320 | tf_op jit(solution)/shard_map/all_to_all | solution.py:13
  237.9 2.4 bitcast_dynamic-update-slice_fusion.2
  241.1 6.2 %all-to-all-start.6 = ((bf16[32,8,1024]{2,1,0:T(8,128)(2,1)}), bf16[32,8,1024]{2,1,0:T(8,128)(2,1)}, u32[]{:S(2)}, u32[]{:S(2)}) async-start(bf16[32,8,1024]{2,1,0:T(8,128)(2,1)} %broadcast_in_dim.25), calls=%async_computation.7 | async-start | bytes 1048576 | tf_op jit(solution)/shard_map/all_to_all | solution.py:13
  247.3 2.0 slice_bitcast_fusion.14
  249.2 17.6 %reduce-scatter.2.cloned.1.call-done = bf16[24,1024]{1,0:T(8,128)(2,1)} async-done(((bf16[384,1024]{1,0:T(8,128)(2,1)}), bf16[24,1024]{1,0:T(8,128)(2,1)}) %reduce-scatter.2.cloned.1.call-update) | async-done | bytes 49168 | tf_op jit(solution)/shard_map/reduce_scatter | solution.py:81
  266.8 1.5 reshape.207
  268.3 1.4 fusion.128
  269.7 1.4 unstack.35
  271.1 2.1 convolution_add_fusion.10
  273.3 1.7 convolution_add_fusion.9
  275.0 2.5 slice_bitcast_fusion.3
  277.5 2.4 bitcast_dynamic-update-slice_fusion.1
  280.7 9.5 %all-to-all-start.7 = ((bf16[32,8,1024]{2,1,0:T(8,128)(2,1)}), bf16[32,8,1024]{2,1,0:T(8,128)(2,1)}, u32[]{:S(2)}, u32[]{:S(2)}) async-start(bf16[32,8,1024]{2,1,0:T(8,128)(2,1)} %broadcast_in_dim.48), calls=%async_computation.8 | async-start | bytes 1048576 | tf_op jit(solution)/shard_map/all_to_all | solution.py:13
  290.2 2.0 slice_bitcast_fusion.13
  292.2 1.4 unstack.39
  293.6 1.4 unstack.37
  295.0 2.1 convolution_add_fusion.7
  297.1 1.2 convolution_add_fusion.6
  298.7 1.7 convolution_add_fusion.5
  300.4 2.6 slice_bitcast_fusion.1
  302.9 3.4 all-to-all-done.7
  306.3 2.4 bitcast_dynamic-update-slice_fusion
  309.6 5.9 %all-to-all-start.8 = ((bf16[32,8,1024]{2,1,0:T(8,128)(2,1)}), bf16[32,8,1024]{2,1,0:T(8,128)(2,1)}, u32[]{:S(2)}, u32[]{:S(2)}) async-start(bf16[32,8,1024]{2,1,0:T(8,128)(2,1)} %broadcast_in_dim.49), calls=%async_computation.9 | async-start | bytes 1048576 | tf_op jit(solution)/shard_map/all_to_all | solution.py:13
  315.5 1.1 slice_bitcast_fusion.12
  316.7 1.9 fusion.29
  318.6 1.2 convolution_add_fusion.3
  320.2 1.2 convolution_add_fusion.2
  321.7 1.7 convolution_add_fusion.1
  323.4 9.2 %all-to-all-done.8 = bf16[32,8,1024]{2,1,0:T(8,128)(2,1)} async-done(((bf16[32,8,1024]{2,1,0:T(8,128)(2,1)}), bf16[32,8,1024]{2,1,0:T(8,128)(2,1)}, u32[]{:S(2)}, u32[]{:S(2)}) %all-to-all-start.8) | async-done | bytes 524320 | tf_op jit(solution)/shard_map/all_to_all | solution.py:13
  332.6 2.4 fusion.38
  (91 shorter events, 13.4 us)
Async XLA Ops:
  6.5 67.3 %copy-start = (bf16[1024,1024]{1,0:T(8,128)(2,1)S(1)}, bf16[1024,1024]{1,0:T(8,128)(2,1)}, u32[]{:S(2)}) copy-start(bf16[1024,1024]{1,0:T(8,128)(2,1)} %param.7) | copy-start | bytes 6291460
  8.4 23.8 %all-to-all-start = ((bf16[32,4,1024]{2,1,0:T(4,128)(2,1)}), bf16[32,4,1024]{2,1,0:T(4,128)(2,1)S(1)}, u32[]{:S(2)}, u32[]{:S(2)}) async-start(bf16[32,4,1024]{2,1,0:T(4,128)(2,1)} %reshape_squeeze.3), calls=%async_computation | async-start | bytes 524288 | tf_op jit(solution)/shard_map/all_to_all | solution.py:13
  20.5 86.8 %all-gather.4.cloned.1.call-start = ((), (), s32[]{:S(2)}) async-start(), calls=%async_computation.10 | async-start | bytes 4734976 | tf_op jit(solution)/shard_map/all_gather | solution.py:31
  52.1 21.7 %all-to-all-start.2 = ((bf16[16,8,1024]{2,1,0:T(8,128)(2,1)}), bf16[16,8,1024]{2,1,0:T(8,128)(2,1)S(1)}, u32[]{:S(2)}, u32[]{:S(2)}) async-start(bf16[16,8,1024]{2,1,0:T(8,128)(2,1)} %fusion.21), calls=%async_computation.2 | async-start | bytes 524288 | tf_op jit(solution)/shard_map/all_to_all | solution.py:13
  62.0 148.7 %all-gather.6.cloned.1.call-start = ((), (), s32[]{:S(2)}) async-start(), calls=%async_computation.12 | async-start | bytes 12255232 | tf_op jit(solution)/shard_map/all_gather | solution.py:51
  64.6 40.3 %collective-permute-start = (bf16[352,1024]{1,0:T(8,128)(2,1)}, bf16[352,1024]{1,0:T(8,128)(2,1)S(1)}, u32[]{:S(2)}, u32[]{:S(2)}) collective-permute-start(bf16[352,1024]{1,0:T(8,128)(2,1)} %get-tuple-element.36), channel_id=1, source_target_pairs={{0,5},{1,6},{2,7},{3,8},{4,9},{16,21},{17,22},{18,23},{19,24},{20,... | collective-permute-start | bytes 2162696 | tf_op jit(solution)/shard_map/ppermute | solution.py:36
  65.9 39.0 %collective-permute-start.1 = (bf16[352,1024]{1,0:T(8,128)(2,1)}, bf16[352,1024]{1,0:T(8,128)(2,1)}, u32[]{:S(2)}, u32[]{:S(2)}) collective-permute-start(bf16[352,1024]{1,0:T(8,128)(2,1)} %get-tuple-element.35), channel_id=1, source_target_pairs={{0,10},{1,11},{2,12},{3,13},{4,14},{16,26},{17,27},{18,28},{19,29}... | collective-permute-start | bytes 2162696 | tf_op jit(solution)/shard_map/ppermute | solution.py:37
  75.5 31.5 %copy-start.24 = (s32[1,32]{1,0:T(1,128)S(1)}, s32[1,32]{1,0:T(1,128)}, u32[]{:S(2)}) copy-start(s32[1,32]{1,0:T(1,128)} %param.9) | copy-start | bytes 388
  161.8 1.3 copy-start.1
  167.1 36.4 %slice-start = ((bf16[32,7,4,1024]{3,2,1,0:T(4,128)(2,1)}), bf16[32,3,4,1024]{3,2,1,0:T(4,128)(2,1)S(1)}, s32[]{:S(2)}) async-start(bf16[32,7,4,1024]{3,2,1,0:T(4,128)(2,1)} %copy-done.1), calls=%async_computation.13 | async-start | bytes 1572864 | tf_op jit(solution)/shard_map/slice | solution.py:68
  167.1 3.6 %collective-permute-start.2 = (bf16[8,16,1024]{2,1,0:T(8,128)(2,1)S(1)}, bf16[8,16,1024]{2,1,0:T(8,128)(2,1)S(1)}, u32[]{:S(2)}, u32[]{:S(2)}) collective-permute-start(bf16[8,16,1024]{2,1,0:T(8,128)(2,1)S(1)} %fusion.40), channel_id=1, source_target_pairs={{0,1},{1,0},{2,3},{3,2},{4,5},{5,4},{6,7},{7,6},{8,9},{9,8},{10,11... | collective-permute-start | bytes 786440 | tf_op jit(solution)/shard_map/ppermute | solution.py:76
  171.5 36.9 %all-to-all-start.4 = ((bf16[8,16,1024]{2,1,0:T(8,128)(2,1)}), bf16[8,16,1024]{2,1,0:T(8,128)(2,1)}, u32[]{:S(2)}, u32[]{:S(2)}) async-start(bf16[8,16,1024]{2,1,0:T(8,128)(2,1)} %fusion.39), calls=%async_computation.4 | async-start | bytes 524288 | tf_op jit(solution)/shard_map/all_to_all | solution.py:13
  192.2 74.6 %reduce-scatter.2.cloned.1.call-start = ((), (), s32[]{:S(2)}) async-start(), calls=%async_computation.11 | async-start | bytes 835584 | tf_op jit(solution)/shard_map/reduce_scatter | solution.py:81
  217.4 20.5 %all-to-all-start.5 = ((bf16[32,8,1024]{2,1,0:T(8,128)(2,1)}), bf16[32,8,1024]{2,1,0:T(8,128)(2,1)}, u32[]{:S(2)}, u32[]{:S(2)}) async-start(bf16[32,8,1024]{2,1,0:T(8,128)(2,1)} %broadcast_in_dim.24), calls=%async_computation.5 | async-start | bytes 1048576 | tf_op jit(solution)/shard_map/all_to_all | solution.py:13
  222.1 2.9 copy-start.23
  223.3 3.5 %copy-start.16 = (bf16[320,1024]{1,0:T(8,128)(2,1)}, bf16[320,1024]{1,0:T(8,128)(2,1)S(1)}, u32[]{:S(2)}) copy-start(bf16[320,1024]{1,0:T(8,128)(2,1)S(1)} %slice_bitcast_fusion.15) | copy-start | bytes 1966084
  225.0 1.8 copy-start.2
  225.0 1.8 copy-start.6
  241.1 36.4 %all-to-all-start.6 = ((bf16[32,8,1024]{2,1,0:T(8,128)(2,1)}), bf16[32,8,1024]{2,1,0:T(8,128)(2,1)}, u32[]{:S(2)}, u32[]{:S(2)}) async-start(bf16[32,8,1024]{2,1,0:T(8,128)(2,1)} %broadcast_in_dim.25), calls=%async_computation.7 | async-start | bytes 1048576 | tf_op jit(solution)/shard_map/all_to_all | solution.py:13
  271.1 2.1 copy-start.3
  271.1 2.1 copy-start.7
  271.1 2.2 copy-start.17
  280.7 25.6 %all-to-all-start.7 = ((bf16[32,8,1024]{2,1,0:T(8,128)(2,1)}), bf16[32,8,1024]{2,1,0:T(8,128)(2,1)}, u32[]{:S(2)}, u32[]{:S(2)}) async-start(bf16[32,8,1024]{2,1,0:T(8,128)(2,1)} %broadcast_in_dim.48), calls=%async_computation.8 | async-start | bytes 1048576 | tf_op jit(solution)/shard_map/all_to_all | solution.py:13
  294.9 2.1 copy-start.10
  294.9 2.1 copy-start.12
  294.9 2.2 copy-start.20
  297.1 1.3 copy-start.4
  297.1 1.3 copy-start.8
  297.1 1.5 copy-start.18
  309.6 23.0 %all-to-all-start.8 = ((bf16[32,8,1024]{2,1,0:T(8,128)(2,1)}), bf16[32,8,1024]{2,1,0:T(8,128)(2,1)}, u32[]{:S(2)}, u32[]{:S(2)}) async-start(bf16[32,8,1024]{2,1,0:T(8,128)(2,1)} %broadcast_in_dim.49), calls=%async_computation.9 | async-start | bytes 1048576 | tf_op jit(solution)/shard_map/all_to_all | solution.py:13
  316.6 1.9 copy-start.14
  316.6 1.9 copy-start.15
  316.6 2.0 copy-start.22
  318.6 1.3 copy-start.11
  318.6 1.3 copy-start.13
  318.6 1.5 copy-start.21
  320.2 1.3 copy-start.5
  320.2 1.3 copy-start.9
  320.2 1.5 copy-start.19
Sparse Core Ops, SparseCore 0:
  33.3 50.9 all-gather.3
  107.2 81.5 all-gather.5
  208.5 58.2 reduce-scatter.1

commit v8 on v7

--- a/solution.py
+++ b/solution.py
@@ -62,13 +62,14 @@
     ahead = jnp.broadcast_to(results[0].reshape(1, held, piece, width), (patches, held, piece, width))
     routed = swap(jnp.concatenate([ahead, chosen], axis=1), PATCH)
     states = [routed[:, :held].reshape(patches, own, width)]
-    soon, late = held + 2, STEPS + 1
+    count = 3
+    soon, late = held + count, STEPS + 1
 
     def terms(rows_of, first, last):
         return dot(rows_of[:, first:last].reshape(-1, width), tile).astype(BF16)
 
-    def per_step(summed, count):
-        return list(summed.reshape(held, count, piece, width).transpose(1, 0, 2, 3).reshape(count, own, width))
+    def per_step(summed, steps):
+        return list(summed.reshape(held, steps, piece, width).transpose(1, 0, 2, 3).reshape(steps, own, width))
 
     near = terms(routed, held, soon).reshape(chips, 2, -1, width)
     kept = jnp.where(lower, near[:, 0], near[:, 1])
@@ -76,9 +77,7 @@
     got = lax.ppermute(sent, "core", [(0, 1), (1, 0)])
     both = (kept.astype(F32) + got.astype(F32)).astype(BF16)
     parts = swap(both, "y")
-    base = per_step(jnp.sum(parts.astype(F32), axis=0), 2)
-    after, _ = lax.optimization_barrier((routed, sent))
-    far = lax.psum_scatter(terms(after, soon, late), LAG, scatter_dimension=0, tiled=True)
+    base = per_step(jnp.sum(parts.astype(F32), axis=0), count)
 
     tiles = [tile_of(1, both)]
     for k in range(1, STEPS):
@@ -87,9 +86,13 @@
             state = lax.dynamic_index_in_dim(states[k - l], listed[l - 1], 0, keepdims=False)
             total = total + dot(state, tiles[l - 1])
         results.append(solve(k, total))
-        if k == 2:
+        if k == 1:
+            after, _ = lax.optimization_barrier((routed, results[k]))
+            far = terms(after, soon, late)
+            far = lax.psum_scatter(far, LAG, scatter_dimension=0, tiled=True)
+        if k == count:
             far, _ = lax.optimization_barrier((far, results[k]))
-            base += per_step(far.astype(F32), back - 2)
+            base += per_step(far.astype(F32), back - count)
         if k + 1 < STEPS:
             tiles.append(tile_of(k + 1, results[k - 1]))
             copies = jnp.broadcast_to(results[k][None], (patches, own, width))

time: 344 us -> 339 us (0.985)
  the two profiles are of different devices: /device:TPU:89 before, /device:TPU:88 now
where the time goes in v8:
time: 339 us; the launch traced here: 337 us
  starting transfers between devices  81.4 us (24%)
  waiting for transfers between devices  74.1 us (22%)
  blocking collectives  70.9 us (21%)
  local copies, waits for them, and re-layouts  43.7 us (13%)
  matrix products  34.9 us (10%)
  between operations  23.4 us (7%)
  other arithmetic  8.27 us (2%)
    all_to_all x2, blocking collectives, swap(): return lax.all_to_all(value, axes, split_axis=0, concat_axis=0, tiled=True)  70.9 us
    all_to_all x7, starting transfers between devices, swap(): return lax.all_to_all(value, axes, split_axis=0, concat_axis=0, tiled=True)  70.3 us
    all_to_all x7, waiting for transfers between devices, swap(): return lax.all_to_all(value, axes, split_axis=0, concat_axis=0, tiled=True)  54.7 us
    dot_general x19, matrix products, dot(): return jnp.dot(a, b, preferred_element_type=F32)  34.9 us
    ppermute x1, waiting for transfers between devices, on_device(): lax.ppermute(tile[third:2 * third], LAG, [(i, i + back) for i in range(ba...  15.4 us
    squeeze x5, local copies, waits for them, and re-layouts, tile_of(): return jnp.concatenate([ready[l - 1], ready[l - 1 + back], last])  11.4 us
    slice x5, local copies, waits for them, and re-layouts, tile_of(): last = ready[l - 1 + 2 * back][3 * third - width:]  9.59 us
    ppermute x1, starting transfers between devices, on_device(): got = lax.ppermute(sent, 'core', [(0, 1), (1, 0)])  9.01 us
  transfers between devices with their start and end apart: 13, of which 9 were waited for; matrix products, arithmetic and copies ran while one was open for 18% of the time, Pallas kernels for 0%

profile of v8, /device:TPU:88, one launch (start us, length us, event | category | flops | bytes accessed | tf_op | source)
XLA Modules:
  0.0 336.6 jit_solution(17143448577234819754)
XLA Ops:
  6.5 1.9 reshape_squeeze.3
  8.5 12.6 %all-to-all-start = ((bf16[32,4,1024]{2,1,0:T(4,128)(2,1)}), bf16[32,4,1024]{2,1,0:T(4,128)(2,1)S(1)}, u32[]{:S(2)}, u32[]{:S(2)}) async-start(bf16[32,4,1024]{2,1,0:T(4,128)(2,1)} %reshape_squeeze.3), calls=%async_computation | async-start | bytes 524288 | tf_op jit(solution)/shard_map/all_to_all | solution.py:13
  21.1 1.2 fusion.130
  23.1 10.2 %all-to-all-done = bf16[32,4,1024]{2,1,0:T(4,128)(2,1)S(1)} async-done(((bf16[32,4,1024]{2,1,0:T(4,128)(2,1)}), bf16[32,4,1024]{2,1,0:T(4,128)(2,1)S(1)}, u32[]{:S(2)}, u32[]{:S(2)}) %all-to-all-start) | async-done | bytes 262176 | tf_op jit(solution)/shard_map/all_to_all | solution.py:13
  33.3 0.9 maximum_maximum_fusion
  34.9 0.8 gather_fusion
  35.7 15.8 %all_to_all.45 = bf16[32,4,1024]{2,1,0:T(4,128)(2,1)S(1)} all-to-all(bf16[32,4,1024]{2,1,0:T(4,128)(2,1)S(1)} %gather_fusion), channel_id=1, replica_groups=mesh['x'=4,'z'=8,'y'=8,'core'=2] {'x','z'}, dimensions={0} | all-to-all | bytes 524288 | tf_op jit(solution)/shard_map/all_to_all | solution.py:13
  51.6 2.8 fusion.21
  54.4 7.4 %all-to-all-start.2 = ((bf16[16,8,1024]{2,1,0:T(8,128)(2,1)}), bf16[16,8,1024]{2,1,0:T(8,128)(2,1)S(1)}, u32[]{:S(2)}, u32[]{:S(2)}) async-start(bf16[16,8,1024]{2,1,0:T(8,128)(2,1)} %fusion.21), calls=%async_computation.2 | async-start | bytes 524288 | tf_op jit(solution)/shard_map/all_to_all | solution.py:13
  61.9 2.6 slice_bitcast_fusion.10
  65.2 1.3 collective-permute-start
  66.5 6.8 %all-to-all-done.2 = bf16[16,8,1024]{2,1,0:T(8,128)(2,1)S(1)} async-done(((bf16[16,8,1024]{2,1,0:T(8,128)(2,1)}), bf16[16,8,1024]{2,1,0:T(8,128)(2,1)S(1)}, u32[]{:S(2)}, u32[]{:S(2)}) %all-to-all-start.2) | async-done | bytes 262176 | tf_op jit(solution)/shard_map/all_to_all | solution.py:13
  73.4 1.0 bitcast_dynamic-update-slice_fusion.4
  74.4 15.4 %collective-permute-done = bf16[352,1024]{1,0:T(8,128)(2,1)} collective-permute-done((bf16[352,1024]{1,0:T(8,128)(2,1)}, bf16[352,1024]{1,0:T(8,128)(2,1)}, u32[]{:S(2)}, u32[]{:S(2)}) %collective-permute-start) | collective-permute-done | bytes 720928 | tf_op jit(solution)/shard_map/ppermute | solution.py:36
  89.7 2.3 bitcast_select_fusion.1
  92.3 4.0 %gather_fusion.1 = bf16[160,4,1024]{2,1,0:T(4,128)(2,1)S(1)} fusion(bf16[544,4,1024]{2,1,0:T(4,128)(2,1)} %all-gather.4.cloned.1.call-done, s32[1024]{0:T(1024)S(1)} %pad_clamp_fusion), kind=kCustom, calls=%fused_computation.1 | custom fusion | bytes 2622080 | tf_op jit(solution)/shard_map/gather | solution.py:60
  96.6 1.2 pad_maximum_fusion.4
  97.8 55.0 %all_to_all.46 = bf16[32,7,4,1024]{3,2,1,0:T(4,128)(2,1)S(1)} all-to-all(bf16[32,7,4,1024]{3,2,1,0:T(4,128)(2,1)S(1)} %pad_maximum_fusion.4), channel_id=1, replica_groups=mesh['x'=4,'z'=8,'y'=8,'core'=2] {'x','z'}, dimensions={0} | all-to-all | bytes 3670016 | tf_op jit(solution)/shard_map/all_to_all | solution.py:13
  152.8 1.2 copy-done.1
  154.3 1.1 reshape.194
  155.4 2.8 fusion.12
  158.3 9.0 %collective-permute-start.2 = (bf16[8,24,1024]{2,1,0:T(8,128)(2,1)S(1)}, bf16[8,24,1024]{2,1,0:T(8,128)(2,1)S(1)}, u32[]{:S(2)}, u32[]{:S(2)}) collective-permute-start(bf16[8,24,1024]{2,1,0:T(8,128)(2,1)S(1)} %fusion.40), channel_id=1, source_target_pairs={{0,1},{1,0},{2,3},{3,2},{4,5},{5,4},{6,7},{7,6},{8,9},{9,8},{10,11... | collective-permute-start | bytes 1179656 | tf_op jit(solution)/shard_map/ppermute | solution.py:77
  167.3 1.4 collective-permute-done.2
  168.7 1.0 fusion.39
  169.7 23.1 %all-to-all-start.4 = ((bf16[8,24,1024]{2,1,0:T(8,128)(2,1)}), bf16[8,24,1024]{2,1,0:T(8,128)(2,1)S(1)}, u32[]{:S(2)}, u32[]{:S(2)}) async-start(bf16[8,24,1024]{2,1,0:T(8,128)(2,1)} %fusion.39), calls=%async_computation.4 | async-start | bytes 786432 | tf_op jit(solution)/shard_map/all_to_all | solution.py:13
  203.9 0.9 reshape.197
  205.0 2.0 slice_bitcast_fusion.16
  207.0 2.3 slice_bitcast_fusion.9
  209.4 2.7 bitcast_dynamic-update-slice_fusion.3
  212.0 0.9 reshape.198
  213.0 3.3 fusion.15
  216.3 0.9 broadcast_in_dim.24
  217.1 5.5 %all-to-all-start.5 = ((bf16[32,8,1024]{2,1,0:T(8,128)(2,1)}), bf16[32,8,1024]{2,1,0:T(8,128)(2,1)S(1)}, u32[]{:S(2)}, u32[]{:S(2)}) async-start(bf16[32,8,1024]{2,1,0:T(8,128)(2,1)} %broadcast_in_dim.24), calls=%async_computation.5 | async-start | bytes 1048576 | tf_op jit(solution)/shard_map/all_to_all | solution.py:13
  222.6 1.4 slice_bitcast_fusion.7
  224.1 1.6 slice_bitcast_fusion.15
  225.7 1.2 convolution_add_fusion.12
  226.9 2.0 slice_bitcast_fusion.14
  228.9 2.6 slice_bitcast_fusion.5
  231.4 8.5 %all-to-all-done.5 = bf16[32,8,1024]{2,1,0:T(8,128)(2,1)S(1)} async-done(((bf16[32,8,1024]{2,1,0:T(8,128)(2,1)}), bf16[32,8,1024]{2,1,0:T(8,128)(2,1)S(1)}, u32[]{:S(2)}, u32[]{:S(2)}) %all-to-all-start.5) | async-done | bytes 524320 | tf_op jit(solution)/shard_map/all_to_all | solution.py:13
  240.0 2.6 bitcast_dynamic-update-slice_fusion.2
  242.6 0.9 broadcast_in_dim.25
  243.4 4.9 %all-to-all-start.6 = ((bf16[32,8,1024]{2,1,0:T(8,128)(2,1)}), bf16[32,8,1024]{2,1,0:T(8,128)(2,1)}, u32[]{:S(2)}, u32[]{:S(2)}) async-start(bf16[32,8,1024]{2,1,0:T(8,128)(2,1)} %broadcast_in_dim.25), calls=%async_computation.6 | async-start | bytes 1048576 | tf_op jit(solution)/shard_map/all_to_all | solution.py:13
  248.4 2.1 convolution_add_fusion.10
  250.9 2.0 slice_bitcast_fusion.13
  252.9 2.5 slice_bitcast_fusion.3
  255.4 9.9 %all-to-all-done.6 = bf16[32,8,1024]{2,1,0:T(8,128)(2,1)} async-done(((bf16[32,8,1024]{2,1,0:T(8,128)(2,1)}), bf16[32,8,1024]{2,1,0:T(8,128)(2,1)}, u32[]{:S(2)}, u32[]{:S(2)}) %all-to-all-start.6) | async-done | bytes 524320 | tf_op jit(solution)/shard_map/all_to_all | solution.py:13
  265.3 2.6 bitcast_dynamic-update-slice_fusion.1
  267.9 2.6 reduce-scatter.2.cloned.1.call-done
  270.5 0.8 reshape.207
  271.3 0.9 broadcast_in_dim.48
  272.1 10.2 %all-to-all-start.7 = ((bf16[32,8,1024]{2,1,0:T(8,128)(2,1)}), bf16[32,8,1024]{2,1,0:T(8,128)(2,1)}, u32[]{:S(2)}, u32[]{:S(2)}) async-start(bf16[32,8,1024]{2,1,0:T(8,128)(2,1)} %broadcast_in_dim.48), calls=%async_computation.8 | async-start | bytes 1048576 | tf_op jit(solution)/shard_map/all_to_all | solution.py:13
  282.4 2.1 convolution_add_fusion.7
  286.1 1.1 convolution_add_fusion.5
  287.2 2.6 slice_bitcast_fusion.1
  289.7 9.2 %all-to-all-done.7 = bf16[32,8,1024]{2,1,0:T(8,128)(2,1)} async-done(((bf16[32,8,1024]{2,1,0:T(8,128)(2,1)}), bf16[32,8,1024]{2,1,0:T(8,128)(2,1)}, u32[]{:S(2)}, u32[]{:S(2)}) %all-to-all-start.7) | async-done | bytes 524320 | tf_op jit(solution)/shard_map/all_to_all | solution.py:13
  299.0 2.6 bitcast_dynamic-update-slice_fusion
  301.6 0.9 broadcast_in_dim.49
  302.4 6.7 %all-to-all-start.8 = ((bf16[32,8,1024]{2,1,0:T(8,128)(2,1)}), bf16[32,8,1024]{2,1,0:T(8,128)(2,1)}, u32[]{:S(2)}, u32[]{:S(2)}) async-start(bf16[32,8,1024]{2,1,0:T(8,128)(2,1)} %broadcast_in_dim.49), calls=%async_computation.9 | async-start | bytes 1048576 | tf_op jit(solution)/shard_map/all_to_all | solution.py:13
  309.1 2.0 slice_bitcast_fusion.12
  311.2 2.1 fusion.29
  314.8 1.2 convolution_add_fusion.2
  316.4 1.1 convolution_add_fusion.1
  317.5 10.0 %all-to-all-done.8 = bf16[32,8,1024]{2,1,0:T(8,128)(2,1)} async-done(((bf16[32,8,1024]{2,1,0:T(8,128)(2,1)}), bf16[32,8,1024]{2,1,0:T(8,128)(2,1)}, u32[]{:S(2)}, u32[]{:S(2)}) %all-to-all-start.8) | async-done | bytes 524320 | tf_op jit(solution)/shard_map/all_to_all | solution.py:13
  327.5 2.6 fusion.38
  (93 shorter events, 8.7 us)
Async XLA Ops:
  6.5 66.8 %copy-start = (bf16[1024,1024]{1,0:T(8,128)(2,1)S(1)}, bf16[1024,1024]{1,0:T(8,128)(2,1)}, u32[]{:S(2)}) copy-start(bf16[1024,1024]{1,0:T(8,128)(2,1)} %param.7) | copy-start | bytes 6291460
  8.5 24.9 %all-to-all-start = ((bf16[32,4,1024]{2,1,0:T(4,128)(2,1)}), bf16[32,4,1024]{2,1,0:T(4,128)(2,1)S(1)}, u32[]{:S(2)}, u32[]{:S(2)}) async-start(bf16[32,4,1024]{2,1,0:T(4,128)(2,1)} %reshape_squeeze.3), calls=%async_computation | async-start | bytes 524288 | tf_op jit(solution)/shard_map/all_to_all | solution.py:13
  21.0 71.3 %all-gather.4.cloned.1.call-start = ((), (), s32[]{:S(2)}) async-start(), calls=%async_computation.10 | async-start | bytes 4734976 | tf_op jit(solution)/shard_map/all_gather | solution.py:31
  54.4 18.9 %copy-start.23 = (bf16[6,8,1024]{2,1,0:T(8,128)(2,1)S(1)}, bf16[6,8,1024]{2,1,0:T(8,128)(2,1)}, u32[]{:S(2)}) copy-start(bf16[6,8,1024]{2,1,0:T(8,128)(2,1)} %param.8) | copy-start | bytes 294916
  54.4 18.9 %all-to-all-start.2 = ((bf16[16,8,1024]{2,1,0:T(8,128)(2,1)}), bf16[16,8,1024]{2,1,0:T(8,128)(2,1)S(1)}, u32[]{:S(2)}, u32[]{:S(2)}) async-start(bf16[16,8,1024]{2,1,0:T(8,128)(2,1)} %fusion.21), calls=%async_computation.2 | async-start | bytes 524288 | tf_op jit(solution)/shard_map/all_to_all | solution.py:13
  61.9 143.2 %all-gather.6.cloned.1.call-start = ((), (), s32[]{:S(2)}) async-start(), calls=%async_computation.12 | async-start | bytes 12255232 | tf_op jit(solution)/shard_map/all_gather | solution.py:51
  64.5 9.9 %collective-permute-start.1 = (bf16[352,1024]{1,0:T(8,128)(2,1)}, bf16[352,1024]{1,0:T(8,128)(2,1)S(1)}, u32[]{:S(2)}, u32[]{:S(2)}) collective-permute-start(bf16[352,1024]{1,0:T(8,128)(2,1)} %get-tuple-element.35), channel_id=1, source_target_pairs={{0,10},{1,11},{2,12},{3,13},{4,14},{16,26},{17,27},{18,28},{19,29}... | collective-permute-start | bytes 2162696 | tf_op jit(solution)/shard_map/ppermute | solution.py:37
  65.2 24.6 %collective-permute-start = (bf16[352,1024]{1,0:T(8,128)(2,1)}, bf16[352,1024]{1,0:T(8,128)(2,1)}, u32[]{:S(2)}, u32[]{:S(2)}) collective-permute-start(bf16[352,1024]{1,0:T(8,128)(2,1)} %get-tuple-element.36), channel_id=1, source_target_pairs={{0,5},{1,6},{2,7},{3,8},{4,9},{16,21},{17,22},{18,23},{19,24},{20,... | collective-permute-start | bytes 2162696 | tf_op jit(solution)/shard_map/ppermute | solution.py:36
  74.4 17.7 %copy-start.24 = (s32[1,32]{1,0:T(1,128)S(1)}, s32[1,32]{1,0:T(1,128)}, u32[]{:S(2)}) copy-start(s32[1,32]{1,0:T(1,128)} %param.9) | copy-start | bytes 388
  152.8 1.3 copy-start.1
  158.2 45.7 %slice-start = ((bf16[32,7,4,1024]{3,2,1,0:T(4,128)(2,1)}), bf16[32,2,4,1024]{3,2,1,0:T(4,128)(2,1)S(1)}, s32[]{:S(2)}) async-start(bf16[32,7,4,1024]{3,2,1,0:T(4,128)(2,1)} %copy-done.1), calls=%async_computation.13 | async-start | bytes 1048576 | tf_op jit(solution)/shard_map/slice | solution.py:64
  158.3 10.4 %collective-permute-start.2 = (bf16[8,24,1024]{2,1,0:T(8,128)(2,1)S(1)}, bf16[8,24,1024]{2,1,0:T(8,128)(2,1)S(1)}, u32[]{:S(2)}, u32[]{:S(2)}) collective-permute-start(bf16[8,24,1024]{2,1,0:T(8,128)(2,1)S(1)} %fusion.40), channel_id=1, source_target_pairs={{0,1},{1,0},{2,3},{3,2},{4,5},{5,4},{6,7},{7,6},{8,9},{9,8},{10,11... | collective-permute-start | bytes 1179656 | tf_op jit(solution)/shard_map/ppermute | solution.py:77
  169.7 35.2 %all-to-all-start.4 = ((bf16[8,24,1024]{2,1,0:T(8,128)(2,1)}), bf16[8,24,1024]{2,1,0:T(8,128)(2,1)S(1)}, u32[]{:S(2)}, u32[]{:S(2)}) async-start(bf16[8,24,1024]{2,1,0:T(8,128)(2,1)} %fusion.39), calls=%async_computation.4 | async-start | bytes 786432 | tf_op jit(solution)/shard_map/all_to_all | solution.py:13
  192.7 77.8 %reduce-scatter.2.cloned.1.call-start = ((), (), s32[]{:S(2)}) async-start(), calls=%async_computation.11 | async-start | bytes 557056 | tf_op jit(solution)/shard_map/reduce_scatter | solution.py:92
  209.4 2.7 slice-start.1
  217.1 22.9 %all-to-all-start.5 = ((bf16[32,8,1024]{2,1,0:T(8,128)(2,1)}), bf16[32,8,1024]{2,1,0:T(8,128)(2,1)S(1)}, u32[]{:S(2)}, u32[]{:S(2)}) async-start(bf16[32,8,1024]{2,1,0:T(8,128)(2,1)} %broadcast_in_dim.24), calls=%async_computation.5 | async-start | bytes 1048576 | tf_op jit(solution)/shard_map/all_to_all | solution.py:13
  224.1 2.8 copy-start.2
  224.1 2.8 copy-start.6
  225.7 1.2 copy-start.16
  243.4 21.9 %all-to-all-start.6 = ((bf16[32,8,1024]{2,1,0:T(8,128)(2,1)}), bf16[32,8,1024]{2,1,0:T(8,128)(2,1)}, u32[]{:S(2)}, u32[]{:S(2)}) async-start(bf16[32,8,1024]{2,1,0:T(8,128)(2,1)} %broadcast_in_dim.25), calls=%async_computation.6 | async-start | bytes 1048576 | tf_op jit(solution)/shard_map/all_to_all | solution.py:13
  248.3 2.1 copy-start.3
  248.3 2.1 copy-start.7
  248.4 2.2 copy-start.17
  272.1 26.8 %all-to-all-start.7 = ((bf16[32,8,1024]{2,1,0:T(8,128)(2,1)}), bf16[32,8,1024]{2,1,0:T(8,128)(2,1)}, u32[]{:S(2)}, u32[]{:S(2)}) async-start(bf16[32,8,1024]{2,1,0:T(8,128)(2,1)} %broadcast_in_dim.48), calls=%async_computation.8 | async-start | bytes 1048576 | tf_op jit(solution)/shard_map/all_to_all | solution.py:13
  282.4 2.1 copy-start.10
  282.4 2.1 copy-start.12
  282.4 2.2 copy-start.20
  284.5 1.1 copy-start.4
  284.5 1.3 copy-start.8
  284.5 1.5 copy-start.18
  302.4 25.0 %all-to-all-start.8 = ((bf16[32,8,1024]{2,1,0:T(8,128)(2,1)}), bf16[32,8,1024]{2,1,0:T(8,128)(2,1)}, u32[]{:S(2)}, u32[]{:S(2)}) async-start(bf16[32,8,1024]{2,1,0:T(8,128)(2,1)} %broadcast_in_dim.49), calls=%async_computation.9 | async-start | bytes 1048576 | tf_op jit(solution)/shard_map/all_to_all | solution.py:13
  311.1 2.1 copy-start.14
  311.2 2.1 copy-start.15
  311.2 2.2 copy-start.22
  313.3 1.1 copy-start.11
  313.3 1.3 copy-start.13
  313.3 1.5 copy-start.21
  314.8 1.3 copy-start.5
  314.8 1.3 copy-start.9
  314.8 1.5 copy-start.19
Sparse Core Ops, SparseCore 0:
  34.4 46.0 all-gather.3
  92.2 95.8 all-gather.5
  216.4 54.0 reduce-scatter.1

commit v9 on v8

--- a/solution.py
+++ b/solution.py
@@ -79,20 +79,22 @@
     parts = swap(both, "y")
     base = per_step(jnp.sum(parts.astype(F32), axis=0), count)
 
+    after, _ = lax.optimization_barrier((routed, both))
+    far = terms(after, soon, late)
+    far = lax.psum_scatter(far, LAG, scatter_dimension=0, tiled=True)
+
     tiles = [tile_of(1, both)]
     for k in range(1, STEPS):
-        total = base[k - 1]
-        for l in range(k, 0, -1):
+        def reached(l):
             state = lax.dynamic_index_in_dim(states[k - l], listed[l - 1], 0, keepdims=False)
-            total = total + dot(state, tiles[l - 1])
+            return dot(state, tiles[l - 1])
+
+        total = sum(reached(l) for l in range(k, 1, -1))
+        if k == count + 1:
+            far, _ = lax.optimization_barrier((far, total))
+            base += per_step(far.astype(F32), back - count)
+        total = base[k - 1] + total + reached(1)
         results.append(solve(k, total))
-        if k == 1:
-            after, _ = lax.optimization_barrier((routed, results[k]))
-            far = terms(after, soon, late)
-            far = lax.psum_scatter(far, LAG, scatter_dimension=0, tiled=True)
-        if k == count:
-            far, _ = lax.optimization_barrier((far, results[k]))
-            base += per_step(far.astype(F32), back - count)
         if k + 1 < STEPS:
             tiles.append(tile_of(k + 1, results[k - 1]))
             copies = jnp.broadcast_to(results[k][None], (patches, own, width))

time: 339 us -> 327 us (0.965)
  the two profiles are of different devices: /device:TPU:88 before, /device:TPU:64 now
where the time goes in v9:
time: 327 us; the launch traced here: 325 us
  waiting for transfers between devices  79.8 us (24%)
  blocking collectives  70.5 us (22%)
  starting transfers between devices  59.2 us (18%)
  local copies, waits for them, and re-layouts  45.7 us (14%)
  matrix products  38.6 us (12%)
  between operations  22.6 us (7%)
  other arithmetic  8.25 us (3%)
    all_to_all x2, blocking collectives, swap(): return lax.all_to_all(value, axes, split_axis=0, concat_axis=0, tiled=True)  70.5 us
    all_to_all x7, starting transfers between devices, swap(): return lax.all_to_all(value, axes, split_axis=0, concat_axis=0, tiled=True)  48.1 us
    all_to_all x7, waiting for transfers between devices, swap(): return lax.all_to_all(value, axes, split_axis=0, concat_axis=0, tiled=True)  42.7 us
    dot_general x19, matrix products, dot(): return jnp.dot(a, b, preferred_element_type=F32)  38.6 us
    ppermute x1, waiting for transfers between devices, on_device(): lax.ppermute(tile[width - third:], LAG, [(i, i + 2 * back) for i in range...  35.4 us
    squeeze x5, local copies, waits for them, and re-layouts, tile_of(): return jnp.concatenate([ready[l - 1], ready[l - 1 + back], last])  10.7 us
    slice x5, local copies, waits for them, and re-layouts, tile_of(): last = ready[l - 1 + 2 * back][3 * third - width:]  7.53 us
    ppermute x1, starting transfers between devices, on_device(): lax.ppermute(tile[width - third:], LAG, [(i, i + 2 * back) for i in range...  6.84 us
  transfers between devices with their start and end apart: 13, of which 9 were waited for; matrix products, arithmetic and copies ran while one was open for 25% of the time, Pallas kernels for 0%

profile of v9, /device:TPU:64, one launch (start us, length us, event | category | flops | bytes accessed | tf_op | source)
XLA Modules:
  0.0 324.8 jit_solution(8944038572507038756)
XLA Ops:
  6.5 1.9 reshape_squeeze.3
  8.5 12.6 %all-to-all-start = ((bf16[32,4,1024]{2,1,0:T(4,128)(2,1)}), bf16[32,4,1024]{2,1,0:T(4,128)(2,1)S(1)}, u32[]{:S(2)}, u32[]{:S(2)}) async-start(bf16[32,4,1024]{2,1,0:T(4,128)(2,1)} %reshape_squeeze.3), calls=%async_computation | async-start | bytes 524288 | tf_op jit(solution)/shard_map/all_to_all | solution.py:13
  21.1 1.2 fusion.132
  23.1 10.2 %all-to-all-done = bf16[32,4,1024]{2,1,0:T(4,128)(2,1)S(1)} async-done(((bf16[32,4,1024]{2,1,0:T(4,128)(2,1)}), bf16[32,4,1024]{2,1,0:T(4,128)(2,1)S(1)}, u32[]{:S(2)}, u32[]{:S(2)}) %all-to-all-start) | async-done | bytes 262176 | tf_op jit(solution)/shard_map/all_to_all | solution.py:13
  33.3 1.0 maximum_maximum_fusion
  35.7 15.8 %all_to_all.45 = bf16[32,4,1024]{2,1,0:T(4,128)(2,1)S(1)} all-to-all(bf16[32,4,1024]{2,1,0:T(4,128)(2,1)S(1)} %gather_fusion), channel_id=1, replica_groups=mesh['x'=4,'z'=8,'y'=8,'core'=2] {'x','z'}, dimensions={0} | all-to-all | bytes 524288 | tf_op jit(solution)/shard_map/all_to_all | solution.py:13
  51.7 2.7 fusion.21
  54.4 7.2 %all-to-all-start.2 = ((bf16[16,8,1024]{2,1,0:T(8,128)(2,1)}), bf16[16,8,1024]{2,1,0:T(8,128)(2,1)S(1)}, u32[]{:S(2)}, u32[]{:S(2)}) async-start(bf16[16,8,1024]{2,1,0:T(8,128)(2,1)} %fusion.21), calls=%async_computation.2 | async-start | bytes 524288 | tf_op jit(solution)/shard_map/all_to_all | solution.py:13
  61.7 2.6 slice_bitcast_fusion.10
  64.3 6.8 %collective-permute-start.1 = (bf16[352,1024]{1,0:T(8,128)(2,1)}, bf16[352,1024]{1,0:T(8,128)(2,1)S(1)}, u32[]{:S(2)}, u32[]{:S(2)}) collective-permute-start(bf16[352,1024]{1,0:T(8,128)(2,1)} %get-tuple-element.35), channel_id=1, source_target_pairs={{0,10},{1,11},{2,12},{3,13},{4,14},{16,26},{17,27},{18,28},{19,29}... | collective-permute-start | bytes 2162696 | tf_op jit(solution)/shard_map/ppermute | solution.py:37
  71.1 2.2 collective-permute-start
  73.3 2.7 all-to-all-done.2
  76.0 1.7 bitcast_dynamic-update-slice_fusion.4
  77.7 35.4 %collective-permute-done.1 = bf16[352,1024]{1,0:T(8,128)(2,1)S(1)} collective-permute-done((bf16[352,1024]{1,0:T(8,128)(2,1)}, bf16[352,1024]{1,0:T(8,128)(2,1)S(1)}, u32[]{:S(2)}, u32[]{:S(2)}) %collective-permute-start.1) | collective-permute-done | bytes 720928 | tf_op jit(solution)/shard_map/ppermute | solution.py:37
  113.1 2.3 bitcast_select_fusion.1
  115.7 4.0 %gather_fusion.1 = bf16[160,4,1024]{2,1,0:T(4,128)(2,1)S(1)} fusion(bf16[544,4,1024]{2,1,0:T(4,128)(2,1)} %all-gather.4.cloned.1.call-done, s32[1024]{0:T(1024)S(1)} %pad_clamp_fusion), kind=kCustom, calls=%fused_computation.1 | custom fusion | bytes 2622080 | tf_op jit(solution)/shard_map/gather | solution.py:60
  119.9 1.2 pad_maximum_fusion.4
  121.1 54.7 %all_to_all.46 = bf16[32,7,4,1024]{3,2,1,0:T(4,128)(2,1)S(1)} all-to-all(bf16[32,7,4,1024]{3,2,1,0:T(4,128)(2,1)S(1)} %pad_maximum_fusion.4), channel_id=1, replica_groups=mesh['x'=4,'z'=8,'y'=8,'core'=2] {'x','z'}, dimensions={0} | all-to-all | bytes 3670016 | tf_op jit(solution)/shard_map/all_to_all | solution.py:13
  175.8 1.3 copy-done.1
  177.4 1.1 reshape.194
  178.5 2.8 fusion.12
  181.4 2.1 collective-permute-start.2
  183.5 1.7 collective-permute-done.2
  185.1 0.9 fusion.39
  186.1 6.6 %all-to-all-start.4 = ((bf16[8,24,1024]{2,1,0:T(8,128)(2,1)}), bf16[8,24,1024]{2,1,0:T(8,128)(2,1)S(1)}, u32[]{:S(2)}, u32[]{:S(2)}) async-start(bf16[8,24,1024]{2,1,0:T(8,128)(2,1)} %fusion.39), calls=%async_computation.4 | async-start | bytes 786432 | tf_op jit(solution)/shard_map/all_to_all | solution.py:13
  203.0 0.9 reshape.197
  204.1 3.1 fusion.15
  209.7 2.0 slice_bitcast_fusion.16
  211.7 1.4 slice_bitcast_fusion.9
  213.2 2.4 bitcast_dynamic-update-slice_fusion.3
  216.4 5.4 %all-to-all-start.5 = ((bf16[32,8,1024]{2,1,0:T(8,128)(2,1)}), bf16[32,8,1024]{2,1,0:T(8,128)(2,1)}, u32[]{:S(2)}, u32[]{:S(2)}) async-start(bf16[32,8,1024]{2,1,0:T(8,128)(2,1)} %broadcast_in_dim.24), calls=%async_computation.5 | async-start | bytes 1048576 | tf_op jit(solution)/shard_map/all_to_all | solution.py:13
  221.8 1.1 slice_bitcast_fusion.15
  223.0 1.7 slice_bitcast_fusion.7
  224.7 1.7 convolution_add_fusion.10
  226.4 2.5 slice_bitcast_fusion.5
  229.0 10.7 %all-to-all-done.5 = bf16[32,8,1024]{2,1,0:T(8,128)(2,1)} async-done(((bf16[32,8,1024]{2,1,0:T(8,128)(2,1)}), bf16[32,8,1024]{2,1,0:T(8,128)(2,1)}, u32[]{:S(2)}, u32[]{:S(2)}) %all-to-all-start.5) | async-done | bytes 524320 | tf_op jit(solution)/shard_map/all_to_all | solution.py:13
  239.7 2.4 bitcast_dynamic-update-slice_fusion.2
  242.9 4.9 %all-to-all-start.6 = ((bf16[32,8,1024]{2,1,0:T(8,128)(2,1)}), bf16[32,8,1024]{2,1,0:T(8,128)(2,1)}, u32[]{:S(2)}, u32[]{:S(2)}) async-start(bf16[32,8,1024]{2,1,0:T(8,128)(2,1)} %broadcast_in_dim.25), calls=%async_computation.6 | async-start | bytes 1048576 | tf_op jit(solution)/shard_map/all_to_all | solution.py:13
  247.8 1.1 slice_bitcast_fusion.14
  249.8 1.7 fusion.70
  251.5 2.1 slice_bitcast_fusion.13
  253.7 2.6 slice_bitcast_fusion.3
  256.2 1.7 fusion.28
  258.0 6.8 %all-to-all-done.6 = bf16[32,8,1024]{2,1,0:T(8,128)(2,1)} async-done(((bf16[32,8,1024]{2,1,0:T(8,128)(2,1)}), bf16[32,8,1024]{2,1,0:T(8,128)(2,1)}, u32[]{:S(2)}, u32[]{:S(2)}) %all-to-all-start.6) | async-done | bytes 524320 | tf_op jit(solution)/shard_map/all_to_all | solution.py:13
  264.8 2.4 bitcast_dynamic-update-slice_fusion.1
  268.0 4.9 %all-to-all-start.7 = ((bf16[32,8,1024]{2,1,0:T(8,128)(2,1)}), bf16[32,8,1024]{2,1,0:T(8,128)(2,1)}, u32[]{:S(2)}, u32[]{:S(2)}) async-start(bf16[32,8,1024]{2,1,0:T(8,128)(2,1)} %broadcast_in_dim.48), calls=%async_computation.8 | async-start | bytes 1048576 | tf_op jit(solution)/shard_map/all_to_all | solution.py:13
  273.0 2.1 fusion.38
  275.1 1.2 convolution_add_fusion.6
  276.6 1.7 convolution_add_fusion.5
  278.3 1.4 reshape.207
  279.7 1.4 fusion.130
  281.1 1.4 unstack.39
  282.5 1.4 unstack.37
  283.9 2.5 slice_bitcast_fusion.1
  286.4 3.4 %all-to-all-done.7 = bf16[32,8,1024]{2,1,0:T(8,128)(2,1)} async-done(((bf16[32,8,1024]{2,1,0:T(8,128)(2,1)}), bf16[32,8,1024]{2,1,0:T(8,128)(2,1)}, u32[]{:S(2)}, u32[]{:S(2)}) %all-to-all-start.7) | async-done | bytes 524320 | tf_op jit(solution)/shard_map/all_to_all | solution.py:13
  289.8 2.4 bitcast_dynamic-update-slice_fusion
  293.1 6.5 %all-to-all-start.8 = ((bf16[32,8,1024]{2,1,0:T(8,128)(2,1)}), bf16[32,8,1024]{2,1,0:T(8,128)(2,1)}, u32[]{:S(2)}, u32[]{:S(2)}) async-start(bf16[32,8,1024]{2,1,0:T(8,128)(2,1)} %broadcast_in_dim.49), calls=%async_computation.9 | async-start | bytes 1048576 | tf_op jit(solution)/shard_map/all_to_all | solution.py:13
  299.5 1.1 slice_bitcast_fusion.12
  300.7 1.9 fusion
  302.7 1.2 convolution_add_fusion.3
  304.2 1.3 convolution_add_fusion.2
  305.7 1.7 fusion.25
  307.4 8.4 %all-to-all-done.8 = bf16[32,8,1024]{2,1,0:T(8,128)(2,1)} async-done(((bf16[32,8,1024]{2,1,0:T(8,128)(2,1)}), bf16[32,8,1024]{2,1,0:T(8,128)(2,1)}, u32[]{:S(2)}, u32[]{:S(2)}) %all-to-all-start.8) | async-done | bytes 524320 | tf_op jit(solution)/shard_map/all_to_all | solution.py:13
  315.9 2.4 fusion.37
  (99 shorter events, 12.5 us)
Async XLA Ops:
  6.5 69.5 %copy-start = (bf16[1024,1024]{1,0:T(8,128)(2,1)S(1)}, bf16[1024,1024]{1,0:T(8,128)(2,1)}, u32[]{:S(2)}) copy-start(bf16[1024,1024]{1,0:T(8,128)(2,1)} %param.7) | copy-start | bytes 6291460
  8.5 24.9 %all-to-all-start = ((bf16[32,4,1024]{2,1,0:T(4,128)(2,1)}), bf16[32,4,1024]{2,1,0:T(4,128)(2,1)S(1)}, u32[]{:S(2)}, u32[]{:S(2)}) async-start(bf16[32,4,1024]{2,1,0:T(4,128)(2,1)} %reshape_squeeze.3), calls=%async_computation | async-start | bytes 524288 | tf_op jit(solution)/shard_map/all_to_all | solution.py:13
  21.1 94.7 %all-gather.4.cloned.1.call-start = ((), (), s32[]{:S(2)}) async-start(), calls=%async_computation.10 | async-start | bytes 4734976 | tf_op jit(solution)/shard_map/all_gather | solution.py:31
  54.4 21.6 %all-to-all-start.2 = ((bf16[16,8,1024]{2,1,0:T(8,128)(2,1)}), bf16[16,8,1024]{2,1,0:T(8,128)(2,1)S(1)}, u32[]{:S(2)}, u32[]{:S(2)}) async-start(bf16[16,8,1024]{2,1,0:T(8,128)(2,1)} %fusion.21), calls=%async_computation.2 | async-start | bytes 524288 | tf_op jit(solution)/shard_map/all_to_all | solution.py:13
  61.6 148.1 %all-gather.6.cloned.1.call-start = ((), (), s32[]{:S(2)}) async-start(), calls=%async_computation.12 | async-start | bytes 12255232 | tf_op jit(solution)/shard_map/all_gather | solution.py:51
  64.3 48.8 %collective-permute-start.1 = (bf16[352,1024]{1,0:T(8,128)(2,1)}, bf16[352,1024]{1,0:T(8,128)(2,1)S(1)}, u32[]{:S(2)}, u32[]{:S(2)}) collective-permute-start(bf16[352,1024]{1,0:T(8,128)(2,1)} %get-tuple-element.35), channel_id=1, source_target_pairs={{0,10},{1,11},{2,12},{3,13},{4,14},{16,26},{17,27},{18,28},{19,29}... | collective-permute-start | bytes 2162696 | tf_op jit(solution)/shard_map/ppermute | solution.py:37
  71.1 42.0 %collective-permute-start = (bf16[352,1024]{1,0:T(8,128)(2,1)}, bf16[352,1024]{1,0:T(8,128)(2,1)}, u32[]{:S(2)}, u32[]{:S(2)}) collective-permute-start(bf16[352,1024]{1,0:T(8,128)(2,1)} %get-tuple-element.36), channel_id=1, source_target_pairs={{0,5},{1,6},{2,7},{3,8},{4,9},{16,21},{17,22},{18,23},{19,24},{20,... | collective-permute-start | bytes 2162696 | tf_op jit(solution)/shard_map/ppermute | solution.py:36
  77.7 37.7 %copy-start.27 = (s32[1,32]{1,0:T(1,128)S(1)}, s32[1,32]{1,0:T(1,128)}, u32[]{:S(2)}) copy-start(s32[1,32]{1,0:T(1,128)} %param.9) | copy-start | bytes 388
  175.8 1.3 copy-start.1
  181.3 21.7 %slice-start = ((bf16[32,7,4,1024]{3,2,1,0:T(4,128)(2,1)}), bf16[32,2,4,1024]{3,2,1,0:T(4,128)(2,1)S(1)}, s32[]{:S(2)}) async-start(bf16[32,7,4,1024]{3,2,1,0:T(4,128)(2,1)} %copy-done.1), calls=%async_computation.13 | async-start | bytes 1048576 | tf_op jit(solution)/shard_map/slice | solution.py:64
  181.4 3.7 %collective-permute-start.2 = (bf16[8,24,1024]{2,1,0:T(8,128)(2,1)S(1)}, bf16[8,24,1024]{2,1,0:T(8,128)(2,1)S(1)}, u32[]{:S(2)}, u32[]{:S(2)}) collective-permute-start(bf16[8,24,1024]{2,1,0:T(8,128)(2,1)S(1)} %fusion.40), channel_id=1, source_target_pairs={{0,1},{1,0},{2,3},{3,2},{4,5},{5,4},{6,7},{7,6},{8,9},{9,8},{10,11... | collective-permute-start | bytes 1179656 | tf_op jit(solution)/shard_map/ppermute | solution.py:77
  186.1 17.9 %slice-start.1 = ((bf16[32,7,4,1024]{3,2,1,0:T(4,128)(2,1)}), bf16[32,2,4,1024]{3,2,1,0:T(4,128)(2,1)S(1)}, s32[]{:S(2)}) async-start(bf16[32,7,4,1024]{3,2,1,0:T(4,128)(2,1)} %copy-done.1), calls=%async_computation.14 | async-start | bytes 1048576 | tf_op jit(solution)/shard_map/slice | solution.py:69
  186.1 21.7 %all-to-all-start.4 = ((bf16[8,24,1024]{2,1,0:T(8,128)(2,1)}), bf16[8,24,1024]{2,1,0:T(8,128)(2,1)S(1)}, u32[]{:S(2)}, u32[]{:S(2)}) async-start(bf16[8,24,1024]{2,1,0:T(8,128)(2,1)} %fusion.39), calls=%async_computation.4 | async-start | bytes 786432 | tf_op jit(solution)/shard_map/all_to_all | solution.py:13
  192.7 85.7 %reduce-scatter.2.cloned.1.call-start = ((), (), s32[]{:S(2)}) async-start(), calls=%async_computation.11 | async-start | bytes 557056 | tf_op jit(solution)/shard_map/reduce_scatter | solution.py:84
  216.4 23.3 %all-to-all-start.5 = ((bf16[32,8,1024]{2,1,0:T(8,128)(2,1)}), bf16[32,8,1024]{2,1,0:T(8,128)(2,1)}, u32[]{:S(2)}, u32[]{:S(2)}) async-start(bf16[32,8,1024]{2,1,0:T(8,128)(2,1)} %broadcast_in_dim.24), calls=%async_computation.5 | async-start | bytes 1048576 | tf_op jit(solution)/shard_map/all_to_all | solution.py:13
  221.8 2.9 copy-start.26
  223.0 3.5 %copy-start.16 = (bf16[320,1024]{1,0:T(8,128)(2,1)}, bf16[320,1024]{1,0:T(8,128)(2,1)S(1)}, u32[]{:S(2)}) copy-start(bf16[320,1024]{1,0:T(8,128)(2,1)S(1)} %slice_bitcast_fusion.15) | copy-start | bytes 1966084
  224.7 1.8 copy-start.2
  224.7 1.8 copy-start.6
  242.9 21.9 %all-to-all-start.6 = ((bf16[32,8,1024]{2,1,0:T(8,128)(2,1)}), bf16[32,8,1024]{2,1,0:T(8,128)(2,1)}, u32[]{:S(2)}, u32[]{:S(2)}) async-start(bf16[32,8,1024]{2,1,0:T(8,128)(2,1)} %broadcast_in_dim.25), calls=%async_computation.6 | async-start | bytes 1048576 | tf_op jit(solution)/shard_map/all_to_all | solution.py:13
  248.9 0.8 copy-start.20
  251.5 4.7 %copy-start.3 = (bf16[352,1024]{1,0:T(8,128)(2,1)S(1)}, bf16[352,1024]{1,0:T(8,128)(2,1)}, u32[]{:S(2)}) copy-start(bf16[352,1024]{1,0:T(8,128)(2,1)} %copy-done.2) | copy-start | bytes 2162692
  251.5 4.7 %copy-start.7 = (bf16[352,1024]{1,0:T(8,128)(2,1)S(1)}, bf16[352,1024]{1,0:T(8,128)(2,1)}, u32[]{:S(2)}) copy-start(bf16[352,1024]{1,0:T(8,128)(2,1)} %copy-done.6) | copy-start | bytes 2162692
  251.5 4.7 %copy-start.17 = (bf16[320,1024]{1,0:T(8,128)(2,1)S(1)}, bf16[320,1024]{1,0:T(8,128)(2,1)}, u32[]{:S(2)}) copy-start(bf16[320,1024]{1,0:T(8,128)(2,1)} %copy-done.16) | copy-start | bytes 1966084
  251.5 4.7 %copy-start.24 = (f32[8,1024]{1,0:T(8,128)S(1)}, f32[8,1024]{1,0:T(8,128)}, u32[]{:S(2)}) copy-start(f32[8,1024]{1,0:T(8,128)} %unstack.35) | copy-start | bytes 98308
  268.0 21.8 %all-to-all-start.7 = ((bf16[32,8,1024]{2,1,0:T(8,128)(2,1)}), bf16[32,8,1024]{2,1,0:T(8,128)(2,1)}, u32[]{:S(2)}, u32[]{:S(2)}) async-start(bf16[32,8,1024]{2,1,0:T(8,128)(2,1)} %broadcast_in_dim.48), calls=%async_computation.8 | async-start | bytes 1048576 | tf_op jit(solution)/shard_map/all_to_all | solution.py:13
  272.9 2.1 copy-start.10
  272.9 2.1 copy-start.12
  272.9 2.2 copy-start.21
  275.1 1.3 copy-start.4
  275.1 1.3 copy-start.8
  275.1 1.5 copy-start.18
  293.1 22.8 %all-to-all-start.8 = ((bf16[32,8,1024]{2,1,0:T(8,128)(2,1)}), bf16[32,8,1024]{2,1,0:T(8,128)(2,1)}, u32[]{:S(2)}, u32[]{:S(2)}) async-start(bf16[32,8,1024]{2,1,0:T(8,128)(2,1)} %broadcast_in_dim.49), calls=%async_computation.9 | async-start | bytes 1048576 | tf_op jit(solution)/shard_map/all_to_all | solution.py:13
  300.7 1.9 copy-start.14
  300.7 1.9 copy-start.15
  300.7 2.0 copy-start.23
  302.7 1.3 copy-start.11
  302.7 1.3 copy-start.13
  302.7 1.5 copy-start.22
  304.2 1.3 copy-start.5
  304.2 1.3 copy-start.9
  304.2 1.5 copy-start.19
  304.2 1.5 copy-start.25
Sparse Core Ops, SparseCore 0:
  34.4 67.2 all-gather.3
  115.6 73.0 all-gather.5
  207.3 57.7 reduce-scatter.1
